TPU v7x, 32 devices: a whole 2x2x4 slice. The times are simulated.
32 devices in a mesh: mp: 2 (over y), fsdp: 8 (over z, core), tp: 2 (over x).
Axes of the slice: x: 2, y: 2, z: 4, core: 2. Of those that a mesh axis runs over, the one named last changes fastest.
Arguments:
- hidden: bfloat16 [2, 1280, 5120], P('mp', 'fsdp'), may hold values from -6 to 6
- live_weight: bfloat16 [2, 5120, 1024], P('mp', 'fsdp', 'tp'), may hold values from -0.078125 to 0.078125
- stale_weight: bfloat16 [2, 5120, 1024], P('mp', 'fsdp', 'tp'), may hold values from -0.078125 to 0.078125
- match: int32 [2, 1280], P('mp', 'fsdp'), may hold values from 0 to 159, as said below
Outputs:
- hidden_grad: bfloat16 [2, 1280, 5120], P('mp', 'fsdp', 'tp')
Inputs may be any that keep to these rules, and one draw needn't show every extreme that they name: Within each model's block of 160 rows, match is a permutation of 0 to 159, and the two models' permutations of a block are inverse to each other.
All inputs are finite; a program needn't handle non-finite values.
Results may differ from a plain program's by a relative error of at most 0.0061.
Values may be sent and summed in bfloat16 or wider, within the bound.
No kernel may reach another device: no remote copies, remote signals or barrier semaphores. Data moves between devices by JAX's collectives and lax.ppermute only.
A program may use at most 64 MiB of HBM per device.

v0:
```python
import jax
import jax.numpy as jnp
from jax import lax
from jax.sharding import PartitionSpec as P


def partner(block, axis, apart):
    count = lax.axis_size(axis)
    route = []
    for low in range(count):
        high = low | 1 << apart
        if high != low and high < count:
            route += [(low, high), (high, low)]
    return lax.ppermute(block, axis, route)


def shards(hidden, live_weight, stale_weight, match):
    hidden_rows = hidden[0]
    live_full = lax.all_gather(live_weight[0], "fsdp", axis=0, tiled=True)
    student = jnp.dot(hidden_rows, live_full, preferred_element_type=jnp.float32)
    stale_piece = stale_weight[0]
    teacher = jnp.dot(
        hidden_rows,
        lax.all_gather(stale_piece, "fsdp", axis=0, tiled=True),
        preferred_element_type=jnp.float32,
    ).astype(jnp.bfloat16)
    teacher = partner(teacher, "mp", 0)
    target = jnp.take(teacher, match[0], axis=0)
    mismatch = (student - target.astype(jnp.float32)).astype(jnp.bfloat16)
    partial_value = lax.dot_general(
        mismatch, live_full, (((1,), (1,)), ((), ())), preferred_element_type=jnp.float32
    )
    summed = lax.psum_scatter(
        partial_value.astype(jnp.bfloat16), "tp", scatter_dimension=1, tiled=True
    )
    return summed[None]


def solution(mesh):
    in_specs = (
        P("mp", "fsdp", None),
        P("mp", "fsdp", "tp"),
        P("mp", "fsdp", "tp"),
        P("mp", "fsdp"),
    )
    out_specs = P("mp", "fsdp", "tp")
    return jax.shard_map(shards, mesh=mesh, in_specs=in_specs, out_specs=out_specs, check_vma=False)
```

profile of v0, /device:TPU:0, one launch (start us, length us, event | category | flops | bytes accessed | tf_op | source)
XLA Modules:
  0.0 164.6 jit_solution(195391604350372213)
XLA Ops:
  6.5 0.0 copy-start
  6.5 0.0 copy-start.1
  6.5 0.0 all-gather.7.cloned.1.call-start
  6.5 0.7 all-gather.7.cloned.1.call-update
  7.3 0.0 all-gather.5.cloned.1.call-start
  7.3 0.7 all-gather.5.cloned.1.call-update
  8.0 0.0 reduce-scatter.2.cloned.1.call-start
  8.1 0.7 compare_select_fusion
  8.7 59.0 %all-gather.7.cloned.1.call-done = bf16[1,5120,512]{2,1,0:T(8,128)(2,1)} async-done(((bf16[1,640,512]{2,1,0:T(8,128)(2,1)}), bf16[1,5120,512]{2,1,0:T(8,128)(2,1)}) %all-gather.7.cloned.1.call-update) | async-done | bytes 5242896 | tf_op jit(solution)/shard_map/all_gather | solution.py:24
  67.8 0.0 copy-done
  67.8 3.5 %fusion.7 = bf16[160,512]{1,0:T(8,128)(2,1)S(1)} fusion(bf16[1,5120,512]{2,1,0:T(8,128)(2,1)} %all-gather.7.cloned.1.call-done, bf16[1,160,5120]{2,1,0:T(8,128)(2,1)S(1)} %copy-done), kind=kOutput, calls=%fused_computation.9 | convolution fusion | flops 838942720 | bytes 7045120 | tf_op jit(solution)/shard_map/dot_general | solution.py:22
  71.3 1.5 collective-permute-start
  72.8 0.0 copy-done.1
  72.9 4.8 %collective-permute-done = bf16[160,512]{1,0:T(8,128)(2,1)S(1)} collective-permute-done((bf16[160,512]{1,0:T(8,128)(2,1)S(1)}, bf16[160,512]{1,0:T(8,128)(2,1)S(1)}, u32[]{:S(2)}, u32[]{:S(2)}) %collective-permute-start) | collective-permute-done | bytes 163872 | tf_op jit(solution)/shard_map/ppermute | solution.py:14
  77.7 0.9 gather_fusion
  78.6 45.6 %all-gather.5.cloned.1.call-done = bf16[1,5120,512]{2,1,0:T(8,128)(2,1)} async-done(((bf16[1,640,512]{2,1,0:T(8,128)(2,1)}), bf16[1,5120,512]{2,1,0:T(8,128)(2,1)}) %all-gather.5.cloned.1.call-update) | async-done | bytes 5242896 | tf_op jit(solution)/shard_map/all_gather | solution.py:19
  124.3 8.1 %convolution_convert_fusion = bf16[160,5120]{1,0:T(8,128)(2,1)} fusion(bf16[1,5120,512]{2,1,0:T(8,128)(2,1)} %all-gather.5.cloned.1.call-done, bf16[1,160,5120]{2,1,0:T(8,128)(2,1)S(1)} %copy-done, bf16[160,512]{1,0:T(8,128)(2,1)S(1)} %gather_fusion, pred[160]{0:T(512)(128)(4,1)S(1)} %compare_and_fusion), kind=kOutput, calls=%fused_computation.1 | convolution fusion | flops 1678868480 | bytes 8683680 | tf_op jit(solution)/shard_map/dot_general | solution.py:30
  132.3 0.0 reduce-scatter.2.cloned.1.call-update
  132.4 25.7 %reduce-scatter.2.cloned.1.call-done = bf16[160,2560]{1,0:T(8,128)(2,1)} async-done(((bf16[160,5120]{1,0:T(8,128)(2,1)}), bf16[160,2560]{1,0:T(8,128)(2,1)}) %reduce-scatter.2.cloned.1.call-update) | async-done | bytes 819216 | tf_op jit(solution)/shard_map/reduce_scatter | solution.py:33
  (2 shorter events, 0.0 us)
Async XLA Ops:
  6.5 61.2 %copy-start = (bf16[1,160,5120]{2,1,0:T(8,128)(2,1)S(1)}, bf16[1,160,5120]{2,1,0:T(8,128)(2,1)}, u32[]{:S(2)}) copy-start(bf16[1,160,5120]{2,1,0:T(8,128)(2,1)} %param.4) | copy-start | bytes 4915204
  6.5 66.3 %copy-start.1 = (s32[1,160]{1,0:T(1,128)S(1)}, s32[1,160]{1,0:T(1,128)}, u32[]{:S(2)}) copy-start(s32[1,160]{1,0:T(1,128)} %param.7) | copy-start | bytes 1924
  6.5 61.2 %all-gather.7.cloned.1.call-start = ((), (), s32[]{:S(2)}) async-start(), calls=%async_computation.3 | async-start | bytes 5898240 | tf_op jit(solution)/shard_map/all_gather | solution.py:24
  7.3 117.0 %all-gather.5.cloned.1.call-start = ((), (), s32[]{:S(2)}) async-start(), calls=%async_computation.2 | async-start | bytes 5898240 | tf_op jit(solution)/shard_map/all_gather | solution.py:19
  8.0 150.1 %reduce-scatter.2.cloned.1.call-start = ((), (), s32[]{:S(2)}) async-start(), calls=%async_computation.1 | async-start | bytes 2457600 | tf_op jit(solution)/shard_map/reduce_scatter | solution.py:33
  71.3 6.4 %collective-permute-start = (bf16[160,512]{1,0:T(8,128)(2,1)S(1)}, bf16[160,512]{1,0:T(8,128)(2,1)S(1)}, u32[]{:S(2)}, u32[]{:S(2)}) collective-permute-start(bf16[160,512]{1,0:T(8,128)(2,1)S(1)} %fusion.7), channel_id=1, source_target_pairs={{0,16},{16,0},{1,17},{17,1},{2,18},{18,2},{3,19},{19,3},{4,20},{20... | collective-permute-start | bytes 491528 | tf_op jit(solution)/shard_map/ppermute | solution.py:14
Sparse Core Ops, SparseCore 0:
  9.0 58.7 all-gather.6
  69.4 54.8 all-gather.4
  132.5 25.5 reduce-scatter.1
where the time goes:
time: 165 us
  waiting for transfers between devices  137 us (83%)
  between operations  13.1 us (8%)
  matrix products  11.6 us (7%)
    all_gather x1, waiting for transfers between devices, shards(): lax.all_gather(stale_piece, 'fsdp', axis=0, tiled=True)  59 us
    all_gather x1, waiting for transfers between devices, shards(): live_full = lax.all_gather(live_weight[0], 'fsdp', axis=0, tiled=True)  45.6 us
    reduce_scatter x1, waiting for transfers between devices, shards(): lax.psum_scatter(partial_value.astype(jnp.bfloat16), 'tp', scatter_dimens...  25.7 us
    dot_general x1, matrix products, shards(): lax.dot_general(mismatch, live_full, (((1,), (1,)), ((), ())), preferred_...  8.07 us
    ppermute x1, waiting for transfers between devices, partner(): return lax.ppermute(block, axis, route)  4.84 us
    dot_general x1, matrix products, shards(): jnp.dot(hidden_rows, lax.all_gather(stale_piece, 'fsdp', axis=0, tiled=Tr...  3.5 us
  transfers between devices with their start and end apart: 4, of which 4 were waited for; matrix products, arithmetic and copies ran while one was open for 3% of the time, Pallas kernels for 0%

commit v1 on v0

v1 whole, which is shorter than its diff:
```python
import jax
import jax.numpy as jnp
from jax import lax
from jax.sharding import PartitionSpec as P

PAIR = ((0, 1), (1, 0), (2, 3), (3, 2))
MID = ((1, 2), (2, 1))
OUT = ((1, 0), (2, 3))
IN = ((0, 1), (3, 2))


def partner(block, axis, apart):
    count = lax.axis_size(axis)
    route = []
    for low in range(count):
        high = low | 1 << apart
        if high != low and high < count:
            route += [(low, high), (high, low)]
    return lax.ppermute(block, axis, route)


def along_z(block, pairs):
    route = [(2 * a + c, 2 * b + c) for a, b in pairs for c in range(2)]
    return lax.ppermute(block, "fsdp", route)


def across_cores(block):
    return partner(block, "fsdp", 0)


def near_over_x(block, near):
    route = []
    for f in range(8):
        own = f // 4
        source = 1 - own if near else own
        route.append((2 * f + source, 2 * f + 1 - source))
    return lax.ppermute(block, ("fsdp", "tp"), route)


def after(values, *gates):
    out = lax.optimization_barrier((tuple(values), gates))
    return out[0]


def dot(a, b):
    return jnp.dot(a, b, preferred_element_type=jnp.float32)


def dot_t(a, b):
    return lax.dot_general(a, b, (((1,), (1,)), ((), ())), preferred_element_type=jnp.float32)


def general(hidden, live_weight, stale_weight, match):
    hidden_rows = hidden[0]
    live_full = lax.all_gather(live_weight[0], "fsdp", axis=0, tiled=True)
    student = dot(hidden_rows, live_full)
    stale_full = lax.all_gather(stale_weight[0], "fsdp", axis=0, tiled=True)
    teacher = dot(hidden_rows, stale_full).astype(jnp.bfloat16)
    teacher = partner(teacher, "mp", 0)
    target = jnp.take(teacher, match[0], axis=0)
    mismatch = (student - target.astype(jnp.float32)).astype(jnp.bfloat16)
    partial_value = dot_t(mismatch, live_full).astype(jnp.bfloat16)
    summed = lax.psum_scatter(partial_value, "tp", scatter_dimension=1, tiled=True)
    return summed[None]


def line_of_four(hidden, live_weight, stale_weight, match):
    h, live, stale = hidden[0], live_weight[0], stale_weight[0]
    tokens, width = h.shape
    rows, cols = live.shape
    f, x = lax.axis_index("fsdp"), lax.axis_index("tp")
    z, c = f // 2, f % 2
    half = z // 2
    end = (z == 0) | (z == 3)
    q_opp = jnp.where(half == 0, 2, 1)
    q_far = jnp.where(half == 0, 3, 0)

    def h_rows(base, q):
        mine = lax.dynamic_slice_in_dim(base, rows * (2 * q + c), rows, 1)
        other = lax.dynamic_slice_in_dim(base, rows * (2 * q + 1 - c), rows, 1)
        return mine, other

    def contrib(base, q, piece, piece_other):
        mine, other = h_rows(base, q)
        return dot(mine, piece) + dot(other, piece_other)

    far_half = lax.dynamic_slice_in_dim(h, (width // 2) * (1 - half), width // 2, 1)

    live_nb = along_z(live, PAIR)
    live_opp_mid = along_z(live, MID)
    live_o = across_cores(live)
    stale_o = across_cores(stale)
    x_own = near_over_x(live, True)

    live_far_mid = along_z(live_nb, MID)
    live_opp_end = along_z(live_opp_mid, OUT)
    stale_1, far_half = after((stale, far_half), live_nb, live_opp_mid)
    stale_nb = along_z(stale_1, PAIR)
    stale_opp = along_z(stale_1, MID)
    h_end = along_z(far_half, IN)
    x_nb = near_over_x(live_nb, True)
    live_nb_o = across_cores(live_nb)
    live_opp = jnp.where(end, live_opp_end, live_opp_mid)
    live_opp_o = across_cores(live_opp)
    x_opp = near_over_x(live_opp, False)

    live_far_end = along_z(live_far_mid, OUT)
    (stale_nb_2,) = after((stale_nb,), live_far_mid)
    stale_far = along_z(stale_nb_2, MID)
    stale_nb_o = across_cores(stale_nb)
    stale_opp_o = across_cores(stale_opp)
    live_far = jnp.where(end, live_far_end, live_far_mid)
    live_far_o = across_cores(live_far)
    x_far = near_over_x(live_far, False)

    student = (
        contrib(h, z, live, live_o)
        + contrib(h, z ^ 1, live_nb, live_nb_o)
        + contrib(h, q_opp, live_opp, live_opp_o)
        + contrib(h, q_far, live_far, live_far_o)
    )

    t_own = contrib(h, z, stale, stale_o) + contrib(h, z ^ 1, stale_nb, stale_nb_o)
    own_far = lax.dynamic_slice_in_dim(h, (width // 2) * (1 - half), width // 2, 1)
    both = jnp.concatenate([own_far, h_end], axis=0)
    base = 2 * (1 - half)
    t_other = contrib(both, q_opp - base, stale_opp, stale_opp_o)
    stale_far_o = across_cores(stale_far)
    t_other = t_other + contrib(both, q_far - base, stale_far, stale_far_o)
    t_mine = t_own + jnp.where(end, 0.0, t_other[:tokens])
    t_mine = t_mine.astype(jnp.bfloat16)
    t_end = t_other[tokens:].astype(jnp.bfloat16)

    target_1 = partner(t_mine, "mp", 0)
    route = []
    for m in range(2):
        for a, b in OUT:
            for core in range(2):
                route.append((8 * m + 2 * a + core, 8 * (1 - m) + 2 * b + core))
    target_2 = lax.ppermute(t_end, ("mp", "fsdp"), route)
    teacher = (target_1.astype(jnp.float32) + target_2.astype(jnp.float32)).astype(jnp.bfloat16)
    pick = (match[0][:, None] == lax.broadcasted_iota(jnp.int32, (tokens, tokens), 1)).astype(jnp.bfloat16)
    target = dot(pick, teacher)
    mismatch = (student - target).astype(jnp.bfloat16)
    mismatch_o = partner(mismatch, "tp", 0)

    near = half == x
    a_own = jnp.where(near, live, live_opp)
    a_own_o = jnp.where(near, live_o, live_opp_o)
    b_own = jnp.where(near, live_nb, live_far)
    b_own_o = jnp.where(near, live_nb_o, live_far_o)
    a_x = jnp.where(near, x_own, x_opp)
    b_x = jnp.where(near, x_nb, x_far)
    a_x_o = across_cores(a_x)
    b_x_o = across_cores(b_x)
    place_a = jnp.where(near, z % 2, half)
    place_b = 1 - place_a

    def ordered(pa, pao, pb, pbo):
        full = jnp.zeros((4 * rows, cols), jnp.bfloat16)
        full = lax.dynamic_update_slice_in_dim(full, pa, rows * (2 * place_a + c), 0)
        full = lax.dynamic_update_slice_in_dim(full, pao, rows * (2 * place_a + 1 - c), 0)
        full = lax.dynamic_update_slice_in_dim(full, pb, rows * (2 * place_b + c), 0)
        full = lax.dynamic_update_slice_in_dim(full, pbo, rows * (2 * place_b + 1 - c), 0)
        return full

    w_own = ordered(a_own, a_own_o, b_own, b_own_o)
    w_x = ordered(a_x, a_x_o, b_x, b_x_o)
    grad = dot_t(mismatch, w_own) + dot_t(mismatch_o, w_x)
    return grad.astype(jnp.bfloat16)[None]


def solution(mesh):
    in_specs = (
        P("mp", "fsdp", None),
        P("mp", "fsdp", "tp"),
        P("mp", "fsdp", "tp"),
        P("mp", "fsdp"),
    )
    out_specs = P("mp", "fsdp", "tp")
    line = mesh.shape["fsdp"] == 8 and mesh.shape["tp"] == 2 and mesh.shape["mp"] == 2
    body = line_of_four if line else general
    return jax.shard_map(body, mesh=mesh, in_specs=in_specs, out_specs=out_specs, check_vma=False)
```

time: 165 us -> 112 us (0.68)
  waiting for transfers between devices: 137 us -> 58 us
  starting transfers between devices: 1.62 us -> 36.8 us
  between operations: 13.1 us -> 0.67 us
  other arithmetic: 0.7 us -> 2.54 us
    all_gather x2 -> x0, waiting for transfers between devices: 105 us -> none  [the longest x1 59 us: shards(): lax.all_gather(stale_piece, 'fsdp', axis=0, tiled=True)]
    ppermute x0 -> x14, waiting for transfers between devices: none -> 53.4 us  [the longest x9 34.9 us: along_z(): return lax.ppermute(block, 'fsdp', route)]
    ppermute x0 -> x14, starting transfers between devices: none -> 30.7 us  [the longest x9 19.3 us: along_z(): return lax.ppermute(block, 'fsdp', route)]
    reduce_scatter x1 -> x0, waiting for transfers between devices: 25.7 us -> none  [shards(): lax.psum_scatter(partial_value.astype(jnp.bfloat16), 'tp', scatter_dimens...]
    ppermute x1 -> x12, starting transfers between devices: 1.54 us -> 6.14 us  [partner(): return lax.ppermute(block, axis, route)]
    dynamic_update_slice x0 -> x6, other arithmetic: none -> 2.54 us  [the longest x2 1.6 us: ordered(): lax.dynamic_update_slice_in_dim(full, pb, rows * (2 * place_b + c), 0)]
    dot_general x2 -> x19, matrix products: 11.6 us -> 12.8 us  [the longest x17 9.92 us: dot(): return jnp.dot(a, b, preferred_element_type=jnp.float32)]
    ppermute x1 -> x12, waiting for transfers between devices: 4.84 us -> 4.6 us  [partner(): return lax.ppermute(block, axis, route)]
  transfers between devices with their start and end apart: 4 -> 26, of which waited for: 4 -> 7; matrix products, arithmetic and copies ran while one was open for 3% -> 12% of each run, Pallas kernels for 0% -> 0%
where the time goes in v1:
time: 112 us; the launch traced here: 111 us
  waiting for transfers between devices  58 us (52%)
  starting transfers between devices  36.8 us (33%)
  matrix products  12.8 us (11%)
  other arithmetic  2.54 us (2%)
    ppermute x9, waiting for transfers between devices, along_z(): return lax.ppermute(block, 'fsdp', route)  34.9 us
    ppermute x9, starting transfers between devices, along_z(): return lax.ppermute(block, 'fsdp', route)  19.3 us
    ppermute x4, waiting for transfers between devices, near_over_x(): return lax.ppermute(block, ('fsdp', 'tp'), route)  18.6 us
    ppermute x4, starting transfers between devices, near_over_x(): return lax.ppermute(block, ('fsdp', 'tp'), route)  10.1 us
    dot_general x17, matrix products, dot(): return jnp.dot(a, b, preferred_element_type=jnp.float32)  9.92 us
    ppermute x12, starting transfers between devices, partner(): return lax.ppermute(block, axis, route)  6.14 us
    ppermute x12, waiting for transfers between devices, partner(): return lax.ppermute(block, axis, route)  4.6 us
    dot_general x2, matrix products, dot_t(): lax.dot_general(a, b, (((1,), (1,)), ((), ())), preferred_element_type=jn...  2.91 us
  transfers between devices with their start and end apart: 26, of which 7 were waited for; matrix products, arithmetic and copies ran while one was open for 12% of the time, Pallas kernels for 0%

profile of v1, /device:TPU:0, one launch (start us, length us, event | category | flops | bytes accessed | tf_op | source)
XLA Modules:
  0.0 111.4 jit_solution(11366179100117701326)
XLA Ops:
  0.0 1.6 %collective-permute-start.3 = (bf16[640,512]{1,0:T(8,128)(2,1)}, bf16[640,512]{1,0:T(8,128)(2,1)}, u32[]{:S(2)}, u32[]{:S(2)}) collective-permute-start(bf16[640,512]{1,0:T(8,128)(2,1)} %bitcast.62), channel_id=1, source_target_pairs={{4,8},{6,10},{8,4},{10,6},{5,9},{7,11},{9,5},{11,7},{20,24},{22,26... | collective-permute-start | bytes 1966088 | tf_op jit(solution)/shard_map/ppermute | solution.py:24
  1.6 5.1 %collective-permute-start.1 = (bf16[640,512]{1,0:T(8,128)(2,1)}, bf16[640,512]{1,0:T(8,128)(2,1)}, u32[]{:S(2)}, u32[]{:S(2)}) collective-permute-start(bf16[640,512]{1,0:T(8,128)(2,1)} %bitcast.63), channel_id=1, source_target_pairs={{0,4},{2,6},{4,0},{6,2},{8,12},{10,14},{12,8},{14,10},{1,5},{3,7},... | collective-permute-start | bytes 1966088 | tf_op jit(solution)/shard_map/ppermute | solution.py:24
  7.4 1.5 %fusion.35 = f32[160,512]{1,0:T(8,128)S(1)} fusion(bf16[1,160,5120]{2,1,0:T(8,128)(2,1)S(1)} %copy-done, s32[]{:T(128)S(6)} %select_n.136, bf16[1,640,512]{2,1,0:T(8,128)(2,1)} %param.6), kind=kOutput, calls=%fused_computation.60 | convolution fusion | flops 104857600 | bytes 1187844 | tf_op jit(solution)/shard_map/dot_general | solution.py:46
  8.9 1.3 %collective-permute-start.4 = (bf16[640,512]{1,0:T(8,128)(2,1)}, bf16[640,512]{1,0:T(8,128)(2,1)S(1)}, u32[]{:S(2)}, u32[]{:S(2)}) collective-permute-start(bf16[640,512]{1,0:T(8,128)(2,1)} %collective-permute-done.3), channel_id=1, source_target_pairs={{4,0},{6,2},{8,12},{10,14},{5,1},{7,3},{9,13},{11,15},{20,16},{22,... | collective-permute-start | bytes 1966088 | tf_op jit(solution)/shard_map/ppermute | solution.py:24
  10.2 1.4 %fusion.37 = f32[160,512]{1,0:T(8,128)S(1)} fusion(bf16[1,160,5120]{2,1,0:T(8,128)(2,1)S(1)} %copy-done, s32[]{:T(128)S(6)} %select_n.136, bf16[1,640,512]{2,1,0:T(8,128)(2,1)} %param.5), kind=kOutput, calls=%fused_computation.62 | convolution fusion | flops 104857600 | bytes 1187844 | tf_op jit(solution)/shard_map/dot_general | solution.py:46
  11.6 9.9 %collective-permute-done.1 = bf16[640,512]{1,0:T(8,128)(2,1)} collective-permute-done((bf16[640,512]{1,0:T(8,128)(2,1)}, bf16[640,512]{1,0:T(8,128)(2,1)}, u32[]{:S(2)}, u32[]{:S(2)}) %collective-permute-start.1) | collective-permute-done | bytes 655392 | tf_op jit(solution)/shard_map/ppermute | solution.py:24
  21.5 3.2 %collective-permute-start.10 = (bf16[640,512]{1,0:T(8,128)(2,1)S(1)}, bf16[640,512]{1,0:T(8,128)(2,1)S(1)}, u32[]{:S(2)}, u32[]{:S(2)}) collective-permute-start(bf16[640,512]{1,0:T(8,128)(2,1)S(1)} %bitcast.67), channel_id=1, source_target_pairs={{0,4},{2,6},{4,0},{6,2},{8,12},{10,14},{12,8},{14,10},{1,5},{3,7},... | collective-permute-start | bytes 1966088 | tf_op jit(solution)/shard_map/ppermute | solution.py:24
  25.4 4.8 %collective-permute-start.12 = (bf16[160,2560]{1,0:T(8,128)(2,1)S(1)}, bf16[160,2560]{1,0:T(8,128)(2,1)S(1)}, u32[]{:S(2)}, u32[]{:S(2)}) collective-permute-start(bf16[160,2560]{1,0:T(8,128)(2,1)S(1)} %dynamic-slice_bitcast_fusion), channel_id=1, source_target_pairs={{0,4},{2,6},{12,8},{14,10},{1,5},{3,7},{13,9},{15,11},{16,20},{18,... | collective-permute-start | bytes 2457608 | tf_op jit(solution)/shard_map/ppermute | solution.py:24
  30.1 1.4 %convolution_add_fusion.4 = f32[160,512]{1,0:T(8,128)S(1)} fusion(f32[160,512]{1,0:T(8,128)S(1)} %fusion.35, bf16[640,512]{1,0:T(8,128)(2,1)} %collective-permute-done.9, bf16[1,160,5120]{2,1,0:T(8,128)(2,1)S(1)} %copy-done, s32[]{:T(128)S(6)} %select_n.137), kind=kOutput, calls=%fused_computation.15 | convolution fusion | flops 104939520 | bytes 1515524 | tf_op jit(solution)/shard_map/dot_general | solution.py:46
  32.6 6.4 %collective-permute-done.4 = bf16[640,512]{1,0:T(8,128)(2,1)S(1)} collective-permute-done((bf16[640,512]{1,0:T(8,128)(2,1)}, bf16[640,512]{1,0:T(8,128)(2,1)S(1)}, u32[]{:S(2)}, u32[]{:S(2)}) %collective-permute-start.4) | collective-permute-done | bytes 655392 | tf_op jit(solution)/shard_map/ppermute | solution.py:24
  39.6 1.4 %fusion.31 = f32[160,512]{1,0:T(8,128)S(1)} fusion(bf16[640,512]{1,0:T(8,128)(2,1)} %collective-permute-done.1, bf16[1,160,5120]{2,1,0:T(8,128)(2,1)S(1)} %copy-done, s32[]{:T(128)S(6)} %select_n.138), kind=kOutput, calls=%fused_computation.56 | convolution fusion | flops 104857600 | bytes 1187844 | tf_op jit(solution)/shard_map/dot_general | solution.py:46
  41.0 10.2 %collective-permute-done.10 = bf16[640,512]{1,0:T(8,128)(2,1)S(1)} collective-permute-done((bf16[640,512]{1,0:T(8,128)(2,1)S(1)}, bf16[640,512]{1,0:T(8,128)(2,1)S(1)}, u32[]{:S(2)}, u32[]{:S(2)}) %collective-permute-start.10) | collective-permute-done | bytes 655392 | tf_op jit(solution)/shard_map/ppermute | solution.py:24
  52.5 4.6 %collective-permute-start.21 = (bf16[640,512]{1,0:T(8,128)(2,1)S(1)}, bf16[640,512]{1,0:T(8,128)(2,1)S(1)}, u32[]{:S(2)}, u32[]{:S(2)}) collective-permute-start(bf16[640,512]{1,0:T(8,128)(2,1)S(1)} %get-tuple-element.14), channel_id=1, source_target_pairs={{0,1},{2,3},{4,5},{6,7},{9,8},{11,10},{13,12},{15,14},{16,17},{18,... | collective-permute-start | bytes 1966088 | tf_op jit(solution)/shard_map/ppermute | solution.py:37
  58.7 1.3 %collective-permute-start.7 = (bf16[640,512]{1,0:T(8,128)(2,1)S(1)}, bf16[640,512]{1,0:T(8,128)(2,1)S(1)}, u32[]{:S(2)}, u32[]{:S(2)}) collective-permute-start(bf16[640,512]{1,0:T(8,128)(2,1)S(1)} %collective-permute-done.6), channel_id=1, source_target_pairs={{4,0},{6,2},{8,12},{10,14},{5,1},{7,3},{9,13},{11,15},{20,16},{22,... | collective-permute-start | bytes 1966088 | tf_op jit(solution)/shard_map/ppermute | solution.py:24
  60.2 7.9 %collective-permute-done.20 = bf16[640,512]{1,0:T(8,128)(2,1)S(1)} collective-permute-done((bf16[640,512]{1,0:T(8,128)(2,1)S(1)}, bf16[640,512]{1,0:T(8,128)(2,1)S(1)}, u32[]{:S(2)}, u32[]{:S(2)}) %collective-permute-start.20) | collective-permute-done | bytes 655392 | tf_op jit(solution)/shard_map/ppermute | solution.py:37
  70.7 8.4 %collective-permute-done.7 = bf16[640,512]{1,0:T(8,128)(2,1)S(1)} collective-permute-done((bf16[640,512]{1,0:T(8,128)(2,1)S(1)}, bf16[640,512]{1,0:T(8,128)(2,1)S(1)}, u32[]{:S(2)}, u32[]{:S(2)}) %collective-permute-start.7) | collective-permute-done | bytes 655392 | tf_op jit(solution)/shard_map/ppermute | solution.py:24
  79.0 1.4 %select_dynamic-update-slice_fusion.1 = (bf16[2560,512]{1,0:T(8,128)(2,1)S(1)}, bf16[640,512]{1,0:T(8,128)(2,1)S(1)}) fusion(bf16[2560,512]{1,0:T(8,128)(2,1)S(1)} %select_dynamic-update-slice_fusion.2, s32[]{:T(128)S(6)} %select_n.165, bf16[640,512]{1,0:T(8,128)(2,1)} %collective-permute-done.1, pred[]{:T(512)S(6)} %eq.32, ...), kind=kLoop, calls=%fused_computation.30 | loop fusion | flops 655360 | bytes 3276806 | tf_op jit(solution)/shard_map/dynamic_update_slice | solution.py:163
  82.6 2.9 %collective-permute-start.24 = (bf16[640,512]{1,0:T(8,128)(2,1)S(1)}, bf16[640,512]{1,0:T(8,128)(2,1)S(1)}, u32[]{:S(2)}, u32[]{:S(2)}) collective-permute-start(bf16[640,512]{1,0:T(8,128)(2,1)S(1)} %get-tuple-element.12), channel_id=1, source_target_pairs={{0,1},{2,3},{4,5},{6,7},{9,8},{11,10},{13,12},{15,14},{16,17},{18,... | collective-permute-start | bytes 1966088 | tf_op jit(solution)/shard_map/ppermute | solution.py:37
  86.0 1.3 %collective-permute-start.18 = (bf16[160,512]{1,0:T(8,128)(2,1)S(1)}, bf16[160,512]{1,0:T(8,128)(2,1)S(1)}, u32[]{:S(2)}, u32[]{:S(2)}) collective-permute-start(bf16[160,512]{1,0:T(8,128)(2,1)S(1)} %slice.15), channel_id=1, source_target_pairs={{4,16},{6,18},{8,28},{10,30},{20,0},{22,2},{24,12},{26,14},{5,17},... | collective-permute-start | bytes 491528 | tf_op jit(solution)/shard_map/ppermute | solution.py:140
  87.6 1.6 %collective-permute-start.17 = (bf16[160,512]{1,0:T(8,128)(2,1)S(1)}, bf16[160,512]{1,0:T(8,128)(2,1)S(1)}, u32[]{:S(2)}, u32[]{:S(2)}) collective-permute-start(bf16[160,512]{1,0:T(8,128)(2,1)S(1)} %fusion.9), channel_id=1, source_target_pairs={{0,16},{16,0},{1,17},{17,1},{2,18},{18,2},{3,19},{19,3},{4,20},{20... | collective-permute-start | bytes 491528 | tf_op jit(solution)/shard_map/ppermute | solution.py:19
  89.3 10.7 %collective-permute-done.24 = bf16[640,512]{1,0:T(8,128)(2,1)S(1)} collective-permute-done((bf16[640,512]{1,0:T(8,128)(2,1)S(1)}, bf16[640,512]{1,0:T(8,128)(2,1)S(1)}, u32[]{:S(2)}, u32[]{:S(2)}) %collective-permute-start.24) | collective-permute-done | bytes 655392 | tf_op jit(solution)/shard_map/ppermute | solution.py:37
  101.1 2.5 %collective-permute-start.19 = (bf16[160,512]{1,0:T(8,128)(2,1)S(1)}, bf16[160,512]{1,0:T(8,128)(2,1)S(1)}, u32[]{:S(2)}, u32[]{:S(2)}) collective-permute-start(bf16[160,512]{1,0:T(8,128)(2,1)S(1)} %fusion.10), channel_id=1, source_target_pairs={{0,1},{1,0},{2,3},{3,2},{4,5},{5,4},{6,7},{7,6},{8,9},{9,8},{10,11... | collective-permute-start | bytes 491528 | tf_op jit(solution)/shard_map/ppermute | solution.py:19
  104.0 4.6 %collective-permute-done.19 = bf16[160,512]{1,0:T(8,128)(2,1)S(1)} collective-permute-done((bf16[160,512]{1,0:T(8,128)(2,1)S(1)}, bf16[160,512]{1,0:T(8,128)(2,1)S(1)}, u32[]{:S(2)}, u32[]{:S(2)}) %collective-permute-start.19) | collective-permute-done | bytes 163872 | tf_op jit(solution)/shard_map/ppermute | solution.py:19
  109.5 1.9 %fusion.1 = bf16[1,160,2560]{2,1,0:T(8,128)(2,1)} fusion(f32[160,2560]{1,0:T(8,128)S(1)} %fusion.75, bf16[160,512]{1,0:T(8,128)(2,1)S(1)} %fusion.10, bf16[2560,512]{1,0:T(8,128)(2,1)S(1)} %select_dynamic-update-slice_fusion), kind=kOutput, calls=%fused_computation.2 | convolution fusion | flops 420249600 | bytes 5242880 | tf_op jit(solution)/shard_map/dot_general | solution.py:50
  (67 shorter events, 13.7 us)
Async XLA Ops:
  0.0 8.9 %collective-permute-start.3 = (bf16[640,512]{1,0:T(8,128)(2,1)}, bf16[640,512]{1,0:T(8,128)(2,1)}, u32[]{:S(2)}, u32[]{:S(2)}) collective-permute-start(bf16[640,512]{1,0:T(8,128)(2,1)} %bitcast.62), channel_id=1, source_target_pairs={{4,8},{6,10},{8,4},{10,6},{5,9},{7,11},{9,5},{11,7},{20,24},{22,26... | collective-permute-start | bytes 1966088 | tf_op jit(solution)/shard_map/ppermute | solution.py:24
  1.6 19.9 %collective-permute-start.1 = (bf16[640,512]{1,0:T(8,128)(2,1)}, bf16[640,512]{1,0:T(8,128)(2,1)}, u32[]{:S(2)}, u32[]{:S(2)}) collective-permute-start(bf16[640,512]{1,0:T(8,128)(2,1)} %bitcast.63), channel_id=1, source_target_pairs={{0,4},{2,6},{4,0},{6,2},{8,12},{10,14},{12,8},{14,10},{1,5},{3,7},... | collective-permute-start | bytes 1966088 | tf_op jit(solution)/shard_map/ppermute | solution.py:24
  6.7 24.8 %collective-permute-start = (bf16[640,512]{1,0:T(8,128)(2,1)}, bf16[640,512]{1,0:T(8,128)(2,1)S(1)}, u32[]{:S(2)}, u32[]{:S(2)}) collective-permute-start(bf16[640,512]{1,0:T(8,128)(2,1)} %bitcast.64), channel_id=1, source_target_pairs={{0,2},{2,0},{4,6},{6,4},{8,10},{10,8},{12,14},{14,12},{1,3},{3,1},... | collective-permute-start | bytes 1966088 | tf_op jit(solution)/shard_map/ppermute | solution.py:19
  6.7 18.6 %collective-permute-start.9 = (bf16[640,512]{1,0:T(8,128)(2,1)}, bf16[640,512]{1,0:T(8,128)(2,1)}, u32[]{:S(2)}, u32[]{:S(2)}) collective-permute-start(bf16[640,512]{1,0:T(8,128)(2,1)} %bitcast.66), channel_id=1, source_target_pairs={{0,2},{2,0},{4,6},{6,4},{8,10},{10,8},{12,14},{14,12},{1,3},{3,1},... | collective-permute-start | bytes 1966088 | tf_op jit(solution)/shard_map/ppermute | solution.py:19
  8.9 30.0 %collective-permute-start.4 = (bf16[640,512]{1,0:T(8,128)(2,1)}, bf16[640,512]{1,0:T(8,128)(2,1)S(1)}, u32[]{:S(2)}, u32[]{:S(2)}) collective-permute-start(bf16[640,512]{1,0:T(8,128)(2,1)} %collective-permute-done.3), channel_id=1, source_target_pairs={{4,0},{6,2},{8,12},{10,14},{5,1},{7,3},{9,13},{11,15},{20,16},{22,... | collective-permute-start | bytes 1966088 | tf_op jit(solution)/shard_map/ppermute | solution.py:24
  21.5 29.7 %collective-permute-start.10 = (bf16[640,512]{1,0:T(8,128)(2,1)S(1)}, bf16[640,512]{1,0:T(8,128)(2,1)S(1)}, u32[]{:S(2)}, u32[]{:S(2)}) collective-permute-start(bf16[640,512]{1,0:T(8,128)(2,1)S(1)} %bitcast.67), channel_id=1, source_target_pairs={{0,4},{2,6},{4,0},{6,2},{8,12},{10,14},{12,8},{14,10},{1,5},{3,7},... | collective-permute-start | bytes 1966088 | tf_op jit(solution)/shard_map/ppermute | solution.py:24
  24.7 32.8 %collective-permute-start.13 = (bf16[640,512]{1,0:T(8,128)(2,1)S(1)}, bf16[640,512]{1,0:T(8,128)(2,1)S(1)}, u32[]{:S(2)}, u32[]{:S(2)}) collective-permute-start(bf16[640,512]{1,0:T(8,128)(2,1)S(1)} %bitcast.68), channel_id=1, source_target_pairs={{4,8},{6,10},{8,4},{10,6},{5,9},{7,11},{9,5},{11,7},{20,24},{22,26... | collective-permute-start | bytes 1966088 | tf_op jit(solution)/shard_map/ppermute | solution.py:24
  25.4 32.2 %collective-permute-start.12 = (bf16[160,2560]{1,0:T(8,128)(2,1)S(1)}, bf16[160,2560]{1,0:T(8,128)(2,1)S(1)}, u32[]{:S(2)}, u32[]{:S(2)}) collective-permute-start(bf16[160,2560]{1,0:T(8,128)(2,1)S(1)} %dynamic-slice_bitcast_fusion), channel_id=1, source_target_pairs={{0,4},{2,6},{12,8},{14,10},{1,5},{3,7},{13,9},{15,11},{16,20},{18,... | collective-permute-start | bytes 2457608 | tf_op jit(solution)/shard_map/ppermute | solution.py:24
  31.5 21.0 %collective-permute-start.6 = (bf16[640,512]{1,0:T(8,128)(2,1)}, bf16[640,512]{1,0:T(8,128)(2,1)S(1)}, u32[]{:S(2)}, u32[]{:S(2)}) collective-permute-start(bf16[640,512]{1,0:T(8,128)(2,1)} %collective-permute-done.1), channel_id=1, source_target_pairs={{4,8},{6,10},{8,4},{10,6},{5,9},{7,11},{9,5},{11,7},{20,24},{22,26... | collective-permute-start | bytes 1966088 | tf_op jit(solution)/shard_map/ppermute | solution.py:24
  39.5 19.2 %collective-permute-start.5 = (bf16[640,512]{1,0:T(8,128)(2,1)S(1)}, bf16[640,512]{1,0:T(8,128)(2,1)S(1)}, u32[]{:S(2)}, u32[]{:S(2)}) collective-permute-start(bf16[640,512]{1,0:T(8,128)(2,1)S(1)} %get-tuple-element.14), channel_id=1, source_target_pairs={{0,2},{2,0},{4,6},{6,4},{8,10},{10,8},{12,14},{14,12},{1,3},{3,1},... | collective-permute-start | bytes 1966088 | tf_op jit(solution)/shard_map/ppermute | solution.py:19
  51.2 16.8 %collective-permute-start.20 = (bf16[640,512]{1,0:T(8,128)(2,1)S(1)}, bf16[640,512]{1,0:T(8,128)(2,1)S(1)}, u32[]{:S(2)}, u32[]{:S(2)}) collective-permute-start(bf16[640,512]{1,0:T(8,128)(2,1)S(1)} %bitcast.65), channel_id=1, source_target_pairs={{1,0},{3,2},{5,4},{7,6},{8,9},{10,11},{12,13},{14,15},{17,16},{19,... | collective-permute-start | bytes 1966088 | tf_op jit(solution)/shard_map/ppermute | solution.py:37
  52.5 16.8 %collective-permute-start.21 = (bf16[640,512]{1,0:T(8,128)(2,1)S(1)}, bf16[640,512]{1,0:T(8,128)(2,1)S(1)}, u32[]{:S(2)}, u32[]{:S(2)}) collective-permute-start(bf16[640,512]{1,0:T(8,128)(2,1)S(1)} %get-tuple-element.14), channel_id=1, source_target_pairs={{0,1},{2,3},{4,5},{6,7},{9,8},{11,10},{13,12},{15,14},{16,17},{18,... | collective-permute-start | bytes 1966088 | tf_op jit(solution)/shard_map/ppermute | solution.py:37
  57.4 23.3 %collective-permute-start.2 = (bf16[640,512]{1,0:T(8,128)(2,1)}, bf16[640,512]{1,0:T(8,128)(2,1)S(1)}, u32[]{:S(2)}, u32[]{:S(2)}) collective-permute-start(bf16[640,512]{1,0:T(8,128)(2,1)} %collective-permute-done.1), channel_id=1, source_target_pairs={{0,2},{2,0},{4,6},{6,4},{8,10},{10,8},{12,14},{14,12},{1,3},{3,1},... | collective-permute-start | bytes 1966088 | tf_op jit(solution)/shard_map/ppermute | solution.py:19
  57.5 12.6 %collective-permute-start.15 = (bf16[640,512]{1,0:T(8,128)(2,1)S(1)}, bf16[640,512]{1,0:T(8,128)(2,1)S(1)}, u32[]{:S(2)}, u32[]{:S(2)}) collective-permute-start(bf16[640,512]{1,0:T(8,128)(2,1)S(1)} %collective-permute-done.10), channel_id=1, source_target_pairs={{4,8},{6,10},{8,4},{10,6},{5,9},{7,11},{9,5},{11,7},{20,24},{22,26... | collective-permute-start | bytes 1966088 | tf_op jit(solution)/shard_map/ppermute | solution.py:24
  58.7 20.4 %collective-permute-start.7 = (bf16[640,512]{1,0:T(8,128)(2,1)S(1)}, bf16[640,512]{1,0:T(8,128)(2,1)S(1)}, u32[]{:S(2)}, u32[]{:S(2)}) collective-permute-start(bf16[640,512]{1,0:T(8,128)(2,1)S(1)} %collective-permute-done.6), channel_id=1, source_target_pairs={{4,0},{6,2},{8,12},{10,14},{5,1},{7,3},{9,13},{11,15},{20,16},{22,... | collective-permute-start | bytes 1966088 | tf_op jit(solution)/shard_map/ppermute | solution.py:24
  68.1 21.2 %collective-permute-start.23 = (bf16[640,512]{1,0:T(8,128)(2,1)}, bf16[640,512]{1,0:T(8,128)(2,1)S(1)}, u32[]{:S(2)}, u32[]{:S(2)}) collective-permute-start(bf16[640,512]{1,0:T(8,128)(2,1)} %collective-permute-done.1), channel_id=1, source_target_pairs={{1,0},{3,2},{5,4},{7,6},{8,9},{10,11},{12,13},{14,15},{17,16},{19,... | collective-permute-start | bytes 1966088 | tf_op jit(solution)/shard_map/ppermute | solution.py:37
  69.4 13.2 %collective-permute-start.14 = (bf16[640,512]{1,0:T(8,128)(2,1)S(1)}, bf16[640,512]{1,0:T(8,128)(2,1)S(1)}, u32[]{:S(2)}, u32[]{:S(2)}) collective-permute-start(bf16[640,512]{1,0:T(8,128)(2,1)S(1)} %collective-permute-done.13), channel_id=1, source_target_pairs={{0,2},{2,0},{4,6},{6,4},{8,10},{10,8},{12,14},{14,12},{1,3},{3,1},... | collective-permute-start | bytes 1966088 | tf_op jit(solution)/shard_map/ppermute | solution.py:19
  70.1 15.8 %collective-permute-start.11 = (bf16[640,512]{1,0:T(8,128)(2,1)S(1)}, bf16[640,512]{1,0:T(8,128)(2,1)S(1)}, u32[]{:S(2)}, u32[]{:S(2)}) collective-permute-start(bf16[640,512]{1,0:T(8,128)(2,1)S(1)} %collective-permute-done.10), channel_id=1, source_target_pairs={{0,2},{2,0},{4,6},{6,4},{8,10},{10,8},{12,14},{14,12},{1,3},{3,1},... | collective-permute-start | bytes 1966088 | tf_op jit(solution)/shard_map/ppermute | solution.py:19
  80.8 19.5 %collective-permute-start.8 = (bf16[640,512]{1,0:T(8,128)(2,1)S(1)}, bf16[640,512]{1,0:T(8,128)(2,1)S(1)}, u32[]{:S(2)}, u32[]{:S(2)}) collective-permute-start(bf16[640,512]{1,0:T(8,128)(2,1)S(1)} %get-tuple-element.12), channel_id=1, source_target_pairs={{0,2},{2,0},{4,6},{6,4},{8,10},{10,8},{12,14},{14,12},{1,3},{3,1},... | collective-permute-start | bytes 1966088 | tf_op jit(solution)/shard_map/ppermute | solution.py:19
  82.1 5.5 %collective-permute-start.22 = (bf16[640,512]{1,0:T(8,128)(2,1)S(1)}, bf16[640,512]{1,0:T(8,128)(2,1)S(1)}, u32[]{:S(2)}, u32[]{:S(2)}) collective-permute-start(bf16[640,512]{1,0:T(8,128)(2,1)S(1)} %get-tuple-element.18), channel_id=1, source_target_pairs={{0,2},{2,0},{4,6},{6,4},{8,10},{10,8},{12,14},{14,12},{1,3},{3,1},... | collective-permute-start | bytes 1966088 | tf_op jit(solution)/shard_map/ppermute | solution.py:19
  82.6 17.4 %collective-permute-start.24 = (bf16[640,512]{1,0:T(8,128)(2,1)S(1)}, bf16[640,512]{1,0:T(8,128)(2,1)S(1)}, u32[]{:S(2)}, u32[]{:S(2)}) collective-permute-start(bf16[640,512]{1,0:T(8,128)(2,1)S(1)} %get-tuple-element.12), channel_id=1, source_target_pairs={{0,1},{2,3},{4,5},{6,7},{9,8},{11,10},{13,12},{15,14},{16,17},{18,... | collective-permute-start | bytes 1966088 | tf_op jit(solution)/shard_map/ppermute | solution.py:37
  86.0 14.6 %collective-permute-start.18 = (bf16[160,512]{1,0:T(8,128)(2,1)S(1)}, bf16[160,512]{1,0:T(8,128)(2,1)S(1)}, u32[]{:S(2)}, u32[]{:S(2)}) collective-permute-start(bf16[160,512]{1,0:T(8,128)(2,1)S(1)} %slice.15), channel_id=1, source_target_pairs={{4,16},{6,18},{8,28},{10,30},{20,0},{22,2},{24,12},{26,14},{5,17},... | collective-permute-start | bytes 491528 | tf_op jit(solution)/shard_map/ppermute | solution.py:140
  87.6 13.0 %collective-permute-start.17 = (bf16[160,512]{1,0:T(8,128)(2,1)S(1)}, bf16[160,512]{1,0:T(8,128)(2,1)S(1)}, u32[]{:S(2)}, u32[]{:S(2)}) collective-permute-start(bf16[160,512]{1,0:T(8,128)(2,1)S(1)} %fusion.9), channel_id=1, source_target_pairs={{0,16},{16,0},{1,17},{17,1},{2,18},{18,2},{3,19},{19,3},{4,20},{20... | collective-permute-start | bytes 491528 | tf_op jit(solution)/shard_map/ppermute | solution.py:19
  101.1 7.4 %collective-permute-start.19 = (bf16[160,512]{1,0:T(8,128)(2,1)S(1)}, bf16[160,512]{1,0:T(8,128)(2,1)S(1)}, u32[]{:S(2)}, u32[]{:S(2)}) collective-permute-start(bf16[160,512]{1,0:T(8,128)(2,1)S(1)} %fusion.10), channel_id=1, source_target_pairs={{0,1},{1,0},{2,3},{3,2},{4,5},{5,4},{6,7},{7,6},{8,9},{9,8},{10,11... | collective-permute-start | bytes 491528 | tf_op jit(solution)/shard_map/ppermute | solution.py:19
  (6 other events, 46.0 us)

commit v2 on v0

v2 whole, which is shorter than its diff:
```python
import jax
import jax.numpy as jnp
import numpy as np
from jax import lax
from jax.experimental import pallas as pl
from jax.experimental.pallas import tpu as pltpu
from jax.sharding import PartitionSpec as P

PAIR = ((0, 1), (1, 0), (2, 3), (3, 2))
MID = ((1, 2), (2, 1))
OUT = ((1, 0), (2, 3))

OWN, OWN_O, NB, NB_O, OPP, OPP_O, FAR, FAR_O, END, NEAR, HALF, PIECE = range(12)


def table():
    rows = []
    for f in range(8):
        for x in range(2):
            z, c = f // 2, f % 2
            half = z // 2
            opp, far = (2, 3) if half == 0 else (1, 0)
            near = int(half == x)
            first = z % 2 if near else half
            row = []
            for q in (z, z ^ 1, opp, far):
                row += [2 * q + c, 2 * q + 1 - c]
            row += [int(z in (0, 3)), near, 1 - half]
            for q in (first, 1 - first):
                row += [2 * q + c, 2 * q + 1 - c]
            rows.append(row)
    return np.array(rows, np.int32)


def partner(block, axis, apart):
    count = lax.axis_size(axis)
    route = []
    for low in range(count):
        high = low | 1 << apart
        if high != low and high < count:
            route += [(low, high), (high, low)]
    return lax.ppermute(block, axis, route)


def along_z(block, pairs):
    route = [(2 * a + c, 2 * b + c) for a, b in pairs for c in range(2)]
    return lax.ppermute(block, "fsdp", route)


def across_cores(block):
    return partner(block, "fsdp", 0)


def near_over_x(block, near):
    route = []
    for f in range(8):
        own = f // 4
        source = 1 - own if near else own
        route.append((2 * f + source, 2 * f + 1 - source))
    return lax.ppermute(block, ("fsdp", "tp"), route)


def after(values, *gates):
    out = lax.optimization_barrier((tuple(values), gates))
    return out[0]


def dot(a, b):
    return jnp.dot(a, b, preferred_element_type=jnp.float32)


def dot_t(a, b):
    return lax.dot_general(a, b, (((1,), (1,)), ((), ())), preferred_element_type=jnp.float32)


def whole(array):
    return pl.BlockSpec(array.shape, lambda i, s: (0,) * array.ndim)


def call(body, places, operands, specs, outs, scratch=(), name=None):
    single = not isinstance(outs, (list, tuple))
    shapes = [outs] if single else list(outs)
    out = pl.pallas_call(
        body,
        out_shape=shapes,
        grid_spec=pltpu.PrefetchScalarGridSpec(
            num_scalar_prefetch=1,
            grid=(1,),
            in_specs=specs,
            out_specs=[pl.BlockSpec(o.shape, lambda i, s, n=len(o.shape): (0,) * n) for o in shapes],
            scratch_shapes=list(scratch),
        ),
        cost_estimate=pl.CostEstimate(flops=1, bytes_accessed=1, transcendentals=0),
        name=name,
    )(places, *operands)
    return out[0] if single else out


ANY = pl.BlockSpec(memory_space=pl.ANY)


def contrib(places, h, mine, other, weight, weight_o, total=None):
    tokens, rows, cols = h.shape[0], *weight.shape

    def body(s, *refs):
        if total is None:
            a, b, w, wo, out = refs
            out[...] = dot(a[...], w[...]) + dot(b[...], wo[...])
        else:
            t, a, b, w, wo, out = refs
            out[...] = t[...] + dot(a[...], w[...]) + dot(b[...], wo[...])

    specs = [
        pl.BlockSpec((tokens, rows), lambda i, s: (0, s[mine])),
        pl.BlockSpec((tokens, rows), lambda i, s: (0, s[other])),
        whole(weight),
        whole(weight_o),
    ]
    operands = [h, h, weight, weight_o]
    if total is not None:
        specs.insert(0, whole(total))
        operands.insert(0, total)
    return call(body, places, operands, specs, jax.ShapeDtypeStruct((tokens, cols), jnp.float32), name="contrib")


def send_or_pass(places, h, piece, first, count):
    tokens, (rows, cols) = h.shape[0], piece.shape
    per_half = h.shape[1] // 2 // cols

    def body(s, *refs):
        blocks, piece_ref, out, sem = refs[:count], refs[count], refs[count + 1], refs[count + 2]

        @pl.when(s[END] == 1)
        def _():
            for k in range(count):
                out[k * tokens:(k + 1) * tokens, :] = blocks[k][...]
            if count * tokens < rows:
                out[count * tokens:, :] = jnp.zeros((rows - count * tokens, cols), out.dtype)

        @pl.when(s[END] == 0)
        def _():
            copy = pltpu.make_async_copy(piece_ref, out, sem)
            copy.start()
            copy.wait()

    specs = [
        pl.BlockSpec((tokens, cols), lambda i, s, k=k: (0, s[HALF] * per_half + first + k))
        for k in range(count)
    ]
    return call(
        body, places, [h] * count + [piece], specs + [ANY],
        jax.ShapeDtypeStruct(piece.shape, piece.dtype), [pltpu.SemaphoreType.DMA], name="send_or_pass",
    )


def choose(places, flag, yes, no):
    def body(s, yes_ref, no_ref, out, sem):
        @pl.when(s[flag] == 1)
        def _():
            copy = pltpu.make_async_copy(yes_ref, out, sem)
            copy.start()
            copy.wait()

        @pl.when(s[flag] == 0)
        def _():
            copy = pltpu.make_async_copy(no_ref, out, sem)
            copy.start()
            copy.wait()

    return call(
        body, places, [yes, no], [ANY, ANY], jax.ShapeDtypeStruct(yes.shape, yes.dtype),
        [pltpu.SemaphoreType.DMA], name="choose",
    )


def teachers(places, h, t_near, stale_opp, stale_opp_o, stale_far, stale_far_o, came_a, came_b):
    tokens, (rows, cols) = h.shape[0], stale_opp.shape
    fit = rows // tokens
    width = h.shape[1] // 2

    def body(s, near, p, po, r, ro, w, wo, v, vo, ca, cb, mine, sent, held):
        for k in range(width // cols):
            source = ca if k < fit else cb
            j = k if k < fit else k - fit
            held[:, k * cols:(k + 1) * cols] = source[j * tokens:(j + 1) * tokens, :]

        def cut(place):
            start = (s[place] - s[HALF] * (width // rows)) * rows
            return held[:, pl.ds(pl.multiple_of(start, 128), rows)]

        far = dot(p[...], w[...]) + dot(po[...], wo[...]) + dot(r[...], v[...]) + dot(ro[...], vo[...])
        mine[...] = (near[...] + jnp.where(s[END] == 1, 0.0, far)).astype(mine.dtype)
        end = dot(cut(OPP), w[...]) + dot(cut(OPP_O), wo[...])
        end = end + dot(cut(FAR), v[...]) + dot(cut(FAR_O), vo[...])
        sent[...] = end.astype(sent.dtype)

    def block(place):
        return pl.BlockSpec((tokens, rows), lambda i, s: (0, s[place]))

    operands = [t_near, h, h, h, h, stale_opp, stale_opp_o, stale_far, stale_far_o, came_a, came_b]
    specs = [whole(t_near), block(OPP), block(OPP_O), block(FAR), block(FAR_O)]
    specs += [whole(o) for o in operands[5:]]
    out = jax.ShapeDtypeStruct((tokens, cols), jnp.bfloat16)
    return call(
        body, places, operands, specs, [out, out], [pltpu.VMEM((tokens, width), h.dtype)], name="teachers"
    )


def difference(places, student, target_1, target_2, match):
    tokens = student.shape[0]

    def body(s, student_ref, one, two, match_ref, out):
        teacher = (one[...].astype(jnp.float32) + two[...].astype(jnp.float32)).astype(jnp.bfloat16)
        rows = lax.broadcasted_iota(jnp.int32, (tokens, tokens), 0)
        pick = (match_ref[...] == rows).astype(jnp.bfloat16)
        target = lax.dot_general(
            pick, teacher, (((0,), (0,)), ((), ())), preferred_element_type=jnp.float32
        )
        out[...] = (student_ref[...] - target).astype(out.dtype)

    operands = [student, target_1, target_2, match]
    return call(
        body, places, operands, [whole(o) for o in operands],
        jax.ShapeDtypeStruct(student.shape, jnp.bfloat16), name="difference",
    )


def gradient(places, left, left_o, near_own, far_own, near_x, far_x):
    tokens = left.shape[0]
    rows, cols = near_own[0].shape

    def body(s, left_ref, left_o_ref, *refs):
        sources, out, held, sems = refs[:16], refs[16], refs[17], refs[18]

        def copies(near):
            picked = []
            for k in range(4):
                picked.append(sources[k if near else 4 + k])
                picked.append(sources[8 + k if near else 12 + k])
            return [
                pltpu.make_async_copy(picked[j], held.at[j], sems.at[j]) for j in range(8)
            ]

        for near in (0, 1):
            @pl.when(s[NEAR] == near)
            def _(near=near):
                started = copies(near)
                for copy in started:
                    copy.start()
                for copy in started:
                    copy.wait()
        for k in range(4):
            value = dot_t(left_ref[...], held[2 * k]) + dot_t(left_o_ref[...], held[2 * k + 1])
            start = pl.multiple_of(s[PIECE + k] * rows, 128)
            out[:, pl.ds(start, rows)] = value.astype(out.dtype)

    operands = [left, left_o, *near_own, *far_own, *near_x, *far_x]
    return call(
        body, places, operands, [whole(left), whole(left_o)] + [ANY] * 16,
        jax.ShapeDtypeStruct((tokens, 4 * rows), jnp.bfloat16),
        [pltpu.VMEM((8, rows, cols), left.dtype), pltpu.SemaphoreType.DMA((8,))], name="gradient",
    )


def general(hidden, live_weight, stale_weight, match):
    hidden_rows = hidden[0]
    live_full = lax.all_gather(live_weight[0], "fsdp", axis=0, tiled=True)
    student = dot(hidden_rows, live_full)
    stale_full = lax.all_gather(stale_weight[0], "fsdp", axis=0, tiled=True)
    teacher = dot(hidden_rows, stale_full).astype(jnp.bfloat16)
    teacher = partner(teacher, "mp", 0)
    target = jnp.take(teacher, match[0], axis=0)
    mismatch = (student - target.astype(jnp.float32)).astype(jnp.bfloat16)
    partial_value = dot_t(mismatch, live_full).astype(jnp.bfloat16)
    summed = lax.psum_scatter(partial_value, "tp", scatter_dimension=1, tiled=True)
    return summed[None]


def line_of_four(hidden, live_weight, stale_weight, match):
    h, live, stale = hidden[0], live_weight[0], stale_weight[0]
    fit = live.shape[0] // h.shape[0]
    place = 2 * lax.axis_index("fsdp") + lax.axis_index("tp")
    places = lax.dynamic_index_in_dim(jnp.asarray(table()), place, 0, keepdims=False)

    live_mid = along_z(live, MID)
    live_nb = along_z(live, PAIR)
    stale_opp = along_z(stale, MID)
    stale_nb = along_z(stale, PAIR)
    x_own = near_over_x(live, True)
    live_o = across_cores(live)
    stale_o = across_cores(stale)
    student = contrib(places, h, OWN, OWN_O, live, live_o)
    t_near = contrib(places, h, OWN, OWN_O, stale, stale_o)

    mid_2, nb_2 = after((live_mid, live_nb), stale_opp, stale_nb, student, t_near)
    live_far_mid = along_z(nb_2, MID)
    came_a = along_z(send_or_pass(places, h, mid_2, 0, fit), PAIR)
    nb_x, stale_nb_2, stale_opp_2 = after((nb_2, stale_nb, stale_opp), x_own, live_o, stale_o)
    x_nb = near_over_x(nb_x, True)
    live_nb_o = across_cores(nb_x)
    stale_nb_o = across_cores(stale_nb_2)
    stale_opp_o = across_cores(stale_opp_2)
    x_own_o = across_cores(x_own)
    student = contrib(places, h, NB, NB_O, nb_x, live_nb_o, student)
    t_near = contrib(places, h, NB, NB_O, stale_nb_2, stale_nb_o, t_near)

    far_3, came_3, nb_3 = after(
        (live_far_mid, came_a, stale_nb), x_own_o, student, t_near, stale_opp_o
    )
    stale_far = along_z(nb_3, MID)
    came_b = along_z(send_or_pass(places, h, far_3, fit, h.shape[1] // 2 // live.shape[1] - fit), PAIR)
    came_x, mid_x = after((came_3, live_mid), x_nb)
    live_opp = choose(places, END, came_x, mid_x)
    x_opp = near_over_x(live_opp, False)
    live_opp_o = across_cores(live_opp)
    x_nb_o = across_cores(x_nb)
    student = contrib(places, h, OPP, OPP_O, live_opp, live_opp_o, student)

    stale_far, came_4, far_4 = after((stale_far, came_b, far_3), x_opp, live_opp_o, student, x_nb_o)
    stale_far_o = across_cores(stale_far)
    t_mine, t_end = teachers(
        places, h, t_near, stale_opp, stale_opp_o, stale_far, stale_far_o, came_3, came_4
    )
    live_far = choose(places, END, came_4, far_4)
    x_far = near_over_x(live_far, False)
    live_far_o = across_cores(live_far)
    x_opp_o = across_cores(x_opp)
    student = contrib(places, h, FAR, FAR_O, live_far, live_far_o, student)

    target_1 = partner(t_mine, "mp", 0)
    route = []
    for m in range(2):
        for a, b in OUT:
            for core in range(2):
                route.append((8 * m + 2 * a + core, 8 * (1 - m) + 2 * b + core))
    target_2 = lax.ppermute(t_end, ("mp", "fsdp"), route)
    mismatch = difference(places, student, target_1, target_2, match)
    mismatch_o = partner(mismatch, "tp", 0)
    (x_far,) = after((x_far,), mismatch)
    x_far_o = across_cores(x_far)
    grad = gradient(
        places, mismatch, mismatch_o,
        (live, live_o, live_nb, live_nb_o), (live_opp, live_opp_o, live_far, live_far_o),
        (x_own, x_own_o, x_nb, x_nb_o), (x_opp, x_opp_o, x_far, x_far_o),
    )
    return grad[None]


def solution(mesh):
    in_specs = (
        P("mp", "fsdp", None),
        P("mp", "fsdp", "tp"),
        P("mp", "fsdp", "tp"),
        P("mp", "fsdp"),
    )
    out_specs = P("mp", "fsdp", "tp")
    line = mesh.shape["fsdp"] == 8 and mesh.shape["tp"] == 2 and mesh.shape["mp"] == 2
    body = line_of_four if line else general
    return jax.shard_map(body, mesh=mesh, in_specs=in_specs, out_specs=out_specs, check_vma=False)
```

time: 165 us -> 130 us (0.79)
  waiting for transfers between devices: 137 us -> 49.4 us
  Pallas kernels: 0 us -> 44.8 us
  starting transfers between devices: 1.62 us -> 27.9 us
  between operations: 13.1 us -> 0.27 us
  matrix products: 11.6 us -> 0 us
  local copies, waits for them, and re-layouts: 0.94 us -> 6.72 us
    all_gather x2 -> x0, waiting for transfers between devices: 105 us -> none  [the longest x1 59 us: shards(): lax.all_gather(stale_piece, 'fsdp', axis=0, tiled=True)]
    pallas_call x0 -> x13, Pallas kernels: none -> 44.8 us  [call(): pl.pallas_call(body, out_shape=shapes, grid_spec=pltpu.PrefetchScalarGrid...]
    ppermute x0 -> x13, waiting for transfers between devices: none -> 42.7 us  [the longest x8 29.6 us: along_z(): return lax.ppermute(block, 'fsdp', route)]
    reduce_scatter x1 -> x0, waiting for transfers between devices: 25.7 us -> none  [shards(): lax.psum_scatter(partial_value.astype(jnp.bfloat16), 'tp', scatter_dimens...]
    ppermute x0 -> x13, starting transfers between devices: none -> 24.6 us  [the longest x8 17.8 us: along_z(): return lax.ppermute(block, 'fsdp', route)]
    dot_general x2 -> x0, matrix products: 11.6 us -> none  [the longest x1 8.07 us: shards(): lax.dot_general(mismatch, live_full, (((1,), (1,)), ((), ())), preferred_...]
    unnamed x4 -> x40, local copies, waits for them, and re-layouts: 0.01 us -> 5.44 us
    ppermute x1 -> x14, waiting for transfers between devices: 4.84 us -> 6.75 us  [partner(): return lax.ppermute(block, axis, route)]
  transfers between devices with their start and end apart: 4 -> 27, of which waited for: 4 -> 8; matrix products, arithmetic and copies ran while one was open for 3% -> 1% of each run, Pallas kernels for 0% -> 27%
where the time goes in v2:
time: 130 us; the launch traced here: 129 us
  waiting for transfers between devices  49.4 us (38%)
  Pallas kernels  44.8 us (34%)
  starting transfers between devices  27.9 us (21%)
  local copies, waits for them, and re-layouts  6.72 us (5%)
    pallas_call x13, Pallas kernels, call(): pl.pallas_call(body, out_shape=shapes, grid_spec=pltpu.PrefetchScalarGrid...  44.8 us
    ppermute x8, waiting for transfers between devices, along_z(): return lax.ppermute(block, 'fsdp', route)  29.6 us
    ppermute x8, starting transfers between devices, along_z(): return lax.ppermute(block, 'fsdp', route)  17.8 us
    ppermute x4, waiting for transfers between devices, near_over_x(): return lax.ppermute(block, ('fsdp', 'tp'), route)  8.37 us
    ppermute x14, waiting for transfers between devices, partner(): return lax.ppermute(block, axis, route)  6.75 us
    ppermute x4, starting transfers between devices, near_over_x(): return lax.ppermute(block, ('fsdp', 'tp'), route)  5.52 us
    unnamed x40, local copies, waits for them, and re-layouts  5.44 us
    ppermute x1, waiting for transfers between devices, line_of_four(): target_2 = lax.ppermute(t_end, ('mp', 'fsdp'), route)  4.72 us
  transfers between devices with their start and end apart: 27, of which 8 were waited for; matrix products, arithmetic and copies ran while one was open for 1% of the time, Pallas kernels for 27%

profile of v2, /device:TPU:0, one launch (start us, length us, event | category | flops | bytes accessed | tf_op | source)
XLA Modules:
  0.0 129.0 jit_solution(16750616429812403218)
XLA Ops:
  1.2 5.9 %collective-permute-start.2 = (bf16[640,512]{1,0:T(8,128)(2,1)}, bf16[640,512]{1,0:T(8,128)(2,1)S(1)}, u32[]{:S(2)}, u32[]{:S(2)}) collective-permute-start(bf16[640,512]{1,0:T(8,128)(2,1)} %bitcast.29), channel_id=1, source_target_pairs={{0,4},{2,6},{4,0},{6,2},{8,12},{10,14},{12,8},{14,10},{1,5},{3,7},... | collective-permute-start | bytes 1966088 | tf_op jit(solution)/shard_map/ppermute | solution.py:47
  12.1 3.3 %contrib.6.refs_0_ = f32[160,512]{1,0:T(8,128)} custom-call(s32[15]{0:T(128)} %dynamic-slice_bitcast_fusion.s, bf16[160,5120]{1,0:T(8,128)(2,1)} %bitcast.6, bf16[160,5120]{1,0:T(8,128)(2,1)} %bitcast.7, bf16[640,512]{1,0:T(8,128)(2,1)} %bitcast.31, bf16[640,512]{1,0:T(8,128)(2,1)} %copy-done), custom_call_target="tpu_custom_call" | custom-call | flops 1 | bytes 1 | tf_op jit(solution)/shard_map/contrib/pallas_call | solution.py:83
  15.5 3.3 %contrib.7.refs_0_ = f32[160,512]{1,0:T(8,128)} custom-call(s32[15]{0:T(128)} %dynamic-slice_bitcast_fusion.s, bf16[160,5120]{1,0:T(8,128)(2,1)} %bitcast.8, bf16[160,5120]{1,0:T(8,128)(2,1)} %bitcast.9, bf16[640,512]{1,0:T(8,128)(2,1)} %bitcast.36, bf16[640,512]{1,0:T(8,128)(2,1)} %copy-done.15), custom_call_target="tpu_custom_call" | custom-call | flops 1 | bytes 1 | tf_op jit(solution)/shard_map/contrib/pallas_call | solution.py:83
  18.8 4.1 %collective-permute-done.2.refs_3_.refs_2_ = bf16[640,512]{1,0:T(8,128)(2,1)S(1)} collective-permute-done((bf16[640,512]{1,0:T(8,128)(2,1)}, bf16[640,512]{1,0:T(8,128)(2,1)S(1)}, u32[]{:S(2)}, u32[]{:S(2)}) %collective-permute-start.2) | collective-permute-done | bytes 655392 | tf_op jit(solution)/shard_map/ppermute | solution.py:47
  22.9 13.2 %collective-permute-done.4.refs_3_ = bf16[640,512]{1,0:T(8,128)(2,1)} collective-permute-done((bf16[640,512]{1,0:T(8,128)(2,1)}, bf16[640,512]{1,0:T(8,128)(2,1)}, u32[]{:S(2)}, u32[]{:S(2)}) %collective-permute-start.4) | collective-permute-done | bytes 655392 | tf_op jit(solution)/shard_map/ppermute | solution.py:47
  37.4 2.8 %send_or_pass.2 = bf16[640,512]{1,0:T(8,128)(2,1)} custom-call(s32[15]{0:T(128)} %dynamic-slice_bitcast_fusion.s, bf16[160,5120]{1,0:T(8,128)(2,1)} %bitcast.10, bf16[160,5120]{1,0:T(8,128)(2,1)} %bitcast.11, bf16[160,5120]{1,0:T(8,128)(2,1)} %bitcast.12, bf16[160,5120]{1,0:T(8,128)(2,1)} %bitcast.13, bf16[640,512]{1,0:T(8,128)(2,1)} %copy-done.6), custom_call_target="tpu_custom_call" | custom-call | flops 1 | bytes 1 | tf_op jit(solution)/shard_map/send_or_pass/pallas_call | solution.py:83
  40.2 4.5 %collective-permute-start.9 = (bf16[640,512]{1,0:T(8,128)(2,1)}, bf16[640,512]{1,0:T(8,128)(2,1)S(1)}, u32[]{:S(2)}, u32[]{:S(2)}) collective-permute-start(bf16[640,512]{1,0:T(8,128)(2,1)} %send_or_pass.2), channel_id=1, source_target_pairs={{0,4},{2,6},{4,0},{6,2},{8,12},{10,14},{12,8},{14,10},{1,5},{3,7},... | collective-permute-start | bytes 1966088 | tf_op jit(solution)/shard_map/ppermute | solution.py:47
  46.2 3.3 %contrib.9.near = f32[160,512]{1,0:T(8,128)} custom-call(s32[15]{0:T(128)} %dynamic-slice_bitcast_fusion.s, f32[160,512]{1,0:T(8,128)} %contrib.7.refs_0_, bf16[160,5120]{1,0:T(8,128)(2,1)} %bitcast.14, bf16[160,5120]{1,0:T(8,128)(2,1)} %bitcast.15, bf16[640,512]{1,0:T(8,128)(2,1)} %collective-permute-done.4.refs_3_, ...), custom_call_target="tpu_custom_call" | custom-call | flops 1 | bytes 1 | tf_op jit(solution)/shard_map/contrib/pallas_call | solution.py:83
  49.5 3.3 %contrib.8.refs_0_ = f32[160,512]{1,0:T(8,128)} custom-call(s32[15]{0:T(128)} %dynamic-slice_bitcast_fusion.s, f32[160,512]{1,0:T(8,128)} %contrib.6.refs_0_, bf16[160,5120]{1,0:T(8,128)(2,1)} %bitcast.16, bf16[160,5120]{1,0:T(8,128)(2,1)} %bitcast.17, bf16[640,512]{1,0:T(8,128)(2,1)} %copy-done.1, bf16[640,512]{1,0:T(8,128)(2,1)} %copy-done.2), custom_call_target="tpu_custom_call" | custom-call | flops 1 | bytes 1 | tf_op jit(solution)/shard_map/contrib/pallas_call | solution.py:83
  52.8 7.5 %collective-permute-done.9.yes_ref.ca = bf16[640,512]{1,0:T(8,128)(2,1)S(1)} collective-permute-done((bf16[640,512]{1,0:T(8,128)(2,1)}, bf16[640,512]{1,0:T(8,128)(2,1)S(1)}, u32[]{:S(2)}, u32[]{:S(2)}) %collective-permute-start.9) | collective-permute-done | bytes 655392 | tf_op jit(solution)/shard_map/ppermute | solution.py:47
  60.3 3.6 %collective-permute-done.13.refs_10_ = bf16[640,512]{1,0:T(8,128)(2,1)} collective-permute-done((bf16[640,512]{1,0:T(8,128)(2,1)S(1)}, bf16[640,512]{1,0:T(8,128)(2,1)}, u32[]{:S(2)}, u32[]{:S(2)}) %collective-permute-start.13) | collective-permute-done | bytes 655392 | tf_op jit(solution)/shard_map/ppermute | solution.py:60
  63.8 2.6 %choose.2.refs_3_.refs_4_ = bf16[640,512]{1,0:T(8,128)(2,1)} custom-call(s32[15]{0:T(128)} %dynamic-slice_bitcast_fusion.s, bf16[640,512]{1,0:T(8,128)(2,1)} %copy-done.7, bf16[640,512]{1,0:T(8,128)(2,1)} %copy-done.6), custom_call_target="tpu_custom_call" | custom-call | flops 1 | bytes 1 | tf_op jit(solution)/shard_map/choose/pallas_call | solution.py:83
  67.9 2.5 %send_or_pass.3 = bf16[640,512]{1,0:T(8,128)(2,1)} custom-call(s32[15]{0:T(128)} %dynamic-slice_bitcast_fusion.s, bf16[160,5120]{1,0:T(8,128)(2,1)} %bitcast.18, bf16[640,512]{1,0:T(8,128)(2,1)} %copy-done.5), custom_call_target="tpu_custom_call" | custom-call | flops 1 | bytes 1 | tf_op jit(solution)/shard_map/send_or_pass/pallas_call | solution.py:83
  70.4 2.2 %collective-permute-start.16 = (bf16[640,512]{1,0:T(8,128)(2,1)}, bf16[640,512]{1,0:T(8,128)(2,1)S(1)}, u32[]{:S(2)}, u32[]{:S(2)}) collective-permute-start(bf16[640,512]{1,0:T(8,128)(2,1)} %send_or_pass.3), channel_id=1, source_target_pairs={{0,4},{2,6},{4,0},{6,2},{8,12},{10,14},{12,8},{14,10},{1,5},{3,7},... | collective-permute-start | bytes 1966088 | tf_op jit(solution)/shard_map/ppermute | solution.py:47
  74.9 3.3 %contrib.10.refs_0_ = f32[160,512]{1,0:T(8,128)} custom-call(s32[15]{0:T(128)} %dynamic-slice_bitcast_fusion.s, f32[160,512]{1,0:T(8,128)} %contrib.8.refs_0_, bf16[160,5120]{1,0:T(8,128)(2,1)} %bitcast.19, bf16[160,5120]{1,0:T(8,128)(2,1)} %bitcast.20, bf16[640,512]{1,0:T(8,128)(2,1)} %choose.2.refs_3_.refs_4_, bf16[640,512]{1,0:T(8,128)(2,1)} %copy-done.3), custom_call_target="tpu_custom_call" | custom-call | flops 1 | bytes 1 | tf_op jit(solution)/shard_map/contrib/pallas_call | solution.py:83
  78.2 4.8 %collective-permute-done.17.refs_12_ = bf16[640,512]{1,0:T(8,128)(2,1)S(1)} collective-permute-done((bf16[640,512]{1,0:T(8,128)(2,1)}, bf16[640,512]{1,0:T(8,128)(2,1)S(1)}, u32[]{:S(2)}, u32[]{:S(2)}) %collective-permute-start.17) | collective-permute-done | bytes 655392 | tf_op jit(solution)/shard_map/ppermute | solution.py:60
  83.0 4.8 %collective-permute-done.16.yes_ref.cb = bf16[640,512]{1,0:T(8,128)(2,1)S(1)} collective-permute-done((bf16[640,512]{1,0:T(8,128)(2,1)}, bf16[640,512]{1,0:T(8,128)(2,1)S(1)}, u32[]{:S(2)}, u32[]{:S(2)}) %collective-permute-start.16) | collective-permute-done | bytes 655392 | tf_op jit(solution)/shard_map/ppermute | solution.py:47
  88.7 2.6 %choose.3.refs_3_.refs_6_ = bf16[640,512]{1,0:T(8,128)(2,1)} custom-call(s32[15]{0:T(128)} %dynamic-slice_bitcast_fusion.s, bf16[640,512]{1,0:T(8,128)(2,1)} %copy-done.8, bf16[640,512]{1,0:T(8,128)(2,1)} %copy-done.5), custom_call_target="tpu_custom_call" | custom-call | flops 1 | bytes 1 | tf_op jit(solution)/shard_map/choose/pallas_call | solution.py:83
  93.8 5.0 %teachers.1 = (bf16[160,512]{1,0:T(8,128)(2,1)}, bf16[160,512]{1,0:T(8,128)(2,1)}) custom-call(s32[15]{0:T(128)} %dynamic-slice_bitcast_fusion.s, f32[160,512]{1,0:T(8,128)} %contrib.9.near, bf16[160,5120]{1,0:T(8,128)(2,1)} %bitcast.21, bf16[160,5120]{1,0:T(8,128)(2,1)} %bitcast.22, bf16[160,5120]{1,0:T(8,128)(2,1)} %bitcast.23, ...), custom_call_target="tpu_custom_call" | custom-call | flops 1 | bytes 1 | tf_op jit(solution)/shard_map/teachers/pallas_call | solution.py:83
  102.6 3.3 %contrib.11.student_ref = f32[160,512]{1,0:T(8,128)} custom-call(s32[15]{0:T(128)} %dynamic-slice_bitcast_fusion.s, f32[160,512]{1,0:T(8,128)} %contrib.10.refs_0_, bf16[160,5120]{1,0:T(8,128)(2,1)} %bitcast.25, bf16[160,5120]{1,0:T(8,128)(2,1)} %bitcast.26, bf16[640,512]{1,0:T(8,128)(2,1)} %choose.3.refs_3_.refs_6_, bf16[640,512]{1,0:T(8,128)(2,1)} %copy-done.4), custom_call_target="tpu_custom_call" | custom-call | flops 1 | bytes 1 | tf_op jit(solution)/shard_map/contrib/pallas_call | solution.py:83
  105.9 4.7 %collective-permute-done.22.two = bf16[160,512]{1,0:T(8,128)(2,1)S(1)} collective-permute-done((bf16[160,512]{1,0:T(8,128)(2,1)}, bf16[160,512]{1,0:T(8,128)(2,1)S(1)}, u32[]{:S(2)}, u32[]{:S(2)}) %collective-permute-start.22) | collective-permute-done | bytes 163872 | tf_op jit(solution)/shard_map/ppermute | solution.py:336
  111.3 2.7 %difference.1.left_ref = bf16[160,512]{1,0:T(8,128)(2,1)} custom-call(s32[15]{0:T(128)} %dynamic-slice_bitcast_fusion.s, f32[160,512]{1,0:T(8,128)} %contrib.11.student_ref, bf16[160,512]{1,0:T(8,128)(2,1)} %copy-done.17, bf16[160,512]{1,0:T(8,128)(2,1)} %copy-done.18, s32[1,160]{1,0:T(1,128)} %match_ref.1), custom_call_target="tpu_custom_call" | custom-call | flops 1 | bytes 1 | tf_op jit(solution)/shard_map/difference/pallas_call | solution.py:83
  114.0 6.7 %collective-permute-done.23.left_o_ref = bf16[160,512]{1,0:T(8,128)(2,1)S(1)} collective-permute-done((bf16[160,512]{1,0:T(8,128)(2,1)}, bf16[160,512]{1,0:T(8,128)(2,1)S(1)}, u32[]{:S(2)}, u32[]{:S(2)}) %collective-permute-start.23) | collective-permute-done | bytes 163872 | tf_op jit(solution)/shard_map/ppermute | solution.py:42
  122.2 6.8 %gradient.1 = bf16[160,2560]{1,0:T(8,128)(2,1)} custom-call(s32[15]{0:T(128)} %dynamic-slice_bitcast_fusion.s, bf16[160,512]{1,0:T(8,128)(2,1)} %difference.1.left_ref, bf16[160,512]{1,0:T(8,128)(2,1)} %copy-done.19, bf16[640,512]{1,0:T(8,128)(2,1)} %bitcast.32, bf16[640,512]{1,0:T(8,128)(2,1)} %copy-done, bf16[640,512]{1,0:T(8,128)(2,1)} %copy-done.1, ...), custom_call_target="tpu_custom_call" | custom-call | flops 1 | bytes 1 | tf_op jit(solution)/shard_map/gradient/pallas_call | solution.py:83
  (84 shorter events, 22.1 us)
Async XLA Ops:
  0.0 8.6 %collective-permute-start = (bf16[640,512]{1,0:T(8,128)(2,1)}, bf16[640,512]{1,0:T(8,128)(2,1)S(1)}, u32[]{:S(2)}, u32[]{:S(2)}) collective-permute-start(bf16[640,512]{1,0:T(8,128)(2,1)} %bitcast.27), channel_id=1, source_target_pairs={{0,2},{2,0},{4,6},{6,4},{8,10},{10,8},{12,14},{14,12},{1,3},{3,1},... | collective-permute-start | bytes 1966088 | tf_op jit(solution)/shard_map/ppermute | solution.py:42
  0.5 9.1 %collective-permute-start.5 = (bf16[640,512]{1,0:T(8,128)(2,1)}, bf16[640,512]{1,0:T(8,128)(2,1)S(1)}, u32[]{:S(2)}, u32[]{:S(2)}) collective-permute-start(bf16[640,512]{1,0:T(8,128)(2,1)} %bitcast.33), channel_id=1, source_target_pairs={{0,2},{2,0},{4,6},{6,4},{8,10},{10,8},{12,14},{14,12},{1,3},{3,1},... | collective-permute-start | bytes 1966088 | tf_op jit(solution)/shard_map/ppermute | solution.py:42
  0.5 18.3 %collective-permute-start.1 = (bf16[640,512]{1,0:T(8,128)(2,1)}, bf16[640,512]{1,0:T(8,128)(2,1)S(1)}, u32[]{:S(2)}, u32[]{:S(2)}) collective-permute-start(bf16[640,512]{1,0:T(8,128)(2,1)} %bitcast.28), channel_id=1, source_target_pairs={{4,8},{6,10},{8,4},{10,6},{5,9},{7,11},{9,5},{11,7},{20,24},{22,26... | collective-permute-start | bytes 1966088 | tf_op jit(solution)/shard_map/ppermute | solution.py:47
  1.2 21.7 %collective-permute-start.2 = (bf16[640,512]{1,0:T(8,128)(2,1)}, bf16[640,512]{1,0:T(8,128)(2,1)S(1)}, u32[]{:S(2)}, u32[]{:S(2)}) collective-permute-start(bf16[640,512]{1,0:T(8,128)(2,1)} %bitcast.29), channel_id=1, source_target_pairs={{0,4},{2,6},{4,0},{6,2},{8,12},{10,14},{12,8},{14,10},{1,5},{3,7},... | collective-permute-start | bytes 1966088 | tf_op jit(solution)/shard_map/ppermute | solution.py:47
  7.1 15.8 %collective-permute-start.3 = (bf16[640,512]{1,0:T(8,128)(2,1)}, bf16[640,512]{1,0:T(8,128)(2,1)}, u32[]{:S(2)}, u32[]{:S(2)}) collective-permute-start(bf16[640,512]{1,0:T(8,128)(2,1)} %bitcast.34), channel_id=1, source_target_pairs={{4,8},{6,10},{8,4},{10,6},{5,9},{7,11},{9,5},{11,7},{20,24},{22,26... | collective-permute-start | bytes 1966088 | tf_op jit(solution)/shard_map/ppermute | solution.py:47
  8.6 27.5 %collective-permute-start.4 = (bf16[640,512]{1,0:T(8,128)(2,1)}, bf16[640,512]{1,0:T(8,128)(2,1)}, u32[]{:S(2)}, u32[]{:S(2)}) collective-permute-start(bf16[640,512]{1,0:T(8,128)(2,1)} %bitcast.35), channel_id=1, source_target_pairs={{0,4},{2,6},{4,0},{6,2},{8,12},{10,14},{12,8},{14,10},{1,5},{3,7},... | collective-permute-start | bytes 1966088 | tf_op jit(solution)/shard_map/ppermute | solution.py:47
  9.6 26.5 %collective-permute-start.6 = (bf16[640,512]{1,0:T(8,128)(2,1)}, bf16[640,512]{1,0:T(8,128)(2,1)S(1)}, u32[]{:S(2)}, u32[]{:S(2)}) collective-permute-start(bf16[640,512]{1,0:T(8,128)(2,1)} %bitcast.30), channel_id=1, source_target_pairs={{1,0},{3,2},{5,4},{7,6},{8,9},{10,11},{12,13},{14,15},{17,16},{19,... | collective-permute-start | bytes 1966088 | tf_op jit(solution)/shard_map/ppermute | solution.py:60
  36.1 8.6 %collective-permute-start.11 = (bf16[640,512]{1,0:T(8,128)(2,1)}, bf16[640,512]{1,0:T(8,128)(2,1)}, u32[]{:S(2)}, u32[]{:S(2)}) collective-permute-start(bf16[640,512]{1,0:T(8,128)(2,1)} %collective-permute-done.4.refs_3_), channel_id=1, source_target_pairs={{0,2},{2,0},{4,6},{6,4},{8,10},{10,8},{12,14},{14,12},{1,3},{3,1},... | collective-permute-start | bytes 1966088 | tf_op jit(solution)/shard_map/ppermute | solution.py:42
  36.1 8.8 %collective-permute-start.7 = (bf16[640,512]{1,0:T(8,128)(2,1)S(1)}, bf16[640,512]{1,0:T(8,128)(2,1)S(1)}, u32[]{:S(2)}, u32[]{:S(2)}) collective-permute-start(bf16[640,512]{1,0:T(8,128)(2,1)S(1)} %collective-permute-done.2.refs_3_.refs_2_), channel_id=1, source_target_pairs={{0,2},{2,0},{4,6},{6,4},{8,10},{10,8},{12,14},{14,12},{1,3},{3,1},... | collective-permute-start | bytes 1966088 | tf_op jit(solution)/shard_map/ppermute | solution.py:42
  36.6 23.7 %collective-permute-start.8 = (bf16[640,512]{1,0:T(8,128)(2,1)S(1)}, bf16[640,512]{1,0:T(8,128)(2,1)S(1)}, u32[]{:S(2)}, u32[]{:S(2)}) collective-permute-start(bf16[640,512]{1,0:T(8,128)(2,1)S(1)} %collective-permute-done.2.refs_3_.refs_2_), channel_id=1, source_target_pairs={{4,8},{6,10},{8,4},{10,6},{5,9},{7,11},{9,5},{11,7},{20,24},{22,26... | collective-permute-start | bytes 1966088 | tf_op jit(solution)/shard_map/ppermute | solution.py:47
  37.3 15.5 %collective-permute-start.12 = (bf16[640,512]{1,0:T(8,128)(2,1)}, bf16[640,512]{1,0:T(8,128)(2,1)}, u32[]{:S(2)}, u32[]{:S(2)}) collective-permute-start(bf16[640,512]{1,0:T(8,128)(2,1)} %collective-permute-done.3.w), channel_id=1, source_target_pairs={{0,2},{2,0},{4,6},{6,4},{8,10},{10,8},{12,14},{14,12},{1,3},{3,1},... | collective-permute-start | bytes 1966088 | tf_op jit(solution)/shard_map/ppermute | solution.py:42
  40.2 20.0 %collective-permute-start.9 = (bf16[640,512]{1,0:T(8,128)(2,1)}, bf16[640,512]{1,0:T(8,128)(2,1)S(1)}, u32[]{:S(2)}, u32[]{:S(2)}) collective-permute-start(bf16[640,512]{1,0:T(8,128)(2,1)} %send_or_pass.2), channel_id=1, source_target_pairs={{0,4},{2,6},{4,0},{6,2},{8,12},{10,14},{12,8},{14,10},{1,5},{3,7},... | collective-permute-start | bytes 1966088 | tf_op jit(solution)/shard_map/ppermute | solution.py:47
  44.7 15.6 %collective-permute-start.10 = (bf16[640,512]{1,0:T(8,128)(2,1)S(1)}, bf16[640,512]{1,0:T(8,128)(2,1)}, u32[]{:S(2)}, u32[]{:S(2)}) collective-permute-start(bf16[640,512]{1,0:T(8,128)(2,1)S(1)} %collective-permute-done.6.refs_8_), channel_id=1, source_target_pairs={{0,2},{2,0},{4,6},{6,4},{8,10},{10,8},{12,14},{14,12},{1,3},{3,1},... | collective-permute-start | bytes 1966088 | tf_op jit(solution)/shard_map/ppermute | solution.py:42
  44.9 18.9 %collective-permute-start.13 = (bf16[640,512]{1,0:T(8,128)(2,1)S(1)}, bf16[640,512]{1,0:T(8,128)(2,1)}, u32[]{:S(2)}, u32[]{:S(2)}) collective-permute-start(bf16[640,512]{1,0:T(8,128)(2,1)S(1)} %collective-permute-done.2.refs_3_.refs_2_), channel_id=1, source_target_pairs={{1,0},{3,2},{5,4},{7,6},{8,9},{10,11},{12,13},{14,15},{17,16},{19,... | collective-permute-start | bytes 1966088 | tf_op jit(solution)/shard_map/ppermute | solution.py:60
  66.4 7.6 %collective-permute-start.14 = (bf16[640,512]{1,0:T(8,128)(2,1)}, bf16[640,512]{1,0:T(8,128)(2,1)S(1)}, u32[]{:S(2)}, u32[]{:S(2)}) collective-permute-start(bf16[640,512]{1,0:T(8,128)(2,1)} %choose.2.refs_3_.refs_4_), channel_id=1, source_target_pairs={{0,2},{2,0},{4,6},{6,4},{8,10},{10,8},{12,14},{14,12},{1,3},{3,1},... | collective-permute-start | bytes 1966088 | tf_op jit(solution)/shard_map/ppermute | solution.py:42
  66.5 16.5 %collective-permute-start.17 = (bf16[640,512]{1,0:T(8,128)(2,1)}, bf16[640,512]{1,0:T(8,128)(2,1)S(1)}, u32[]{:S(2)}, u32[]{:S(2)}) collective-permute-start(bf16[640,512]{1,0:T(8,128)(2,1)} %choose.2.refs_3_.refs_4_), channel_id=1, source_target_pairs={{0,1},{2,3},{4,5},{6,7},{9,8},{11,10},{13,12},{15,14},{16,17},{18,... | collective-permute-start | bytes 1966088 | tf_op jit(solution)/shard_map/ppermute | solution.py:60
  70.4 17.5 %collective-permute-start.16 = (bf16[640,512]{1,0:T(8,128)(2,1)}, bf16[640,512]{1,0:T(8,128)(2,1)S(1)}, u32[]{:S(2)}, u32[]{:S(2)}) collective-permute-start(bf16[640,512]{1,0:T(8,128)(2,1)} %send_or_pass.3), channel_id=1, source_target_pairs={{0,4},{2,6},{4,0},{6,2},{8,12},{10,14},{12,8},{14,10},{1,5},{3,7},... | collective-permute-start | bytes 1966088 | tf_op jit(solution)/shard_map/ppermute | solution.py:47
  72.5 15.3 %collective-permute-start.15 = (bf16[640,512]{1,0:T(8,128)(2,1)}, bf16[640,512]{1,0:T(8,128)(2,1)}, u32[]{:S(2)}, u32[]{:S(2)}) collective-permute-start(bf16[640,512]{1,0:T(8,128)(2,1)} %collective-permute-done.4.refs_3_), channel_id=1, source_target_pairs={{4,8},{6,10},{8,4},{10,6},{5,9},{7,11},{9,5},{11,7},{20,24},{22,26... | collective-permute-start | bytes 1966088 | tf_op jit(solution)/shard_map/ppermute | solution.py:47
  74.0 13.8 %collective-permute-start.18 = (bf16[640,512]{1,0:T(8,128)(2,1)}, bf16[640,512]{1,0:T(8,128)(2,1)S(1)}, u32[]{:S(2)}, u32[]{:S(2)}) collective-permute-start(bf16[640,512]{1,0:T(8,128)(2,1)} %collective-permute-done.13.refs_10_), channel_id=1, source_target_pairs={{0,2},{2,0},{4,6},{6,4},{8,10},{10,8},{12,14},{14,12},{1,3},{3,1},... | collective-permute-start | bytes 1966088 | tf_op jit(solution)/shard_map/ppermute | solution.py:42
  91.3 10.4 %collective-permute-start.19 = (bf16[640,512]{1,0:T(8,128)(2,1)}, bf16[640,512]{1,0:T(8,128)(2,1)S(1)}, u32[]{:S(2)}, u32[]{:S(2)}) collective-permute-start(bf16[640,512]{1,0:T(8,128)(2,1)} %choose.3.refs_3_.refs_6_), channel_id=1, source_target_pairs={{0,2},{2,0},{4,6},{6,4},{8,10},{10,8},{12,14},{14,12},{1,3},{3,1},... | collective-permute-start | bytes 1966088 | tf_op jit(solution)/shard_map/ppermute | solution.py:42
  91.4 22.5 %collective-permute-start.25 = (bf16[640,512]{1,0:T(8,128)(2,1)}, bf16[640,512]{1,0:T(8,128)(2,1)S(1)}, u32[]{:S(2)}, u32[]{:S(2)}) collective-permute-start(bf16[640,512]{1,0:T(8,128)(2,1)} %choose.3.refs_3_.refs_6_), channel_id=1, source_target_pairs={{0,1},{2,3},{4,5},{6,7},{9,8},{11,10},{13,12},{15,14},{16,17},{18,... | collective-permute-start | bytes 1966088 | tf_op jit(solution)/shard_map/ppermute | solution.py:60
  98.8 7.0 %collective-permute-start.21 = (bf16[160,512]{1,0:T(8,128)(2,1)}, bf16[160,512]{1,0:T(8,128)(2,1)S(1)}, u32[]{:S(2)}, u32[]{:S(2)}) collective-permute-start(bf16[160,512]{1,0:T(8,128)(2,1)} %get-tuple-element.34), channel_id=1, source_target_pairs={{0,16},{16,0},{1,17},{17,1},{2,18},{18,2},{3,19},{19,3},{4,20},{20... | collective-permute-start | bytes 491528 | tf_op jit(solution)/shard_map/ppermute | solution.py:42
  100.3 10.2 %collective-permute-start.22 = (bf16[160,512]{1,0:T(8,128)(2,1)}, bf16[160,512]{1,0:T(8,128)(2,1)S(1)}, u32[]{:S(2)}, u32[]{:S(2)}) collective-permute-start(bf16[160,512]{1,0:T(8,128)(2,1)} %get-tuple-element.35), channel_id=1, source_target_pairs={{4,16},{6,18},{8,28},{10,30},{20,0},{22,2},{24,12},{26,14},{5,17},... | collective-permute-start | bytes 491528 | tf_op jit(solution)/shard_map/ppermute | solution.py:336
  101.6 12.4 %collective-permute-start.24 = (bf16[640,512]{1,0:T(8,128)(2,1)S(1)}, bf16[640,512]{1,0:T(8,128)(2,1)S(1)}, u32[]{:S(2)}, u32[]{:S(2)}) collective-permute-start(bf16[640,512]{1,0:T(8,128)(2,1)S(1)} %collective-permute-done.17.refs_12_), channel_id=1, source_target_pairs={{0,2},{2,0},{4,6},{6,4},{8,10},{10,8},{12,14},{14,12},{1,3},{3,1},... | collective-permute-start | bytes 1966088 | tf_op jit(solution)/shard_map/ppermute | solution.py:42
  (23 other events, 146.7 us)

commit v3 on v2

v3 whole, which is shorter than its diff:
```python
import jax
import jax.numpy as jnp
import numpy as np
from jax import lax
from jax.experimental import pallas as pl
from jax.experimental.pallas import tpu as pltpu
from jax.sharding import PartitionSpec as P

PAIR = ((0, 1), (1, 0), (2, 3), (3, 2))
MID = ((1, 2), (2, 1))
OUT = ((1, 0), (2, 3))

OWN, OWN_O, NB, NB_O, OPP, OPP_O, FAR, FAR_O, END, NEAR, HALF, PIECE = range(12)


def table():
    rows = []
    for f in range(8):
        for x in range(2):
            z, c = f // 2, f % 2
            half = z // 2
            opp, far = (2, 3) if half == 0 else (1, 0)
            near = int(half == x)
            first = z % 2 if near else half
            row = []
            for q in (z, z ^ 1, opp, far):
                row += [2 * q + c, 2 * q + 1 - c]
            row += [int(z in (0, 3)), near, 1 - half]
            for q in (first, 1 - first):
                row += [2 * q + c, 2 * q + 1 - c]
            rows.append(row)
    return np.array(rows, np.int32)


def partner(block, axis, apart):
    count = lax.axis_size(axis)
    route = []
    for low in range(count):
        high = low | 1 << apart
        if high != low and high < count:
            route += [(low, high), (high, low)]
    return lax.ppermute(block, axis, route)


def along_z(block, pairs):
    route = [(2 * a + c, 2 * b + c) for a, b in pairs for c in range(2)]
    return lax.ppermute(block, "fsdp", route)


def across_cores(block):
    return partner(block, "fsdp", 0)


def over_x(block, middle):
    route = []
    for f in range(8):
        half, z = f // 4, f // 2
        if middle in (False, True):
            route.append((2 * f + 1 - half, 2 * f + half))
        if middle is None or z in ((1, 2) if middle is True else (0, 3) if middle == END else ()):
            route.append((2 * f + half, 2 * f + 1 - half))
    return lax.ppermute(block, ("fsdp", "tp"), route)


def after(values, *gates):
    out = lax.optimization_barrier((tuple(values), gates))
    return out[0]


def dot(a, b):
    return jnp.dot(a, b, preferred_element_type=jnp.float32)


def dot_t(a, b):
    return lax.dot_general(a, b, (((1,), (1,)), ((), ())), preferred_element_type=jnp.float32)


def call(body, places, operands, outs, name):
    single = not isinstance(outs, (list, tuple))
    shapes = [outs] if single else list(outs)
    out = pl.pallas_call(
        body,
        out_shape=shapes,
        in_specs=[pl.BlockSpec(memory_space=pltpu.SMEM)] + [pl.BlockSpec(memory_space=pltpu.VMEM)] * len(operands),
        out_specs=[pl.BlockSpec(memory_space=pltpu.VMEM)] * len(shapes),
        cost_estimate=pl.CostEstimate(flops=1, bytes_accessed=1, transcendentals=0),
        compiler_params=pltpu.CompilerParams(vmem_limit_bytes=16 * 2 ** 20),
        name=name,
    )(places, *operands)
    return out[0] if single else out


def columns(ref, start, size):
    return ref[:, pl.ds(pl.multiple_of(start, 128), size)]


def contrib(places, h, mine, other, weight, weight_o, total=None):
    tokens, rows, cols = h.shape[0], *weight.shape

    def body(s, h_ref, w, wo, *rest):
        value = dot(columns(h_ref, s[mine] * rows, rows), w[...])
        value = value + dot(columns(h_ref, s[other] * rows, rows), wo[...])
        if total is not None:
            value = value + rest[0][...]
        rest[-1][...] = value

    operands = [h, weight, weight_o] + ([] if total is None else [total])
    return call(body, places, operands, jax.ShapeDtypeStruct((tokens, cols), jnp.float32), "contrib")


def as_rows(places, h, shape, first, piece=None):
    tokens, (rows, cols) = h.shape[0], shape
    total = h.shape[1] // 2

    def body(s, h_ref, *refs):
        out = refs[-1]

        @pl.when(s[END] == 1)
        def _():
            count = min(rows // tokens, total // cols - first)
            for k in range(count):
                start = s[HALF] * total + (first + k) * cols
                out[k * tokens:(k + 1) * tokens, :] = columns(h_ref, start, cols)
            if count * tokens < rows:
                out[count * tokens:, :] = jnp.zeros((rows - count * tokens, cols), out.dtype)

        @pl.when(s[END] == 0)
        def _():
            out[...] = jnp.zeros(shape, out.dtype) if piece is None else refs[0][...]

    return call(
        body, places, [h] + ([] if piece is None else [piece]), jax.ShapeDtypeStruct(shape, h.dtype), "as_rows"
    )


def choose(places, flag, yes, no):
    def body(s, yes_ref, no_ref, out):
        @pl.when(s[flag] == 1)
        def _():
            out[...] = yes_ref[...]

        @pl.when(s[flag] == 0)
        def _():
            out[...] = no_ref[...]

    return call(body, places, [yes, no], jax.ShapeDtypeStruct(yes.shape, yes.dtype), "choose")


def tick(places, value):
    def body(s, value_ref, out):
        out[...] = value_ref[:16, :128]

    return call(body, places, [value], jax.ShapeDtypeStruct((16, 128), value.dtype), "tick")


def to_opposite(places, h, total, nb, nb_o, opp, opp_o):
    tokens, (rows, cols) = h.shape[0], nb.shape

    def body(s, h_ref, total_ref, n, no, p, po, out):
        value = total_ref[...]
        for place, weight in ((NB, n), (NB_O, no)):
            value = value + dot(columns(h_ref, s[place] * rows, rows), weight[...])
        out[...] = value

        @pl.when(s[END] == 0)
        def _():
            more = dot(columns(h_ref, s[OPP] * rows, rows), p[...])
            out[...] += more + dot(columns(h_ref, s[OPP_O] * rows, rows), po[...])

    return call(
        body, places, [h, total, nb, nb_o, opp, opp_o], jax.ShapeDtypeStruct((tokens, cols), jnp.float32), "to_opposite"
    )


def teachers(places, h, t_near, stale_opp, stale_opp_o, stale_far, stale_far_o, came_a, came_b):
    tokens, (rows, cols) = h.shape[0], stale_opp.shape
    fit = rows // tokens
    width = h.shape[1] // 2

    def body(s, h_ref, near, w, wo, v, vo, ca, cb, mine, sent, held):
        @pl.when(s[END] == 1)
        def _():
            mine[...] = near[...].astype(mine.dtype)
            sent[...] = jnp.zeros(sent.shape, sent.dtype)

        @pl.when(s[END] == 0)
        def _():
            for k in range(width // cols):
                source, j = (ca, k) if k < fit else (cb, k - fit)
                held[:, k * cols:(k + 1) * cols] = source[j * tokens:(j + 1) * tokens, :]

            def away(place):
                return columns(held, s[place] * rows - s[HALF] * width, rows)

            end = dot(away(OPP), w[...]) + dot(away(OPP_O), wo[...])
            both = jnp.concatenate([columns(h_ref, s[FAR] * rows, rows), away(FAR)], axis=0)
            both_o = jnp.concatenate([columns(h_ref, s[FAR_O] * rows, rows), away(FAR_O)], axis=0)
            far = dot(both, v[...]) + dot(both_o, vo[...])
            mine[...] = (near[...] + far[:tokens]).astype(mine.dtype)
            sent[...] = (end + far[tokens:]).astype(sent.dtype)

    operands = [h, t_near, stale_opp, stale_opp_o, stale_far, stale_far_o, came_a, came_b]
    out = jax.ShapeDtypeStruct((tokens, cols), jnp.bfloat16)

    def with_scratch(*refs):
        pl.run_scoped(lambda held: body(*refs, held), pltpu.VMEM((tokens, width), h.dtype))

    return call(with_scratch, places, operands, [out, out], "teachers")


def difference(places, student, target_1, target_2, match):
    tokens = student.shape[0]

    def body(s, student_ref, one, two, match_ref, out):
        teacher = (one[...].astype(jnp.float32) + two[...].astype(jnp.float32)).astype(jnp.bfloat16)
        rows = lax.broadcasted_iota(jnp.int32, (tokens, tokens), 0)
        pick = (match_ref[...] == rows).astype(jnp.bfloat16)
        target = lax.dot_general(
            pick, teacher, (((0,), (0,)), ((), ())), preferred_element_type=jnp.float32
        )
        out[...] = (student_ref[...] - target).astype(out.dtype)

    operands = [student, target_1, target_2, match]
    return call(body, places, operands, jax.ShapeDtypeStruct(student.shape, jnp.bfloat16), "difference")


def gradient(places, left, choices, total=None):
    tokens = left.shape[0]
    rows, cols = choices[0][0].shape
    pieces = []
    for choice in choices:
        pieces += [p for p in choice if not any(p is q for q in pieces)]
    where = [[next(j for j, q in enumerate(pieces) if q is p) for p in choice] for choice in choices]
    dtype = jnp.float32 if total is None else left.dtype

    def body(s, left_ref, *refs):
        out = refs[-1]

        def run(choice):
            for k in range(4):
                start = pl.multiple_of(s[PIECE + k] * rows, 128)
                value = dot_t(left_ref[...], refs[where[choice][k]][...])
                if total is not None:
                    value = value + refs[len(pieces)][:, pl.ds(start, rows)]
                out[:, pl.ds(start, rows)] = value.astype(out.dtype)

        if where[0] == where[1]:
            pl.when(s[NEAR] == 0)(lambda: run(0))
        else:
            pl.when((s[NEAR] == 0) & (s[END] == 0))(lambda: run(0))
            pl.when((s[NEAR] == 0) & (s[END] == 1))(lambda: run(1))
        pl.when(s[NEAR] == 1)(lambda: run(2))

    operands = [left, *pieces] + ([] if total is None else [total])
    return call(body, places, operands, jax.ShapeDtypeStruct((tokens, 4 * rows), dtype), "gradient")


def general(hidden, live_weight, stale_weight, match):
    hidden_rows = hidden[0]
    live_full = lax.all_gather(live_weight[0], "fsdp", axis=0, tiled=True)
    student = dot(hidden_rows, live_full)
    stale_full = lax.all_gather(stale_weight[0], "fsdp", axis=0, tiled=True)
    teacher = dot(hidden_rows, stale_full).astype(jnp.bfloat16)
    teacher = partner(teacher, "mp", 0)
    target = jnp.take(teacher, match[0], axis=0)
    mismatch = (student - target.astype(jnp.float32)).astype(jnp.bfloat16)
    partial_value = dot_t(mismatch, live_full).astype(jnp.bfloat16)
    summed = lax.psum_scatter(partial_value, "tp", scatter_dimension=1, tiled=True)
    return summed[None]


def line_of_four(hidden, live_weight, stale_weight, match):
    h, live, stale = hidden[0], live_weight[0], stale_weight[0]
    fit = live.shape[0] // h.shape[0]
    place = 2 * lax.axis_index("fsdp") + lax.axis_index("tp")
    places = lax.dynamic_index_in_dim(jnp.asarray(table()), place, 0, keepdims=False)

    live_mid = along_z(live, MID)
    live_nb = along_z(live, PAIR)
    stale_opp = along_z(stale, MID)
    stale_nb = along_z(stale, PAIR)
    x_1 = over_x(live, False)
    live_o = across_cores(live)
    stale_o = across_cores(stale)
    student = contrib(places, h, OWN, OWN_O, live, live_o)
    t_near = contrib(places, h, OWN, OWN_O, stale, stale_o)

    mid_2, nb_2, s_opp, s_nb = after(
        (live_mid, live_nb, stale_opp, stale_nb), tick(places, stale_nb), student, t_near
    )
    live_far_mid = along_z(nb_2, MID)
    came_a = along_z(as_rows(places, h, live.shape, 0, mid_2), PAIR)
    nb_x, mid_x, own_x, s_opp, s_nb = after((nb_2, mid_2, x_1, s_opp, s_nb), live_o, stale_o)
    x_2 = over_x(choose(places, NEAR, mid_x, nb_x), True)
    live_nb_o = across_cores(nb_x)
    stale_nb_o = across_cores(s_nb)
    stale_opp_o = across_cores(s_opp)
    x_1_o = across_cores(own_x)
    student = contrib(places, h, NB, NB_O, nb_x, live_nb_o, student)
    t_near = to_opposite(places, h, t_near, s_nb, stale_nb_o, s_opp, stale_opp_o)

    far_3, came_3, nb_3 = after((live_far_mid, came_a, stale_nb), tick(places, came_a), student, t_near)
    stale_far = along_z(nb_3, MID)
    came_b = along_z(as_rows(places, h, live.shape, fit, far_3), PAIR)
    came_x, far_x, x_2 = after((came_3, far_3, x_2), x_1_o, student, t_near)
    x_3 = over_x(choose(places, END, came_x, far_x), None)

    stale_far, came_4 = after((stale_far, came_b), tick(places, came_b))
    stale_far_o = across_cores(stale_far)
    x_4 = over_x(came_4, END)
    (t_near,) = after((t_near,), x_3)
    t_mine, t_end = teachers(
        places, h, t_near, stale_opp, stale_opp_o, stale_far, stale_far_o, came_3, came_4
    )
    came_t, mid_t, far_t, came_t4, x_2t, x_3t = after((came_3, live_mid, far_3, came_4, x_2, x_3), t_mine)
    live_opp = choose(places, END, came_t, mid_t)
    live_far = choose(places, END, came_t4, far_t)
    live_opp_o = across_cores(live_opp)
    live_far_o = across_cores(live_far)
    x_2_o = across_cores(x_2t)
    x_3_o = across_cores(x_3t)
    student = contrib(places, h, OPP, OPP_O, live_opp, live_opp_o, student)
    student = contrib(places, h, FAR, FAR_O, live_far, live_far_o, student)

    target_1 = partner(t_mine, "mp", 0)
    route = []
    for m in range(2):
        for a, b in OUT:
            for core in range(2):
                route.append((8 * m + 2 * a + core, 8 * (1 - m) + 2 * b + core))
    target_2 = lax.ppermute(t_end, ("mp", "fsdp"), route)
    mismatch = difference(places, student, target_1, target_2, match)
    mismatch_o = partner(mismatch, "tp", 0)
    (x_4,) = after((x_4,), mismatch)
    x_4_o = across_cores(x_4)
    own = gradient(
        places, mismatch,
        ((live_opp, live_opp_o, live_far, live_far_o),) * 2 + ((live, live_o, live_nb, live_nb_o),),
    )
    grad = gradient(
        places, mismatch_o,
        ((x_2, x_2_o, x_3, x_3_o), (x_3, x_3_o, x_4, x_4_o), (x_1, x_1_o, x_2, x_2_o)), own,
    )
    return grad[None]


def solution(mesh):
    in_specs = (
        P("mp", "fsdp", None),
        P("mp", "fsdp", "tp"),
        P("mp", "fsdp", "tp"),
        P("mp", "fsdp"),
    )
    out_specs = P("mp", "fsdp", "tp")
    line = mesh.shape["fsdp"] == 8 and mesh.shape["tp"] == 2 and mesh.shape["mp"] == 2
    body = line_of_four if line else general
    return jax.shard_map(body, mesh=mesh, in_specs=in_specs, out_specs=out_specs, check_vma=False)
```

time: 130 us -> 109 us (0.84)
  Pallas kernels: 44.8 us -> 15.2 us
  starting transfers between devices: 27.9 us -> 37.2 us
  local copies, waits for them, and re-layouts: 6.72 us -> 4.38 us
  waiting for transfers between devices: 49.4 us -> 51 us
    pallas_call x13 -> x16, Pallas kernels: 44.8 us -> 15.2 us  [call(): pl.pallas_call(body, out_shape=shapes, in_specs=[pl.BlockSpec(memory_spac...]
    ppermute x8, waiting for transfers between devices: 29.6 us -> 36.1 us  [along_z(): return lax.ppermute(block, 'fsdp', route)]
    ppermute x4, starting transfers between devices: 5.52 us -> 10.4 us  [over_x(): return lax.ppermute(block, ('fsdp', 'tp'), route)]
    ppermute x14, starting transfers between devices: 3.24 us -> 6.67 us  [partner(): return lax.ppermute(block, axis, route)]
    ppermute x4, waiting for transfers between devices: 8.37 us -> 6.31 us  [over_x(): return lax.ppermute(block, ('fsdp', 'tp'), route)]
    unnamed x40 -> x16, local copies, waits for them, and re-layouts: 5.44 us -> 3.68 us
    ppermute x1, waiting for transfers between devices: 4.72 us -> 3.3 us  [line_of_four(): target_2 = lax.ppermute(t_end, ('mp', 'fsdp'), route)]
    ppermute x14, waiting for transfers between devices: 6.75 us -> 5.34 us  [partner(): return lax.ppermute(block, axis, route)]
  transfers between devices with their start and end apart: 27 -> 27, of which waited for: 8 -> 9; matrix products, arithmetic and copies ran while one was open for 1% -> 1% of each run, Pallas kernels for 27% -> 10%
where the time goes in v3:
time: 109 us; the launch traced here: 108 us
  waiting for transfers between devices  51 us (47%)
  starting transfers between devices  37.2 us (34%)
  Pallas kernels  15.2 us (14%)
  local copies, waits for them, and re-layouts  4.38 us (4%)
    ppermute x8, waiting for transfers between devices, along_z(): return lax.ppermute(block, 'fsdp', route)  36.1 us
    ppermute x8, starting transfers between devices, along_z(): return lax.ppermute(block, 'fsdp', route)  18.8 us
    pallas_call x16, Pallas kernels, call(): pl.pallas_call(body, out_shape=shapes, in_specs=[pl.BlockSpec(memory_spac...  15.2 us
    ppermute x4, starting transfers between devices, over_x(): return lax.ppermute(block, ('fsdp', 'tp'), route)  10.4 us
    ppermute x14, starting transfers between devices, partner(): return lax.ppermute(block, axis, route)  6.67 us
    ppermute x4, waiting for transfers between devices, over_x(): return lax.ppermute(block, ('fsdp', 'tp'), route)  6.31 us
    ppermute x14, waiting for transfers between devices, partner(): return lax.ppermute(block, axis, route)  5.34 us
    unnamed x16, local copies, waits for them, and re-layouts  3.68 us
  transfers between devices with their start and end apart: 27, of which 9 were waited for; matrix products, arithmetic and copies ran while one was open for 1% of the time, Pallas kernels for 10%

profile of v3, /device:TPU:0, one launch (start us, length us, event | category | flops | bytes accessed | tf_op | source)
XLA Modules:
  0.0 108.1 jit_solution(10869075900862604507)
XLA Ops:
  0.5 3.0 %collective-permute-start.1 = (bf16[640,512]{1,0:T(8,128)(2,1)}, bf16[640,512]{1,0:T(8,128)(2,1)S(1)}, u32[]{:S(2)}, u32[]{:S(2)}) collective-permute-start(bf16[640,512]{1,0:T(8,128)(2,1)} %bitcast.16), channel_id=1, source_target_pairs={{0,4},{2,6},{4,0},{6,2},{8,12},{10,14},{12,8},{14,10},{1,5},{3,7},... | collective-permute-start | bytes 1966088 | tf_op jit(solution)/shard_map/ppermute | solution.py:47
  4.2 4.4 %collective-permute-start.3 = (bf16[640,512]{1,0:T(8,128)(2,1)}, bf16[640,512]{1,0:T(8,128)(2,1)S(1)}, u32[]{:S(2)}, u32[]{:S(2)}) collective-permute-start(bf16[640,512]{1,0:T(8,128)(2,1)} %bitcast.22), channel_id=1, source_target_pairs={{0,4},{2,6},{4,0},{6,2},{8,12},{10,14},{12,8},{14,10},{1,5},{3,7},... | collective-permute-start | bytes 1966088 | tf_op jit(solution)/shard_map/ppermute | solution.py:47
  10.2 1.3 %collective-permute-start.8 = (bf16[640,512]{1,0:T(8,128)(2,1)}, bf16[640,512]{1,0:T(8,128)(2,1)}, u32[]{:S(2)}, u32[]{:S(2)}) collective-permute-start(bf16[640,512]{1,0:T(8,128)(2,1)} %bitcast.18), channel_id=1, source_target_pairs={{1,0},{3,2},{5,4},{7,6},{8,9},{10,11},{12,13},{14,15},{17,16},{19,... | collective-permute-start | bytes 1966088 | tf_op jit(solution)/shard_map/ppermute | solution.py:62
  12.2 1.4 %copy-done = bf16[1,160,5120]{2,1,0:T(8,128)(2,1)S(1)} copy-done((bf16[1,160,5120]{2,1,0:T(8,128)(2,1)S(1)}, bf16[1,160,5120]{2,1,0:T(8,128)(2,1)}, u32[]{:S(2)}) %copy-start) | copy-done | bytes 1638424
  13.6 1.1 %copy-done.2 = bf16[1,640,512]{2,1,0:T(8,128)(2,1)S(1)} copy-done((bf16[1,640,512]{2,1,0:T(8,128)(2,1)S(1)}, bf16[1,640,512]{2,1,0:T(8,128)(2,1)}, u32[]{:S(2)}) %copy-start.2) | copy-done | bytes 655384
  17.0 2.3 %collective-permute-done.1.w.no_ref.refs_6_ = bf16[640,512]{1,0:T(8,128)(2,1)S(1)} collective-permute-done((bf16[640,512]{1,0:T(8,128)(2,1)}, bf16[640,512]{1,0:T(8,128)(2,1)S(1)}, u32[]{:S(2)}, u32[]{:S(2)}) %collective-permute-start.1) | collective-permute-done | bytes 655392 | tf_op jit(solution)/shard_map/ppermute | solution.py:47
  19.3 13.4 %collective-permute-done.3.n = bf16[640,512]{1,0:T(8,128)(2,1)S(1)} collective-permute-done((bf16[640,512]{1,0:T(8,128)(2,1)}, bf16[640,512]{1,0:T(8,128)(2,1)S(1)}, u32[]{:S(2)}, u32[]{:S(2)}) %collective-permute-start.3) | collective-permute-done | bytes 655392 | tf_op jit(solution)/shard_map/ppermute | solution.py:47
  33.9 4.8 %collective-permute-start.7 = (bf16[640,512]{1,0:T(8,128)(2,1)S(1)}, bf16[640,512]{1,0:T(8,128)(2,1)S(1)}, u32[]{:S(2)}, u32[]{:S(2)}) collective-permute-start(bf16[640,512]{1,0:T(8,128)(2,1)S(1)} %as_rows.2), channel_id=1, source_target_pairs={{0,4},{2,6},{4,0},{6,2},{8,12},{10,14},{12,8},{14,10},{1,5},{3,7},... | collective-permute-start | bytes 1966088 | tf_op jit(solution)/shard_map/ppermute | solution.py:47
  40.0 1.3 %collective-permute-start.14 = (bf16[640,512]{1,0:T(8,128)(2,1)S(1)}, bf16[640,512]{1,0:T(8,128)(2,1)S(1)}, u32[]{:S(2)}, u32[]{:S(2)}) collective-permute-start(bf16[640,512]{1,0:T(8,128)(2,1)S(1)} %choose.4), channel_id=1, source_target_pairs={{1,0},{3,2},{5,4},{4,5},{7,6},{6,7},{8,9},{9,8},{10,11},{11,10},{1... | collective-permute-start | bytes 1966088 | tf_op jit(solution)/shard_map/ppermute | solution.py:62
  43.5 10.5 %collective-permute-done.7.yes_ref.refs_7_ = bf16[640,512]{1,0:T(8,128)(2,1)S(1)} collective-permute-done((bf16[640,512]{1,0:T(8,128)(2,1)S(1)}, bf16[640,512]{1,0:T(8,128)(2,1)S(1)}, u32[]{:S(2)}, u32[]{:S(2)}) %collective-permute-start.7) | collective-permute-done | bytes 655392 | tf_op jit(solution)/shard_map/ppermute | solution.py:47
  54.7 3.8 %collective-permute-start.13 = (bf16[640,512]{1,0:T(8,128)(2,1)S(1)}, bf16[640,512]{1,0:T(8,128)(2,1)S(1)}, u32[]{:S(2)}, u32[]{:S(2)}) collective-permute-start(bf16[640,512]{1,0:T(8,128)(2,1)S(1)} %as_rows.3), channel_id=1, source_target_pairs={{0,4},{2,6},{4,0},{6,2},{8,12},{10,14},{12,8},{14,10},{1,5},{3,7},... | collective-permute-start | bytes 1966088 | tf_op jit(solution)/shard_map/ppermute | solution.py:47
  59.8 3.4 %collective-permute-start.16 = (bf16[640,512]{1,0:T(8,128)(2,1)S(1)}, bf16[640,512]{1,0:T(8,128)(2,1)S(1)}, u32[]{:S(2)}, u32[]{:S(2)}) collective-permute-start(bf16[640,512]{1,0:T(8,128)(2,1)S(1)} %choose.5), channel_id=1, source_target_pairs={{0,1},{2,3},{4,5},{6,7},{9,8},{11,10},{13,12},{15,14},{16,17},{18,... | collective-permute-start | bytes 1966088 | tf_op jit(solution)/shard_map/ppermute | solution.py:62
  63.3 9.9 %collective-permute-done.13.refs_8_.yes_ref = bf16[640,512]{1,0:T(8,128)(2,1)S(1)} collective-permute-done((bf16[640,512]{1,0:T(8,128)(2,1)S(1)}, bf16[640,512]{1,0:T(8,128)(2,1)S(1)}, u32[]{:S(2)}, u32[]{:S(2)}) %collective-permute-start.13) | collective-permute-done | bytes 655392 | tf_op jit(solution)/shard_map/ppermute | solution.py:47
  73.1 3.7 %collective-permute-done.16.refs_2_ = bf16[640,512]{1,0:T(8,128)(2,1)S(1)} collective-permute-done((bf16[640,512]{1,0:T(8,128)(2,1)S(1)}, bf16[640,512]{1,0:T(8,128)(2,1)S(1)}, u32[]{:S(2)}, u32[]{:S(2)}) %collective-permute-start.16) | collective-permute-done | bytes 655392 | tf_op jit(solution)/shard_map/ppermute | solution.py:62
  79.2 4.4 %collective-permute-start.25 = (bf16[640,512]{1,0:T(8,128)(2,1)S(1)}, bf16[640,512]{1,0:T(8,128)(2,1)S(1)}, u32[]{:S(2)}, u32[]{:S(2)}) collective-permute-start(bf16[640,512]{1,0:T(8,128)(2,1)S(1)} %collective-permute-done.13.refs_8_.yes_ref), channel_id=1, source_target_pairs={{0,1},{2,3},{13,12},{15,14},{16,17},{18,19},{29,28},{31,30}} | collective-permute-start | bytes 1966088 | tf_op jit(solution)/shard_map/ppermute | solution.py:62
  83.7 1.3 %collective-permute-start.21 = (bf16[160,512]{1,0:T(8,128)(2,1)S(1)}, bf16[160,512]{1,0:T(8,128)(2,1)S(1)}, u32[]{:S(2)}, u32[]{:S(2)}) collective-permute-start(bf16[160,512]{1,0:T(8,128)(2,1)S(1)} %get-tuple-element.55), channel_id=1, source_target_pairs={{4,16},{6,18},{8,28},{10,30},{20,0},{22,2},{24,12},{26,14},{5,17},... | collective-permute-start | bytes 491528 | tf_op jit(solution)/shard_map/ppermute | solution.py:331
  85.0 1.6 %collective-permute-start.20 = (bf16[160,512]{1,0:T(8,128)(2,1)S(1)}, bf16[160,512]{1,0:T(8,128)(2,1)S(1)}, u32[]{:S(2)}, u32[]{:S(2)}) collective-permute-start(bf16[160,512]{1,0:T(8,128)(2,1)S(1)} %get-tuple-element.50), channel_id=1, source_target_pairs={{0,16},{16,0},{1,17},{17,1},{2,18},{18,2},{3,19},{19,3},{4,20},{20... | collective-permute-start | bytes 491528 | tf_op jit(solution)/shard_map/ppermute | solution.py:42
  89.1 3.3 %collective-permute-done.21.two = bf16[160,512]{1,0:T(8,128)(2,1)S(1)} collective-permute-done((bf16[160,512]{1,0:T(8,128)(2,1)S(1)}, bf16[160,512]{1,0:T(8,128)(2,1)S(1)}, u32[]{:S(2)}, u32[]{:S(2)}) %collective-permute-start.21) | collective-permute-done | bytes 163872 | tf_op jit(solution)/shard_map/ppermute | solution.py:331
  92.4 2.0 %collective-permute-done.20.one = bf16[160,512]{1,0:T(8,128)(2,1)S(1)} collective-permute-done((bf16[160,512]{1,0:T(8,128)(2,1)S(1)}, bf16[160,512]{1,0:T(8,128)(2,1)S(1)}, u32[]{:S(2)}, u32[]{:S(2)}) %collective-permute-start.20) | collective-permute-done | bytes 163872 | tf_op jit(solution)/shard_map/ppermute | solution.py:42
  95.2 2.6 %collective-permute-done.25.refs_4_ = bf16[640,512]{1,0:T(8,128)(2,1)S(1)} collective-permute-done((bf16[640,512]{1,0:T(8,128)(2,1)S(1)}, bf16[640,512]{1,0:T(8,128)(2,1)S(1)}, u32[]{:S(2)}, u32[]{:S(2)}) %collective-permute-start.25) | collective-permute-done | bytes 655392 | tf_op jit(solution)/shard_map/ppermute | solution.py:62
  97.8 2.5 %collective-permute-start.22 = (bf16[160,512]{1,0:T(8,128)(2,1)S(1)}, bf16[160,512]{1,0:T(8,128)(2,1)S(1)}, u32[]{:S(2)}, u32[]{:S(2)}) collective-permute-start(bf16[160,512]{1,0:T(8,128)(2,1)S(1)} %difference.1.left_ref), channel_id=1, source_target_pairs={{0,1},{1,0},{2,3},{3,2},{4,5},{5,4},{6,7},{7,6},{8,9},{9,8},{10,11... | collective-permute-start | bytes 491528 | tf_op jit(solution)/shard_map/ppermute | solution.py:42
  100.3 1.5 %gradient.2.refs_8_ = f32[160,2560]{1,0:T(8,128)S(1)} custom-call(s32[15]{0:T(128)S(1)} %dynamic-slice_bitcast_fusion.s.refs_0_, bf16[160,512]{1,0:T(8,128)(2,1)S(1)} %difference.1.left_ref, bf16[640,512]{1,0:T(8,128)(2,1)S(1)} %choose.7.w.refs_0_, bf16[640,512]{1,0:T(8,128)(2,1)S(1)} %collective-permute-done.19.wo.refs_1_, ...), custom_call_target="tpu_custom_call" | custom-call | flops 1 | bytes 1 | tf_op jit(solution)/shard_map/gradient/pallas_call | solution.py:81
  101.8 3.3 %collective-permute-done.22.left_ref = bf16[160,512]{1,0:T(8,128)(2,1)S(1)} collective-permute-done((bf16[160,512]{1,0:T(8,128)(2,1)S(1)}, bf16[160,512]{1,0:T(8,128)(2,1)S(1)}, u32[]{:S(2)}, u32[]{:S(2)}) %collective-permute-start.22) | collective-permute-done | bytes 163872 | tf_op jit(solution)/shard_map/ppermute | solution.py:42
  105.2 3.0 %gradient.3 = bf16[160,2560]{1,0:T(8,128)(2,1)} custom-call(s32[15]{0:T(128)S(1)} %dynamic-slice_bitcast_fusion.s.refs_0_, bf16[160,512]{1,0:T(8,128)(2,1)S(1)} %collective-permute-done.22.left_ref, bf16[640,512]{1,0:T(8,128)(2,1)S(1)} %collective-permute-done.14.refs_0_, bf16[640,512]{1,0:T(8,128)(2,1)S(1)} %collective-permute-done.23.refs_1_, ...), custom_call_target="tpu_custom_call" | custom-call | flops 1 | bytes 1 | tf_op jit(solution)/shard_map/gradient/pallas_call | solution.py:81
  (63 shorter events, 18.0 us)
Async XLA Ops:
  0.0 8.7 %collective-permute-start.4 = (bf16[640,512]{1,0:T(8,128)(2,1)}, bf16[640,512]{1,0:T(8,128)(2,1)S(1)}, u32[]{:S(2)}, u32[]{:S(2)}) collective-permute-start(bf16[640,512]{1,0:T(8,128)(2,1)} %bitcast.15), channel_id=1, source_target_pairs={{0,2},{2,0},{4,6},{6,4},{8,10},{10,8},{12,14},{14,12},{1,3},{3,1},... | collective-permute-start | bytes 1966088 | tf_op jit(solution)/shard_map/ppermute | solution.py:42
  0.5 8.9 %collective-permute-start.5 = (bf16[640,512]{1,0:T(8,128)(2,1)}, bf16[640,512]{1,0:T(8,128)(2,1)S(1)}, u32[]{:S(2)}, u32[]{:S(2)}) collective-permute-start(bf16[640,512]{1,0:T(8,128)(2,1)} %bitcast.21), channel_id=1, source_target_pairs={{0,2},{2,0},{4,6},{6,4},{8,10},{10,8},{12,14},{14,12},{1,3},{3,1},... | collective-permute-start | bytes 1966088 | tf_op jit(solution)/shard_map/ppermute | solution.py:42
  0.5 18.8 %collective-permute-start.1 = (bf16[640,512]{1,0:T(8,128)(2,1)}, bf16[640,512]{1,0:T(8,128)(2,1)S(1)}, u32[]{:S(2)}, u32[]{:S(2)}) collective-permute-start(bf16[640,512]{1,0:T(8,128)(2,1)} %bitcast.16), channel_id=1, source_target_pairs={{0,4},{2,6},{4,0},{6,2},{8,12},{10,14},{12,8},{14,10},{1,5},{3,7},... | collective-permute-start | bytes 1966088 | tf_op jit(solution)/shard_map/ppermute | solution.py:47
  3.5 15.8 %collective-permute-start = (bf16[640,512]{1,0:T(8,128)(2,1)}, bf16[640,512]{1,0:T(8,128)(2,1)S(1)}, u32[]{:S(2)}, u32[]{:S(2)}) collective-permute-start(bf16[640,512]{1,0:T(8,128)(2,1)} %bitcast.17), channel_id=1, source_target_pairs={{4,8},{6,10},{8,4},{10,6},{5,9},{7,11},{9,5},{11,7},{20,24},{22,26... | collective-permute-start | bytes 1966088 | tf_op jit(solution)/shard_map/ppermute | solution.py:47
  4.2 28.5 %collective-permute-start.3 = (bf16[640,512]{1,0:T(8,128)(2,1)}, bf16[640,512]{1,0:T(8,128)(2,1)S(1)}, u32[]{:S(2)}, u32[]{:S(2)}) collective-permute-start(bf16[640,512]{1,0:T(8,128)(2,1)} %bitcast.22), channel_id=1, source_target_pairs={{0,4},{2,6},{4,0},{6,2},{8,12},{10,14},{12,8},{14,10},{1,5},{3,7},... | collective-permute-start | bytes 1966088 | tf_op jit(solution)/shard_map/ppermute | solution.py:47
  8.7 24.0 %collective-permute-start.2 = (bf16[640,512]{1,0:T(8,128)(2,1)}, bf16[640,512]{1,0:T(8,128)(2,1)S(1)}, u32[]{:S(2)}, u32[]{:S(2)}) collective-permute-start(bf16[640,512]{1,0:T(8,128)(2,1)} %bitcast.23), channel_id=1, source_target_pairs={{4,8},{6,10},{8,4},{10,6},{5,9},{7,11},{9,5},{11,7},{20,24},{22,26... | collective-permute-start | bytes 1966088 | tf_op jit(solution)/shard_map/ppermute | solution.py:47
  10.2 22.5 %collective-permute-start.8 = (bf16[640,512]{1,0:T(8,128)(2,1)}, bf16[640,512]{1,0:T(8,128)(2,1)}, u32[]{:S(2)}, u32[]{:S(2)}) collective-permute-start(bf16[640,512]{1,0:T(8,128)(2,1)} %bitcast.18), channel_id=1, source_target_pairs={{1,0},{3,2},{5,4},{7,6},{8,9},{10,11},{12,13},{14,15},{17,16},{19,... | collective-permute-start | bytes 1966088 | tf_op jit(solution)/shard_map/ppermute | solution.py:62
  32.7 9.6 %collective-permute-start.10 = (bf16[640,512]{1,0:T(8,128)(2,1)S(1)}, bf16[640,512]{1,0:T(8,128)(2,1)S(1)}, u32[]{:S(2)}, u32[]{:S(2)}) collective-permute-start(bf16[640,512]{1,0:T(8,128)(2,1)S(1)} %collective-permute-done.3.n), channel_id=1, source_target_pairs={{0,2},{2,0},{4,6},{6,4},{8,10},{10,8},{12,14},{14,12},{1,3},{3,1},... | collective-permute-start | bytes 1966088 | tf_op jit(solution)/shard_map/ppermute | solution.py:42
  33.2 9.4 %collective-permute-start.11 = (bf16[640,512]{1,0:T(8,128)(2,1)S(1)}, bf16[640,512]{1,0:T(8,128)(2,1)S(1)}, u32[]{:S(2)}, u32[]{:S(2)}) collective-permute-start(bf16[640,512]{1,0:T(8,128)(2,1)S(1)} %collective-permute-done.2.p.refs_3_), channel_id=1, source_target_pairs={{0,2},{2,0},{4,6},{6,4},{8,10},{10,8},{12,14},{14,12},{1,3},{3,1},... | collective-permute-start | bytes 1966088 | tf_op jit(solution)/shard_map/ppermute | solution.py:42
  33.9 20.2 %collective-permute-start.7 = (bf16[640,512]{1,0:T(8,128)(2,1)S(1)}, bf16[640,512]{1,0:T(8,128)(2,1)S(1)}, u32[]{:S(2)}, u32[]{:S(2)}) collective-permute-start(bf16[640,512]{1,0:T(8,128)(2,1)S(1)} %as_rows.2), channel_id=1, source_target_pairs={{0,4},{2,6},{4,0},{6,2},{8,12},{10,14},{12,8},{14,10},{1,5},{3,7},... | collective-permute-start | bytes 1966088 | tf_op jit(solution)/shard_map/ppermute | solution.py:47
  38.7 15.4 %collective-permute-start.6 = (bf16[640,512]{1,0:T(8,128)(2,1)S(1)}, bf16[640,512]{1,0:T(8,128)(2,1)S(1)}, u32[]{:S(2)}, u32[]{:S(2)}) collective-permute-start(bf16[640,512]{1,0:T(8,128)(2,1)S(1)} %collective-permute-done.1.w.no_ref.refs_6_), channel_id=1, source_target_pairs={{4,8},{6,10},{8,4},{10,6},{5,9},{7,11},{9,5},{11,7},{20,24},{22,26... | collective-permute-start | bytes 1966088 | tf_op jit(solution)/shard_map/ppermute | solution.py:47
  40.0 19.2 %collective-permute-start.14 = (bf16[640,512]{1,0:T(8,128)(2,1)S(1)}, bf16[640,512]{1,0:T(8,128)(2,1)S(1)}, u32[]{:S(2)}, u32[]{:S(2)}) collective-permute-start(bf16[640,512]{1,0:T(8,128)(2,1)S(1)} %choose.4), channel_id=1, source_target_pairs={{1,0},{3,2},{5,4},{4,5},{7,6},{6,7},{8,9},{9,8},{10,11},{11,10},{1... | collective-permute-start | bytes 1966088 | tf_op jit(solution)/shard_map/ppermute | solution.py:62
  42.3 17.0 %collective-permute-start.15 = (bf16[640,512]{1,0:T(8,128)(2,1)}, bf16[640,512]{1,0:T(8,128)(2,1)S(1)}, u32[]{:S(2)}, u32[]{:S(2)}) collective-permute-start(bf16[640,512]{1,0:T(8,128)(2,1)} %collective-permute-done.8.refs_6_), channel_id=1, source_target_pairs={{0,2},{2,0},{4,6},{6,4},{8,10},{10,8},{12,14},{14,12},{1,3},{3,1},... | collective-permute-start | bytes 1966088 | tf_op jit(solution)/shard_map/ppermute | solution.py:42
  54.7 18.5 %collective-permute-start.13 = (bf16[640,512]{1,0:T(8,128)(2,1)S(1)}, bf16[640,512]{1,0:T(8,128)(2,1)S(1)}, u32[]{:S(2)}, u32[]{:S(2)}) collective-permute-start(bf16[640,512]{1,0:T(8,128)(2,1)S(1)} %as_rows.3), channel_id=1, source_target_pairs={{0,4},{2,6},{4,0},{6,2},{8,12},{10,14},{12,8},{14,10},{1,5},{3,7},... | collective-permute-start | bytes 1966088 | tf_op jit(solution)/shard_map/ppermute | solution.py:47
  58.5 14.6 %collective-permute-start.12 = (bf16[640,512]{1,0:T(8,128)(2,1)S(1)}, bf16[640,512]{1,0:T(8,128)(2,1)S(1)}, u32[]{:S(2)}, u32[]{:S(2)}) collective-permute-start(bf16[640,512]{1,0:T(8,128)(2,1)S(1)} %collective-permute-done.3.n), channel_id=1, source_target_pairs={{4,8},{6,10},{8,4},{10,6},{5,9},{7,11},{9,5},{11,7},{20,24},{22,26... | collective-permute-start | bytes 1966088 | tf_op jit(solution)/shard_map/ppermute | solution.py:47
  59.8 17.0 %collective-permute-start.16 = (bf16[640,512]{1,0:T(8,128)(2,1)S(1)}, bf16[640,512]{1,0:T(8,128)(2,1)S(1)}, u32[]{:S(2)}, u32[]{:S(2)}) collective-permute-start(bf16[640,512]{1,0:T(8,128)(2,1)S(1)} %choose.5), channel_id=1, source_target_pairs={{0,1},{2,3},{4,5},{6,7},{9,8},{11,10},{13,12},{15,14},{16,17},{18,... | collective-permute-start | bytes 1966088 | tf_op jit(solution)/shard_map/ppermute | solution.py:62
  78.0 8.6 %collective-permute-start.19 = (bf16[640,512]{1,0:T(8,128)(2,1)S(1)}, bf16[640,512]{1,0:T(8,128)(2,1)S(1)}, u32[]{:S(2)}, u32[]{:S(2)}) collective-permute-start(bf16[640,512]{1,0:T(8,128)(2,1)S(1)} %choose.7.w.refs_0_), channel_id=1, source_target_pairs={{0,2},{2,0},{4,6},{6,4},{8,10},{10,8},{12,14},{14,12},{1,3},{3,1},... | collective-permute-start | bytes 1966088 | tf_op jit(solution)/shard_map/ppermute | solution.py:42
  78.7 8.9 %collective-permute-start.18 = (bf16[640,512]{1,0:T(8,128)(2,1)S(1)}, bf16[640,512]{1,0:T(8,128)(2,1)S(1)}, u32[]{:S(2)}, u32[]{:S(2)}) collective-permute-start(bf16[640,512]{1,0:T(8,128)(2,1)S(1)} %choose.6.w.refs_2_), channel_id=1, source_target_pairs={{0,2},{2,0},{4,6},{6,4},{8,10},{10,8},{12,14},{14,12},{1,3},{3,1},... | collective-permute-start | bytes 1966088 | tf_op jit(solution)/shard_map/ppermute | solution.py:42
  79.2 18.5 %collective-permute-start.25 = (bf16[640,512]{1,0:T(8,128)(2,1)S(1)}, bf16[640,512]{1,0:T(8,128)(2,1)S(1)}, u32[]{:S(2)}, u32[]{:S(2)}) collective-permute-start(bf16[640,512]{1,0:T(8,128)(2,1)S(1)} %collective-permute-done.13.refs_8_.yes_ref), channel_id=1, source_target_pairs={{0,1},{2,3},{13,12},{15,14},{16,17},{18,19},{29,28},{31,30}} | collective-permute-start | bytes 1966088 | tf_op jit(solution)/shard_map/ppermute | solution.py:62
  83.7 8.8 %collective-permute-start.21 = (bf16[160,512]{1,0:T(8,128)(2,1)S(1)}, bf16[160,512]{1,0:T(8,128)(2,1)S(1)}, u32[]{:S(2)}, u32[]{:S(2)}) collective-permute-start(bf16[160,512]{1,0:T(8,128)(2,1)S(1)} %get-tuple-element.55), channel_id=1, source_target_pairs={{4,16},{6,18},{8,28},{10,30},{20,0},{22,2},{24,12},{26,14},{5,17},... | collective-permute-start | bytes 491528 | tf_op jit(solution)/shard_map/ppermute | solution.py:331
  85.0 9.4 %collective-permute-start.20 = (bf16[160,512]{1,0:T(8,128)(2,1)S(1)}, bf16[160,512]{1,0:T(8,128)(2,1)S(1)}, u32[]{:S(2)}, u32[]{:S(2)}) collective-permute-start(bf16[160,512]{1,0:T(8,128)(2,1)S(1)} %get-tuple-element.50), channel_id=1, source_target_pairs={{0,16},{16,0},{1,17},{17,1},{2,18},{18,2},{3,19},{19,3},{4,20},{20... | collective-permute-start | bytes 491528 | tf_op jit(solution)/shard_map/ppermute | solution.py:42
  86.6 15.2 %collective-permute-start.23 = (bf16[640,512]{1,0:T(8,128)(2,1)S(1)}, bf16[640,512]{1,0:T(8,128)(2,1)S(1)}, u32[]{:S(2)}, u32[]{:S(2)}) collective-permute-start(bf16[640,512]{1,0:T(8,128)(2,1)S(1)} %collective-permute-done.14.refs_0_), channel_id=1, source_target_pairs={{0,2},{2,0},{4,6},{6,4},{8,10},{10,8},{12,14},{14,12},{1,3},{3,1},... | collective-permute-start | bytes 1966088 | tf_op jit(solution)/shard_map/ppermute | solution.py:42
  87.6 14.2 %collective-permute-start.24 = (bf16[640,512]{1,0:T(8,128)(2,1)S(1)}, bf16[640,512]{1,0:T(8,128)(2,1)S(1)}, u32[]{:S(2)}, u32[]{:S(2)}) collective-permute-start(bf16[640,512]{1,0:T(8,128)(2,1)S(1)} %collective-permute-done.16.refs_2_), channel_id=1, source_target_pairs={{0,2},{2,0},{4,6},{6,4},{8,10},{10,8},{12,14},{14,12},{1,3},{3,1},... | collective-permute-start | bytes 1966088 | tf_op jit(solution)/shard_map/ppermute | solution.py:42
  97.8 7.4 %collective-permute-start.26 = (bf16[640,512]{1,0:T(8,128)(2,1)S(1)}, bf16[640,512]{1,0:T(8,128)(2,1)S(1)}, u32[]{:S(2)}, u32[]{:S(2)}) collective-permute-start(bf16[640,512]{1,0:T(8,128)(2,1)S(1)} %collective-permute-done.25.refs_4_), channel_id=1, source_target_pairs={{0,2},{2,0},{4,6},{6,4},{8,10},{10,8},{12,14},{14,12},{1,3},{3,1},... | collective-permute-start | bytes 1966088 | tf_op jit(solution)/shard_map/ppermute | solution.py:42
  (11 other events, 51.0 us)

commit v4 on v3

--- a/solution.py
+++ b/solution.py
@@ -8,9 +8,10 @@
 
 PAIR = ((0, 1), (1, 0), (2, 3), (3, 2))
 MID = ((1, 2), (2, 1))
+IN = ((0, 1), (3, 2))
 OUT = ((1, 0), (2, 3))
 
-OWN, OWN_O, NB, NB_O, OPP, OPP_O, FAR, FAR_O, END, NEAR, HALF, PIECE = range(12)
+OWN, OWN_O, NB, NB_O, OPP, OPP_O, FAR, FAR_O, END, NEAR, SENT, CAME, PIECE = range(13)
 
 
 def table():
@@ -25,7 +26,7 @@
             row = []
             for q in (z, z ^ 1, opp, far):
                 row += [2 * q + c, 2 * q + 1 - c]
-            row += [int(z in (0, 3)), near, 1 - half]
+            row += [int(z in (0, 3)), near, int(z == 0), int(z == 1)]
             for q in (first, 1 - first):
                 row += [2 * q + c, 2 * q + 1 - c]
             rows.append(row)
@@ -94,35 +95,43 @@
     return ref[:, pl.ds(pl.multiple_of(start, 128), size)]
 
 
-def contrib(places, h, mine, other, weight, weight_o, total=None):
-    tokens, rows, cols = h.shape[0], *weight.shape
-
-    def body(s, h_ref, w, wo, *rest):
-        value = dot(columns(h_ref, s[mine] * rows, rows), w[...])
-        value = value + dot(columns(h_ref, s[other] * rows, rows), wo[...])
-        if total is not None:
-            value = value + rest[0][...]
-        rest[-1][...] = value
-
-    operands = [h, weight, weight_o] + ([] if total is None else [total])
+def contrib(places, h, mine, other, pairs, total=None):
+    tokens, (rows, cols) = h.shape[0], pairs[0][0].shape
+
+    def body(s, h_ref, *refs):
+        def run(w, wo):
+            value = dot(columns(h_ref, s[mine] * rows, rows), w[...])
+            value = value + dot(columns(h_ref, s[other] * rows, rows), wo[...])
+            if total is not None:
+                value = value + refs[-2][...]
+            refs[-1][...] = value
+
+        if len(pairs) == 1:
+            run(*refs[:2])
+        else:
+            for end in (0, 1):
+                pl.when(s[END] == end)(lambda end=end: run(*refs[2 * end:2 * end + 2]))
+
+    operands = [h] + [p for pair in pairs for p in pair] + ([] if total is None else [total])
     return call(body, places, operands, jax.ShapeDtypeStruct((tokens, cols), jnp.float32), "contrib")
 
 
 def as_rows(places, h, shape, first, piece=None):
     tokens, (rows, cols) = h.shape[0], shape
-    total = h.shape[1] // 2
+    quarter = h.shape[1] // 4
+    total = 3 * quarter
 
     def body(s, h_ref, *refs):
         out = refs[-1]
 
         @pl.when(s[END] == 1)
         def _():
-            count = min(rows // tokens, total // cols - first)
-            for k in range(count):
-                start = s[HALF] * total + (first + k) * cols
-                out[k * tokens:(k + 1) * tokens, :] = columns(h_ref, start, cols)
-            if count * tokens < rows:
-                out[count * tokens:, :] = jnp.zeros((rows - count * tokens, cols), out.dtype)
+            for k in range(rows // tokens):
+                start = (first + k) * cols
+                size = min(cols, total - start)
+                out[k * tokens:(k + 1) * tokens, :size] = columns(h_ref, s[SENT] * quarter + start, size)
+                if size < cols:
+                    out[k * tokens:(k + 1) * tokens, size:] = jnp.zeros((tokens, cols - size), out.dtype)
 
         @pl.when(s[END] == 0)
         def _():
@@ -153,31 +162,31 @@
     return call(body, places, [value], jax.ShapeDtypeStruct((16, 128), value.dtype), "tick")
 
 
-def to_opposite(places, h, total, nb, nb_o, opp, opp_o):
+def near_ends(places, h, total, nb, nb_o, opp, opp_o):
     tokens, (rows, cols) = h.shape[0], nb.shape
 
     def body(s, h_ref, total_ref, n, no, p, po, out):
-        value = total_ref[...]
-        for place, weight in ((NB, n), (NB_O, no)):
-            value = value + dot(columns(h_ref, s[place] * rows, rows), weight[...])
-        out[...] = value
+        @pl.when(s[END] == 1)
+        def _():
+            out[...] = total_ref[...]
 
         @pl.when(s[END] == 0)
         def _():
-            more = dot(columns(h_ref, s[OPP] * rows, rows), p[...])
-            out[...] += more + dot(columns(h_ref, s[OPP_O] * rows, rows), po[...])
+            value = total_ref[...]
+            for place, weight in ((NB, n), (NB_O, no), (OPP, p), (OPP_O, po)):
+                value = value + dot(columns(h_ref, s[place] * rows, rows), weight[...])
+            out[...] = value
 
     return call(
-        body, places, [h, total, nb, nb_o, opp, opp_o], jax.ShapeDtypeStruct((tokens, cols), jnp.float32), "to_opposite"
-    )
-
-
-def teachers(places, h, t_near, stale_opp, stale_opp_o, stale_far, stale_far_o, came_a, came_b):
-    tokens, (rows, cols) = h.shape[0], stale_opp.shape
-    fit = rows // tokens
-    width = h.shape[1] // 2
-
-    def body(s, h_ref, near, w, wo, v, vo, ca, cb, mine, sent, held):
+        body, places, [h, total, nb, nb_o, opp, opp_o], jax.ShapeDtypeStruct((tokens, cols), jnp.float32), "near_ends"
+    )
+
+
+def teachers(places, h, t_near, weights, came):
+    tokens, (rows, cols) = h.shape[0], weights[0].shape
+    quarter = h.shape[1] // 4
+
+    def body(s, h_ref, near, w, wo, p, po, v, vo, ca, cb, mine, sent, held):
         @pl.when(s[END] == 1)
         def _():
             mine[...] = near[...].astype(mine.dtype)
@@ -185,27 +194,28 @@
 
         @pl.when(s[END] == 0)
         def _():
-            for k in range(width // cols):
-                source, j = (ca, k) if k < fit else (cb, k - fit)
-                held[:, k * cols:(k + 1) * cols] = source[j * tokens:(j + 1) * tokens, :]
+            for k in range(-(-3 * quarter // cols)):
+                source, j = (ca, k) if k < rows // tokens else (cb, k - rows // tokens)
+                size = min(cols, 3 * quarter - k * cols)
+                held[:, k * cols:k * cols + size] = source[j * tokens:(j + 1) * tokens, :size]
 
             def away(place):
-                return columns(held, s[place] * rows - s[HALF] * width, rows)
-
-            end = dot(away(OPP), w[...]) + dot(away(OPP_O), wo[...])
-            both = jnp.concatenate([columns(h_ref, s[FAR] * rows, rows), away(FAR)], axis=0)
-            both_o = jnp.concatenate([columns(h_ref, s[FAR_O] * rows, rows), away(FAR_O)], axis=0)
-            far = dot(both, v[...]) + dot(both_o, vo[...])
+                return columns(held, s[place] * rows - s[CAME] * quarter, rows)
+
+            end = dot(away(OWN), w[...]) + dot(away(OWN_O), wo[...])
+            end = end + dot(away(OPP), p[...]) + dot(away(OPP_O), po[...])
+            own = jnp.concatenate([columns(h_ref, s[FAR] * rows, rows), away(FAR)], axis=0)
+            own_o = jnp.concatenate([columns(h_ref, s[FAR_O] * rows, rows), away(FAR_O)], axis=0)
+            far = dot(own, v[...]) + dot(own_o, vo[...])
             mine[...] = (near[...] + far[:tokens]).astype(mine.dtype)
             sent[...] = (end + far[tokens:]).astype(sent.dtype)
 
-    operands = [h, t_near, stale_opp, stale_opp_o, stale_far, stale_far_o, came_a, came_b]
     out = jax.ShapeDtypeStruct((tokens, cols), jnp.bfloat16)
 
     def with_scratch(*refs):
-        pl.run_scoped(lambda held: body(*refs, held), pltpu.VMEM((tokens, width), h.dtype))
-
-    return call(with_scratch, places, operands, [out, out], "teachers")
+        pl.run_scoped(lambda held: body(*refs, held), pltpu.VMEM((tokens, 3 * quarter), h.dtype))
+
+    return call(with_scratch, places, [h, t_near, *weights, *came], [out, out], "teachers")
 
 
 def difference(places, student, target_1, target_2, match):
@@ -277,50 +287,55 @@
 
     live_mid = along_z(live, MID)
     live_nb = along_z(live, PAIR)
-    stale_opp = along_z(stale, MID)
-    stale_nb = along_z(stale, PAIR)
     x_1 = over_x(live, False)
     live_o = across_cores(live)
     stale_o = across_cores(stale)
-    student = contrib(places, h, OWN, OWN_O, live, live_o)
-    t_near = contrib(places, h, OWN, OWN_O, stale, stale_o)
-
-    mid_2, nb_2, s_opp, s_nb = after(
-        (live_mid, live_nb, stale_opp, stale_nb), tick(places, stale_nb), student, t_near
-    )
+    student = contrib(places, h, OWN, OWN_O, [(live, live_o)])
+    t_near = contrib(places, h, OWN, OWN_O, [(stale, stale_o)])
+
+    mid_2, nb_2 = after((live_mid, live_nb), tick(places, live_nb), student, t_near)
     live_far_mid = along_z(nb_2, MID)
-    came_a = along_z(as_rows(places, h, live.shape, 0, mid_2), PAIR)
-    nb_x, mid_x, own_x, s_opp, s_nb = after((nb_2, mid_2, x_1, s_opp, s_nb), live_o, stale_o)
+    both = along_z(choose(places, END, stale, mid_2), PAIR)
+    nb_x, mid_x, own_x = after((nb_2, mid_2, x_1), live_o, stale_o)
     x_2 = over_x(choose(places, NEAR, mid_x, nb_x), True)
     live_nb_o = across_cores(nb_x)
-    stale_nb_o = across_cores(s_nb)
-    stale_opp_o = across_cores(s_opp)
+    live_mid_o = across_cores(mid_x)
     x_1_o = across_cores(own_x)
-    student = contrib(places, h, NB, NB_O, nb_x, live_nb_o, student)
-    t_near = to_opposite(places, h, t_near, s_nb, stale_nb_o, s_opp, stale_opp_o)
-
-    far_3, came_3, nb_3 = after((live_far_mid, came_a, stale_nb), tick(places, came_a), student, t_near)
-    stale_far = along_z(nb_3, MID)
-    came_b = along_z(as_rows(places, h, live.shape, fit, far_3), PAIR)
-    came_x, far_x, x_2 = after((came_3, far_3, x_2), x_1_o, student, t_near)
-    x_3 = over_x(choose(places, END, came_x, far_x), None)
-
-    stale_far, came_4 = after((stale_far, came_b), tick(places, came_b))
+
+    far_3, both_3, stale_3 = after((live_far_mid, both, stale), tick(places, both))
+    stale_opp = along_z(stale_3, MID)
+    came_a = along_z(as_rows(places, h, live.shape, 0, far_3), PAIR)
+    both_x, far_x, x_2, nb_x3 = after((both_3, far_3, x_2, live_nb), live_nb_o, live_mid_o, x_1_o)
+    x_3 = over_x(choose(places, END, both_x, far_x), None)
+    both_o = across_cores(both_3)
+    far_3o = across_cores(far_3)
+    student = contrib(places, h, NB, NB_O, [(nb_x3, live_nb_o)], student)
+
+    both_4, opp_4, came_4 = after((both_3, stale_opp, came_a), tick(places, came_a), student)
+    rest = -(-3 * h.shape[1] // (4 * live.shape[1])) - fit
+    (h_4,) = after((h,), stale_3)
+    more = as_rows(places, h_4, (rest * h.shape[0], live.shape[1]), fit)
+    (more,) = after((more,), opp_4)
+    stale_far = along_z(both_4, MID)
+    came_b = along_z(more, IN)
+    came_x, x_3, opp_x = after((came_4, x_3, opp_4), both_o, far_3o)
+    x_4 = over_x(came_x, END)
+    stale_opp_o = across_cores(opp_4)
+    came_4o = across_cores(came_4)
+    student = contrib(places, h, OPP, OPP_O, [(live_mid, live_mid_o), (both_3, both_o)], student)
+    t_near = near_ends(places, h, t_near, both_4, both_o, opp_4, stale_opp_o)
+
+    stale_far, came_b = after((stale_far, came_b), tick(places, came_b), student, t_near)
     stale_far_o = across_cores(stale_far)
-    x_4 = over_x(came_4, END)
-    (t_near,) = after((t_near,), x_3)
+    (t_near,) = after((t_near,), x_4, came_4o)
     t_mine, t_end = teachers(
-        places, h, t_near, stale_opp, stale_opp_o, stale_far, stale_far_o, came_3, came_4
-    )
-    came_t, mid_t, far_t, came_t4, x_2t, x_3t = after((came_3, live_mid, far_3, came_4, x_2, x_3), t_mine)
-    live_opp = choose(places, END, came_t, mid_t)
-    live_far = choose(places, END, came_t4, far_t)
-    live_opp_o = across_cores(live_opp)
-    live_far_o = across_cores(live_far)
+        places, h, t_near, (stale, stale_o, opp_4, stale_opp_o, stale_far, stale_far_o), (came_4, came_b)
+    )
+    x_2t, x_3t, x_4t, student = after((x_2, x_3, x_4, student), t_mine)
     x_2_o = across_cores(x_2t)
     x_3_o = across_cores(x_3t)
-    student = contrib(places, h, OPP, OPP_O, live_opp, live_opp_o, student)
-    student = contrib(places, h, FAR, FAR_O, live_far, live_far_o, student)
+    x_4_o = across_cores(x_4t)
+    student = contrib(places, h, FAR, FAR_O, [(far_3, far_3o), (came_4, came_4o)], student)
 
     target_1 = partner(t_mine, "mp", 0)
     route = []
@@ -331,11 +346,13 @@
     target_2 = lax.ppermute(t_end, ("mp", "fsdp"), route)
     mismatch = difference(places, student, target_1, target_2, match)
     mismatch_o = partner(mismatch, "tp", 0)
-    (x_4,) = after((x_4,), mismatch)
-    x_4_o = across_cores(x_4)
     own = gradient(
         places, mismatch,
-        ((live_opp, live_opp_o, live_far, live_far_o),) * 2 + ((live, live_o, live_nb, live_nb_o),),
+        (
+            (live_mid, live_mid_o, far_3, far_3o),
+            (both_3, both_o, came_4, came_4o),
+            (live, live_o, live_nb, live_nb_o),
+        ),
     )
     grad = gradient(
         places, mismatch_o,

time: 109 us -> 105 us (0.963)
  waiting for transfers between devices: 51 us -> 48.5 us
  starting transfers between devices: 37.2 us -> 39.1 us
  Pallas kernels: 15.2 us -> 13.7 us
    ppermute x8, starting transfers between devices: 18.8 us -> 21.9 us  [along_z(): return lax.ppermute(block, 'fsdp', route)]
    ppermute x1, waiting for transfers between devices: 3.3 us -> 6.14 us  [line_of_four(): target_2 = lax.ppermute(t_end, ('mp', 'fsdp'), route)]
    ppermute x8, waiting for transfers between devices: 36.1 us -> 33.8 us  [along_z(): return lax.ppermute(block, 'fsdp', route)]
    ppermute x4, waiting for transfers between devices: 6.31 us -> 4.58 us  [over_x(): return lax.ppermute(block, ('fsdp', 'tp'), route)]
    pallas_call x16 -> x15, Pallas kernels: 15.2 us -> 13.7 us  [call(): pl.pallas_call(body, out_shape=shapes, in_specs=[pl.BlockSpec(memory_spac...]
    ppermute x14 -> x15, waiting for transfers between devices: 5.34 us -> 3.94 us  [partner(): return lax.ppermute(block, axis, route)]
    ppermute x4, starting transfers between devices: 10.4 us -> 9.1 us  [over_x(): return lax.ppermute(block, ('fsdp', 'tp'), route)]
    unnamed x16 -> x12, local copies, waits for them, and re-layouts: 3.68 us -> 2.64 us
  transfers between devices with their start and end apart: 27 -> 28, of which waited for: 9 -> 9; matrix products, arithmetic and copies ran while one was open for 1% -> 1% of each run, Pallas kernels for 10% -> 10%
where the time goes in v4:
time: 105 us
  waiting for transfers between devices  48.5 us (46%)
  starting transfers between devices  39.1 us (37%)
  Pallas kernels  13.7 us (13%)
  local copies, waits for them, and re-layouts  3.34 us (3%)
    ppermute x8, waiting for transfers between devices, along_z(): return lax.ppermute(block, 'fsdp', route)  33.8 us
    ppermute x8, starting transfers between devices, along_z(): return lax.ppermute(block, 'fsdp', route)  21.9 us
    pallas_call x15, Pallas kernels, call(): pl.pallas_call(body, out_shape=shapes, in_specs=[pl.BlockSpec(memory_spac...  13.7 us
    ppermute x4, starting transfers between devices, over_x(): return lax.ppermute(block, ('fsdp', 'tp'), route)  9.1 us
    ppermute x15, starting transfers between devices, partner(): return lax.ppermute(block, axis, route)  6.72 us
    ppermute x1, waiting for transfers between devices, line_of_four(): target_2 = lax.ppermute(t_end, ('mp', 'fsdp'), route)  6.14 us
    ppermute x4, waiting for transfers between devices, over_x(): return lax.ppermute(block, ('fsdp', 'tp'), route)  4.58 us
    ppermute x15, waiting for transfers between devices, partner(): return lax.ppermute(block, axis, route)  3.94 us
  transfers between devices with their start and end apart: 28, of which 9 were waited for; matrix products, arithmetic and copies ran while one was open for 1% of the time, Pallas kernels for 10%

profile of v4, /device:TPU:0, one launch (start us, length us, event | category | flops | bytes accessed | tf_op | source)
XLA Modules:
  0.0 105.0 jit_solution(9343818014691852331)
XLA Ops:
  0.5 3.0 %collective-permute-start.1 = (bf16[640,512]{1,0:T(8,128)(2,1)}, bf16[640,512]{1,0:T(8,128)(2,1)S(1)}, u32[]{:S(2)}, u32[]{:S(2)}) collective-permute-start(bf16[640,512]{1,0:T(8,128)(2,1)} %bitcast.21), channel_id=1, source_target_pairs={{0,4},{2,6},{4,0},{6,2},{8,12},{10,14},{12,8},{14,10},{1,5},{3,7},... | collective-permute-start | bytes 1966088 | tf_op jit(solution)/shard_map/ppermute | solution.py:48
  4.2 1.3 %collective-permute-start.9 = (bf16[640,512]{1,0:T(8,128)(2,1)}, bf16[640,512]{1,0:T(8,128)(2,1)S(1)}, u32[]{:S(2)}, u32[]{:S(2)}) collective-permute-start(bf16[640,512]{1,0:T(8,128)(2,1)} %bitcast.23), channel_id=1, source_target_pairs={{1,0},{3,2},{5,4},{7,6},{8,9},{10,11},{12,13},{14,15},{17,16},{19,... | collective-permute-start | bytes 1966088 | tf_op jit(solution)/shard_map/ppermute | solution.py:63
  6.2 1.4 %copy-done = bf16[1,160,5120]{2,1,0:T(8,128)(2,1)S(1)} copy-done((bf16[1,160,5120]{2,1,0:T(8,128)(2,1)S(1)}, bf16[1,160,5120]{2,1,0:T(8,128)(2,1)}, u32[]{:S(2)}) %copy-start) | copy-done | bytes 1638424
  7.7 1.1 %copy-done.3 = bf16[1,640,512]{2,1,0:T(8,128)(2,1)S(1)} copy-done((bf16[1,640,512]{2,1,0:T(8,128)(2,1)S(1)}, bf16[1,640,512]{2,1,0:T(8,128)(2,1)}, u32[]{:S(2)}) %copy-start.3) | copy-done | bytes 655384
  10.8 7.8 %collective-permute-done.1.no_ref.refs_0_.refs_10_ = bf16[640,512]{1,0:T(8,128)(2,1)S(1)} collective-permute-done((bf16[640,512]{1,0:T(8,128)(2,1)}, bf16[640,512]{1,0:T(8,128)(2,1)S(1)}, u32[]{:S(2)}, u32[]{:S(2)}) %collective-permute-start.1) | collective-permute-done | bytes 655392 | tf_op jit(solution)/shard_map/ppermute | solution.py:48
  19.3 4.8 %collective-permute-start.5 = (bf16[640,512]{1,0:T(8,128)(2,1)S(1)}, bf16[640,512]{1,0:T(8,128)(2,1)S(1)}, u32[]{:S(2)}, u32[]{:S(2)}) collective-permute-start(bf16[640,512]{1,0:T(8,128)(2,1)S(1)} %choose.3), channel_id=1, source_target_pairs={{0,4},{2,6},{4,0},{6,2},{8,12},{10,14},{12,8},{14,10},{1,5},{3,7},... | collective-permute-start | bytes 1966088 | tf_op jit(solution)/shard_map/ppermute | solution.py:48
  25.4 1.3 %collective-permute-start.10 = (bf16[640,512]{1,0:T(8,128)(2,1)S(1)}, bf16[640,512]{1,0:T(8,128)(2,1)S(1)}, u32[]{:S(2)}, u32[]{:S(2)}) collective-permute-start(bf16[640,512]{1,0:T(8,128)(2,1)S(1)} %choose.4), channel_id=1, source_target_pairs={{1,0},{3,2},{5,4},{4,5},{7,6},{6,7},{8,9},{9,8},{10,11},{11,10},{1... | collective-permute-start | bytes 1966088 | tf_op jit(solution)/shard_map/ppermute | solution.py:63
  27.3 10.9 %collective-permute-done.5.yes_ref.refs_2_.n.refs_4_ = bf16[640,512]{1,0:T(8,128)(2,1)S(1)} collective-permute-done((bf16[640,512]{1,0:T(8,128)(2,1)S(1)}, bf16[640,512]{1,0:T(8,128)(2,1)S(1)}, u32[]{:S(2)}, u32[]{:S(2)}) %collective-permute-start.5) | collective-permute-done | bytes 655392 | tf_op jit(solution)/shard_map/ppermute | solution.py:48
  38.7 3.7 %collective-permute-start.8 = (bf16[640,512]{1,0:T(8,128)(2,1)S(1)}, bf16[640,512]{1,0:T(8,128)(2,1)S(1)}, u32[]{:S(2)}, u32[]{:S(2)}) collective-permute-start(bf16[640,512]{1,0:T(8,128)(2,1)S(1)} %as_rows.2), channel_id=1, source_target_pairs={{0,4},{2,6},{4,0},{6,2},{8,12},{10,14},{12,8},{14,10},{1,5},{3,7},... | collective-permute-start | bytes 1966088 | tf_op jit(solution)/shard_map/ppermute | solution.py:48
  44.1 3.1 %collective-permute-start.15 = (bf16[640,512]{1,0:T(8,128)(2,1)S(1)}, bf16[640,512]{1,0:T(8,128)(2,1)S(1)}, u32[]{:S(2)}, u32[]{:S(2)}) collective-permute-start(bf16[640,512]{1,0:T(8,128)(2,1)S(1)} %choose.5), channel_id=1, source_target_pairs={{0,1},{2,3},{4,5},{6,7},{9,8},{11,10},{13,12},{15,14},{16,17},{18,... | collective-permute-start | bytes 1966088 | tf_op jit(solution)/shard_map/ppermute | solution.py:63
  49.4 6.6 %collective-permute-done.8.refs_9_.refs_2_.refs_6_ = bf16[640,512]{1,0:T(8,128)(2,1)S(1)} collective-permute-done((bf16[640,512]{1,0:T(8,128)(2,1)S(1)}, bf16[640,512]{1,0:T(8,128)(2,1)S(1)}, u32[]{:S(2)}, u32[]{:S(2)}) %collective-permute-start.8) | collective-permute-done | bytes 655392 | tf_op jit(solution)/shard_map/ppermute | solution.py:48
  56.0 7.6 %collective-permute-start.20 = (bf16[640,512]{1,0:T(8,128)(2,1)S(1)}, bf16[640,512]{1,0:T(8,128)(2,1)S(1)}, u32[]{:S(2)}, u32[]{:S(2)}) collective-permute-start(bf16[640,512]{1,0:T(8,128)(2,1)S(1)} %as_rows.3), channel_id=1, source_target_pairs={{0,4},{2,6},{12,8},{14,10},{1,5},{3,7},{13,9},{15,11},{16,20},{18,... | collective-permute-start | bytes 1966088 | tf_op jit(solution)/shard_map/ppermute | solution.py:48
  64.6 3.4 %collective-permute-start.17 = (bf16[640,512]{1,0:T(8,128)(2,1)S(1)}, bf16[640,512]{1,0:T(8,128)(2,1)S(1)}, u32[]{:S(2)}, u32[]{:S(2)}) collective-permute-start(bf16[640,512]{1,0:T(8,128)(2,1)S(1)} %collective-permute-done.8.refs_9_.refs_2_.refs_6_), channel_id=1, source_target_pairs={{0,1},{2,3},{13,12},{15,14},{16,17},{18,19},{29,28},{31,30}} | collective-permute-start | bytes 1966088 | tf_op jit(solution)/shard_map/ppermute | solution.py:63
  69.6 8.6 %collective-permute-done.20.refs_10_ = bf16[640,512]{1,0:T(8,128)(2,1)S(1)} collective-permute-done((bf16[640,512]{1,0:T(8,128)(2,1)S(1)}, bf16[640,512]{1,0:T(8,128)(2,1)S(1)}, u32[]{:S(2)}, u32[]{:S(2)}) %collective-permute-start.20) | collective-permute-done | bytes 655392 | tf_op jit(solution)/shard_map/ppermute | solution.py:48
  78.2 4.2 %collective-permute-done.17.refs_4_ = bf16[640,512]{1,0:T(8,128)(2,1)S(1)} collective-permute-done((bf16[640,512]{1,0:T(8,128)(2,1)S(1)}, bf16[640,512]{1,0:T(8,128)(2,1)S(1)}, u32[]{:S(2)}, u32[]{:S(2)}) %collective-permute-start.17) | collective-permute-done | bytes 655392 | tf_op jit(solution)/shard_map/ppermute | solution.py:63
  83.6 1.4 %collective-permute-start.23 = (bf16[160,512]{1,0:T(8,128)(2,1)S(1)}, bf16[160,512]{1,0:T(8,128)(2,1)S(1)}, u32[]{:S(2)}, u32[]{:S(2)}) collective-permute-start(bf16[160,512]{1,0:T(8,128)(2,1)S(1)} %get-tuple-element.57), channel_id=1, source_target_pairs={{4,16},{6,18},{8,28},{10,30},{20,0},{22,2},{24,12},{26,14},{5,17},... | collective-permute-start | bytes 491528 | tf_op jit(solution)/shard_map/ppermute | solution.py:346
  85.0 1.6 %collective-permute-start.22 = (bf16[160,512]{1,0:T(8,128)(2,1)S(1)}, bf16[160,512]{1,0:T(8,128)(2,1)S(1)}, u32[]{:S(2)}, u32[]{:S(2)}) collective-permute-start(bf16[160,512]{1,0:T(8,128)(2,1)S(1)} %get-tuple-element.55), channel_id=1, source_target_pairs={{0,16},{16,0},{1,17},{17,1},{2,18},{18,2},{3,19},{19,3},{4,20},{20... | collective-permute-start | bytes 491528 | tf_op jit(solution)/shard_map/ppermute | solution.py:43
  86.6 1.0 contrib.9.student_ref
  87.6 6.1 %collective-permute-done.23.two = bf16[160,512]{1,0:T(8,128)(2,1)S(1)} collective-permute-done((bf16[160,512]{1,0:T(8,128)(2,1)S(1)}, bf16[160,512]{1,0:T(8,128)(2,1)S(1)}, u32[]{:S(2)}, u32[]{:S(2)}) %collective-permute-start.23) | collective-permute-done | bytes 163872 | tf_op jit(solution)/shard_map/ppermute | solution.py:346
  93.8 1.4 %collective-permute-done.22.one = bf16[160,512]{1,0:T(8,128)(2,1)S(1)} collective-permute-done((bf16[160,512]{1,0:T(8,128)(2,1)S(1)}, bf16[160,512]{1,0:T(8,128)(2,1)S(1)}, u32[]{:S(2)}, u32[]{:S(2)}) %collective-permute-start.22) | collective-permute-done | bytes 163872 | tf_op jit(solution)/shard_map/ppermute | solution.py:43
  95.9 2.5 %collective-permute-start.24 = (bf16[160,512]{1,0:T(8,128)(2,1)S(1)}, bf16[160,512]{1,0:T(8,128)(2,1)S(1)}, u32[]{:S(2)}, u32[]{:S(2)}) collective-permute-start(bf16[160,512]{1,0:T(8,128)(2,1)S(1)} %difference.1.left_ref), channel_id=1, source_target_pairs={{0,1},{1,0},{2,3},{3,2},{4,5},{5,4},{6,7},{7,6},{8,9},{9,8},{10,11... | collective-permute-start | bytes 491528 | tf_op jit(solution)/shard_map/ppermute | solution.py:43
  98.5 1.5 %gradient.2.refs_8_ = f32[160,2560]{1,0:T(8,128)S(1)} custom-call(s32[16]{0:T(128)S(1)} %dynamic-slice_bitcast_fusion.s.refs_0_, bf16[160,512]{1,0:T(8,128)(2,1)S(1)} %difference.1.left_ref, bf16[640,512]{1,0:T(8,128)(2,1)S(1)} %collective-permute-done.no_ref.yes_ref.refs_0_, bf16[640,512]{1,0:T(8,128)(2,1)S(1)} %collective-permute-done.12.refs_1_, ...), custom_call_target="tpu_custom_call" | custom-call | flops 1 | bytes 1 | tf_op jit(solution)/shard_map/gradient/pallas_call | solution.py:82
  100.0 2.5 %collective-permute-done.24.left_ref = bf16[160,512]{1,0:T(8,128)(2,1)S(1)} collective-permute-done((bf16[160,512]{1,0:T(8,128)(2,1)S(1)}, bf16[160,512]{1,0:T(8,128)(2,1)S(1)}, u32[]{:S(2)}, u32[]{:S(2)}) %collective-permute-start.24) | collective-permute-done | bytes 163872 | tf_op jit(solution)/shard_map/ppermute | solution.py:43
  102.5 2.4 %gradient.3 = bf16[160,2560]{1,0:T(8,128)(2,1)} custom-call(s32[16]{0:T(128)S(1)} %dynamic-slice_bitcast_fusion.s.refs_0_, bf16[160,512]{1,0:T(8,128)(2,1)S(1)} %collective-permute-done.24.left_ref, bf16[640,512]{1,0:T(8,128)(2,1)S(1)} %collective-permute-done.10.refs_0_, bf16[640,512]{1,0:T(8,128)(2,1)S(1)} %collective-permute-done.25.refs_1_, ...), custom_call_target="tpu_custom_call" | custom-call | flops 1 | bytes 1 | tf_op jit(solution)/shard_map/gradient/pallas_call | solution.py:82
  (60 shorter events, 15.4 us)
Async XLA Ops:
  0.5 9.3 %collective-permute-start.3 = (bf16[640,512]{1,0:T(8,128)(2,1)}, bf16[640,512]{1,0:T(8,128)(2,1)S(1)}, u32[]{:S(2)}, u32[]{:S(2)}) collective-permute-start(bf16[640,512]{1,0:T(8,128)(2,1)} %bitcast.15), channel_id=1, source_target_pairs={{0,2},{2,0},{4,6},{6,4},{8,10},{10,8},{12,14},{14,12},{1,3},{3,1},... | collective-permute-start | bytes 1966088 | tf_op jit(solution)/shard_map/ppermute | solution.py:43
  0.5 18.1 %collective-permute-start.1 = (bf16[640,512]{1,0:T(8,128)(2,1)}, bf16[640,512]{1,0:T(8,128)(2,1)S(1)}, u32[]{:S(2)}, u32[]{:S(2)}) collective-permute-start(bf16[640,512]{1,0:T(8,128)(2,1)} %bitcast.21), channel_id=1, source_target_pairs={{0,4},{2,6},{4,0},{6,2},{8,12},{10,14},{12,8},{14,10},{1,5},{3,7},... | collective-permute-start | bytes 1966088 | tf_op jit(solution)/shard_map/ppermute | solution.py:48
  3.5 15.1 %collective-permute-start = (bf16[640,512]{1,0:T(8,128)(2,1)}, bf16[640,512]{1,0:T(8,128)(2,1)S(1)}, u32[]{:S(2)}, u32[]{:S(2)}) collective-permute-start(bf16[640,512]{1,0:T(8,128)(2,1)} %bitcast.22), channel_id=1, source_target_pairs={{4,8},{6,10},{8,4},{10,6},{5,9},{7,11},{9,5},{11,7},{20,24},{22,26... | collective-permute-start | bytes 1966088 | tf_op jit(solution)/shard_map/ppermute | solution.py:48
  4.2 20.5 %collective-permute-start.9 = (bf16[640,512]{1,0:T(8,128)(2,1)}, bf16[640,512]{1,0:T(8,128)(2,1)S(1)}, u32[]{:S(2)}, u32[]{:S(2)}) collective-permute-start(bf16[640,512]{1,0:T(8,128)(2,1)} %bitcast.23), channel_id=1, source_target_pairs={{1,0},{3,2},{5,4},{7,6},{8,9},{10,11},{12,13},{14,15},{17,16},{19,... | collective-permute-start | bytes 1966088 | tf_op jit(solution)/shard_map/ppermute | solution.py:63
  19.3 18.9 %collective-permute-start.5 = (bf16[640,512]{1,0:T(8,128)(2,1)S(1)}, bf16[640,512]{1,0:T(8,128)(2,1)S(1)}, u32[]{:S(2)}, u32[]{:S(2)}) collective-permute-start(bf16[640,512]{1,0:T(8,128)(2,1)S(1)} %choose.3), channel_id=1, source_target_pairs={{0,4},{2,6},{4,0},{6,2},{8,12},{10,14},{12,8},{14,10},{1,5},{3,7},... | collective-permute-start | bytes 1966088 | tf_op jit(solution)/shard_map/ppermute | solution.py:48
  24.1 14.1 %collective-permute-start.4 = (bf16[640,512]{1,0:T(8,128)(2,1)S(1)}, bf16[640,512]{1,0:T(8,128)(2,1)S(1)}, u32[]{:S(2)}, u32[]{:S(2)}) collective-permute-start(bf16[640,512]{1,0:T(8,128)(2,1)S(1)} %collective-permute-done.1.no_ref.refs_0_.refs_10_), channel_id=1, source_target_pairs={{4,8},{6,10},{8,4},{10,6},{5,9},{7,11},{9,5},{11,7},{20,24},{22,26... | collective-permute-start | bytes 1966088 | tf_op jit(solution)/shard_map/ppermute | solution.py:48
  25.4 17.4 %collective-permute-start.10 = (bf16[640,512]{1,0:T(8,128)(2,1)S(1)}, bf16[640,512]{1,0:T(8,128)(2,1)S(1)}, u32[]{:S(2)}, u32[]{:S(2)}) collective-permute-start(bf16[640,512]{1,0:T(8,128)(2,1)S(1)} %choose.4), channel_id=1, source_target_pairs={{1,0},{3,2},{5,4},{4,5},{7,6},{6,7},{8,9},{9,8},{10,11},{11,10},{1... | collective-permute-start | bytes 1966088 | tf_op jit(solution)/shard_map/ppermute | solution.py:63
  26.7 16.8 %collective-permute-start.12 = (bf16[640,512]{1,0:T(8,128)(2,1)S(1)}, bf16[640,512]{1,0:T(8,128)(2,1)S(1)}, u32[]{:S(2)}, u32[]{:S(2)}) collective-permute-start(bf16[640,512]{1,0:T(8,128)(2,1)S(1)} %collective-permute-done.no_ref.yes_ref.refs_0_), channel_id=1, source_target_pairs={{0,2},{2,0},{4,6},{6,4},{8,10},{10,8},{12,14},{14,12},{1,3},{3,1},... | collective-permute-start | bytes 1966088 | tf_op jit(solution)/shard_map/ppermute | solution.py:43
  26.8 16.7 %collective-permute-start.13 = (bf16[640,512]{1,0:T(8,128)(2,1)S(1)}, bf16[640,512]{1,0:T(8,128)(2,1)S(1)}, u32[]{:S(2)}, u32[]{:S(2)}) collective-permute-start(bf16[640,512]{1,0:T(8,128)(2,1)S(1)} %collective-permute-done.9.refs_6_), channel_id=1, source_target_pairs={{0,2},{2,0},{4,6},{6,4},{8,10},{10,8},{12,14},{14,12},{1,3},{3,1},... | collective-permute-start | bytes 1966088 | tf_op jit(solution)/shard_map/ppermute | solution.py:43
  38.7 17.2 %collective-permute-start.8 = (bf16[640,512]{1,0:T(8,128)(2,1)S(1)}, bf16[640,512]{1,0:T(8,128)(2,1)S(1)}, u32[]{:S(2)}, u32[]{:S(2)}) collective-permute-start(bf16[640,512]{1,0:T(8,128)(2,1)S(1)} %as_rows.2), channel_id=1, source_target_pairs={{0,4},{2,6},{4,0},{6,2},{8,12},{10,14},{12,8},{14,10},{1,5},{3,7},... | collective-permute-start | bytes 1966088 | tf_op jit(solution)/shard_map/ppermute | solution.py:48
  42.8 13.2 %collective-permute-start.7 = (bf16[640,512]{1,0:T(8,128)(2,1)S(1)}, bf16[640,512]{1,0:T(8,128)(2,1)S(1)}, u32[]{:S(2)}, u32[]{:S(2)}) collective-permute-start(bf16[640,512]{1,0:T(8,128)(2,1)S(1)} %bitcast.18), channel_id=1, source_target_pairs={{4,8},{6,10},{8,4},{10,6},{5,9},{7,11},{9,5},{11,7},{20,24},{22,26... | collective-permute-start | bytes 1966088 | tf_op jit(solution)/shard_map/ppermute | solution.py:48
  44.1 19.4 %collective-permute-start.15 = (bf16[640,512]{1,0:T(8,128)(2,1)S(1)}, bf16[640,512]{1,0:T(8,128)(2,1)S(1)}, u32[]{:S(2)}, u32[]{:S(2)}) collective-permute-start(bf16[640,512]{1,0:T(8,128)(2,1)S(1)} %choose.5), channel_id=1, source_target_pairs={{0,1},{2,3},{4,5},{6,7},{9,8},{11,10},{13,12},{15,14},{16,17},{18,... | collective-permute-start | bytes 1966088 | tf_op jit(solution)/shard_map/ppermute | solution.py:63
  47.2 17.0 %collective-permute-start.6 = (bf16[640,512]{1,0:T(8,128)(2,1)S(1)}, bf16[640,512]{1,0:T(8,128)(2,1)S(1)}, u32[]{:S(2)}, u32[]{:S(2)}) collective-permute-start(bf16[640,512]{1,0:T(8,128)(2,1)S(1)} %collective-permute-done.4.refs_0_.no_ref.refs_2_), channel_id=1, source_target_pairs={{0,2},{2,0},{4,6},{6,4},{8,10},{10,8},{12,14},{14,12},{1,3},{3,1},... | collective-permute-start | bytes 1966088 | tf_op jit(solution)/shard_map/ppermute | solution.py:43
  47.3 17.3 %collective-permute-start.16 = (bf16[640,512]{1,0:T(8,128)(2,1)S(1)}, bf16[640,512]{1,0:T(8,128)(2,1)S(1)}, u32[]{:S(2)}, u32[]{:S(2)}) collective-permute-start(bf16[640,512]{1,0:T(8,128)(2,1)S(1)} %collective-permute-done.5.yes_ref.refs_2_.n.refs_4_), channel_id=1, source_target_pairs={{0,2},{2,0},{4,6},{6,4},{8,10},{10,8},{12,14},{14,12},{1,3},{3,1},... | collective-permute-start | bytes 1966088 | tf_op jit(solution)/shard_map/ppermute | solution.py:43
  56.0 13.0 %collective-permute-start.18 = (bf16[640,512]{1,0:T(8,128)(2,1)S(1)}, bf16[640,512]{1,0:T(8,128)(2,1)S(1)}, u32[]{:S(2)}, u32[]{:S(2)}) collective-permute-start(bf16[640,512]{1,0:T(8,128)(2,1)S(1)} %collective-permute-done.7.p.refs_5_), channel_id=1, source_target_pairs={{0,2},{2,0},{4,6},{6,4},{8,10},{10,8},{12,14},{14,12},{1,3},{3,1},... | collective-permute-start | bytes 1966088 | tf_op jit(solution)/shard_map/ppermute | solution.py:43
  56.0 22.2 %collective-permute-start.20 = (bf16[640,512]{1,0:T(8,128)(2,1)S(1)}, bf16[640,512]{1,0:T(8,128)(2,1)S(1)}, u32[]{:S(2)}, u32[]{:S(2)}) collective-permute-start(bf16[640,512]{1,0:T(8,128)(2,1)S(1)} %as_rows.3), channel_id=1, source_target_pairs={{0,4},{2,6},{12,8},{14,10},{1,5},{3,7},{13,9},{15,11},{16,20},{18,... | collective-permute-start | bytes 1966088 | tf_op jit(solution)/shard_map/ppermute | solution.py:48
  63.5 14.6 %collective-permute-start.19 = (bf16[640,512]{1,0:T(8,128)(2,1)S(1)}, bf16[640,512]{1,0:T(8,128)(2,1)S(1)}, u32[]{:S(2)}, u32[]{:S(2)}) collective-permute-start(bf16[640,512]{1,0:T(8,128)(2,1)S(1)} %collective-permute-done.5.yes_ref.refs_2_.n.refs_4_), channel_id=1, source_target_pairs={{4,8},{6,10},{8,4},{10,6},{5,9},{7,11},{9,5},{11,7},{20,24},{22,26... | collective-permute-start | bytes 1966088 | tf_op jit(solution)/shard_map/ppermute | solution.py:48
  64.3 13.9 %collective-permute-start.14 = (bf16[640,512]{1,0:T(8,128)(2,1)S(1)}, bf16[640,512]{1,0:T(8,128)(2,1)S(1)}, u32[]{:S(2)}, u32[]{:S(2)}) collective-permute-start(bf16[640,512]{1,0:T(8,128)(2,1)S(1)} %collective-permute-done.8.refs_9_.refs_2_.refs_6_), channel_id=1, source_target_pairs={{0,2},{2,0},{4,6},{6,4},{8,10},{10,8},{12,14},{14,12},{1,3},{3,1},... | collective-permute-start | bytes 1966088 | tf_op jit(solution)/shard_map/ppermute | solution.py:43
  64.6 17.8 %collective-permute-start.17 = (bf16[640,512]{1,0:T(8,128)(2,1)S(1)}, bf16[640,512]{1,0:T(8,128)(2,1)S(1)}, u32[]{:S(2)}, u32[]{:S(2)}) collective-permute-start(bf16[640,512]{1,0:T(8,128)(2,1)S(1)} %collective-permute-done.8.refs_9_.refs_2_.refs_6_), channel_id=1, source_target_pairs={{0,1},{2,3},{13,12},{15,14},{16,17},{18,19},{29,28},{31,30}} | collective-permute-start | bytes 1966088 | tf_op jit(solution)/shard_map/ppermute | solution.py:63
  83.0 19.5 %collective-permute-start.25 = (bf16[640,512]{1,0:T(8,128)(2,1)S(1)}, bf16[640,512]{1,0:T(8,128)(2,1)S(1)}, u32[]{:S(2)}, u32[]{:S(2)}) collective-permute-start(bf16[640,512]{1,0:T(8,128)(2,1)S(1)} %collective-permute-done.10.refs_0_), channel_id=1, source_target_pairs={{0,2},{2,0},{4,6},{6,4},{8,10},{10,8},{12,14},{14,12},{1,3},{3,1},... | collective-permute-start | bytes 1966088 | tf_op jit(solution)/shard_map/ppermute | solution.py:43
  83.0 19.5 %collective-permute-start.26 = (bf16[640,512]{1,0:T(8,128)(2,1)S(1)}, bf16[640,512]{1,0:T(8,128)(2,1)S(1)}, u32[]{:S(2)}, u32[]{:S(2)}) collective-permute-start(bf16[640,512]{1,0:T(8,128)(2,1)S(1)} %collective-permute-done.15.refs_2_), channel_id=1, source_target_pairs={{0,2},{2,0},{4,6},{6,4},{8,10},{10,8},{12,14},{14,12},{1,3},{3,1},... | collective-permute-start | bytes 1966088 | tf_op jit(solution)/shard_map/ppermute | solution.py:43
  83.5 19.0 %collective-permute-start.27 = (bf16[640,512]{1,0:T(8,128)(2,1)S(1)}, bf16[640,512]{1,0:T(8,128)(2,1)S(1)}, u32[]{:S(2)}, u32[]{:S(2)}) collective-permute-start(bf16[640,512]{1,0:T(8,128)(2,1)S(1)} %collective-permute-done.17.refs_4_), channel_id=1, source_target_pairs={{0,2},{2,0},{4,6},{6,4},{8,10},{10,8},{12,14},{14,12},{1,3},{3,1},... | collective-permute-start | bytes 1966088 | tf_op jit(solution)/shard_map/ppermute | solution.py:43
  83.6 10.1 %collective-permute-start.23 = (bf16[160,512]{1,0:T(8,128)(2,1)S(1)}, bf16[160,512]{1,0:T(8,128)(2,1)S(1)}, u32[]{:S(2)}, u32[]{:S(2)}) collective-permute-start(bf16[160,512]{1,0:T(8,128)(2,1)S(1)} %get-tuple-element.57), channel_id=1, source_target_pairs={{4,16},{6,18},{8,28},{10,30},{20,0},{22,2},{24,12},{26,14},{5,17},... | collective-permute-start | bytes 491528 | tf_op jit(solution)/shard_map/ppermute | solution.py:346
  85.0 10.1 %collective-permute-start.22 = (bf16[160,512]{1,0:T(8,128)(2,1)S(1)}, bf16[160,512]{1,0:T(8,128)(2,1)S(1)}, u32[]{:S(2)}, u32[]{:S(2)}) collective-permute-start(bf16[160,512]{1,0:T(8,128)(2,1)S(1)} %get-tuple-element.55), channel_id=1, source_target_pairs={{0,16},{16,0},{1,17},{17,1},{2,18},{18,2},{3,19},{19,3},{4,20},{20... | collective-permute-start | bytes 491528 | tf_op jit(solution)/shard_map/ppermute | solution.py:43
  (10 other events, 79.8 us)

commit v5 on v4

--- a/solution.py
+++ b/solution.py
@@ -305,9 +305,9 @@
     far_3, both_3, stale_3 = after((live_far_mid, both, stale), tick(places, both))
     stale_opp = along_z(stale_3, MID)
     came_a = along_z(as_rows(places, h, live.shape, 0, far_3), PAIR)
+    both_o = across_cores(both_3)
     both_x, far_x, x_2, nb_x3 = after((both_3, far_3, x_2, live_nb), live_nb_o, live_mid_o, x_1_o)
     x_3 = over_x(choose(places, END, both_x, far_x), None)
-    both_o = across_cores(both_3)
     far_3o = across_cores(far_3)
     student = contrib(places, h, NB, NB_O, [(nb_x3, live_nb_o)], student)
 
@@ -315,15 +315,15 @@
     rest = -(-3 * h.shape[1] // (4 * live.shape[1])) - fit
     (h_4,) = after((h,), stale_3)
     more = as_rows(places, h_4, (rest * h.shape[0], live.shape[1]), fit)
+    stale_opp_o = across_cores(opp_4)
     (more,) = after((more,), opp_4)
     stale_far = along_z(both_4, MID)
     came_b = along_z(more, IN)
-    came_x, x_3, opp_x = after((came_4, x_3, opp_4), both_o, far_3o)
+    came_x, x_3 = after((came_4, x_3))
     x_4 = over_x(came_x, END)
-    stale_opp_o = across_cores(opp_4)
     came_4o = across_cores(came_4)
+    t_near = near_ends(places, h, t_near, both_4, both_o, opp_4, stale_opp_o)
     student = contrib(places, h, OPP, OPP_O, [(live_mid, live_mid_o), (both_3, both_o)], student)
-    t_near = near_ends(places, h, t_near, both_4, both_o, opp_4, stale_opp_o)
 
     stale_far, came_b = after((stale_far, came_b), tick(places, came_b), student, t_near)
     stale_far_o = across_cores(stale_far)
@@ -331,11 +331,12 @@
     t_mine, t_end = teachers(
         places, h, t_near, (stale, stale_o, opp_4, stale_opp_o, stale_far, stale_far_o), (came_4, came_b)
     )
-    x_2t, x_3t, x_4t, student = after((x_2, x_3, x_4, student), t_mine)
+    (student,) = after((student,), t_mine)
+    x_2t, x_3t, x_4t = after((x_2, x_3, x_4), t_mine)
+    student = contrib(places, h, FAR, FAR_O, [(far_3, far_3o), (came_4, came_4o)], student)
     x_2_o = across_cores(x_2t)
     x_3_o = across_cores(x_3t)
     x_4_o = across_cores(x_4t)
-    student = contrib(places, h, FAR, FAR_O, [(far_3, far_3o), (came_4, came_4o)], student)
 
     target_1 = partner(t_mine, "mp", 0)
     route = []

time: 105 us -> 104 us (level)
  starting transfers between devices: 39.1 us -> 38 us
    ppermute x1, waiting for transfers between devices: 6.14 us -> 4.16 us  [line_of_four(): target_2 = lax.ppermute(t_end, ('mp', 'fsdp'), route)]
    ppermute x8, starting transfers between devices: 21.9 us -> 20.7 us  [along_z(): return lax.ppermute(block, 'fsdp', route)]
  transfers between devices with their start and end apart: 28 -> 28, of which waited for: 9 -> 10; matrix products, arithmetic and copies ran while one was open for 1% -> 1% of each run, Pallas kernels for 10% -> 11%
where the time goes in v5:
time: 104 us; the launch traced here: 103 us
  waiting for transfers between devices  47.8 us (46%)
  starting transfers between devices  38 us (37%)
  Pallas kernels  13.7 us (13%)
  local copies, waits for them, and re-layouts  3.34 us (3%)
    ppermute x8, waiting for transfers between devices, along_z(): return lax.ppermute(block, 'fsdp', route)  34.5 us
    ppermute x8, starting transfers between devices, along_z(): return lax.ppermute(block, 'fsdp', route)  20.7 us
    pallas_call x15, Pallas kernels, call(): pl.pallas_call(body, out_shape=shapes, in_specs=[pl.BlockSpec(memory_spac...  13.7 us
    ppermute x4, starting transfers between devices, over_x(): return lax.ppermute(block, ('fsdp', 'tp'), route)  9.21 us
    ppermute x15, starting transfers between devices, partner(): return lax.ppermute(block, axis, route)  6.67 us
    ppermute x15, waiting for transfers between devices, partner(): return lax.ppermute(block, axis, route)  4.82 us
    ppermute x4, waiting for transfers between devices, over_x(): return lax.ppermute(block, ('fsdp', 'tp'), route)  4.28 us
    ppermute x1, waiting for transfers between devices, line_of_four(): target_2 = lax.ppermute(t_end, ('mp', 'fsdp'), route)  4.16 us
  transfers between devices with their start and end apart: 28, of which 10 were waited for; matrix products, arithmetic and copies ran while one was open for 1% of the time, Pallas kernels for 11%

profile of v5, /device:TPU:0, one launch (start us, length us, event | category | flops | bytes accessed | tf_op | source)
XLA Modules:
  0.0 103.2 jit_solution(7017283044180288724)
XLA Ops:
  1.2 5.9 %collective-permute-start.1 = (bf16[640,512]{1,0:T(8,128)(2,1)}, bf16[640,512]{1,0:T(8,128)(2,1)S(1)}, u32[]{:S(2)}, u32[]{:S(2)}) collective-permute-start(bf16[640,512]{1,0:T(8,128)(2,1)} %bitcast.22), channel_id=1, source_target_pairs={{0,4},{2,6},{4,0},{6,2},{8,12},{10,14},{12,8},{14,10},{1,5},{3,7},... | collective-permute-start | bytes 1966088 | tf_op jit(solution)/shard_map/ppermute | solution.py:48
  7.1 1.3 %collective-permute-start.9 = (bf16[640,512]{1,0:T(8,128)(2,1)}, bf16[640,512]{1,0:T(8,128)(2,1)S(1)}, u32[]{:S(2)}, u32[]{:S(2)}) collective-permute-start(bf16[640,512]{1,0:T(8,128)(2,1)} %bitcast.23), channel_id=1, source_target_pairs={{1,0},{3,2},{5,4},{7,6},{8,9},{10,11},{12,13},{14,15},{17,16},{19,... | collective-permute-start | bytes 1966088 | tf_op jit(solution)/shard_map/ppermute | solution.py:63
  9.1 1.4 %copy-done = bf16[1,160,5120]{2,1,0:T(8,128)(2,1)S(1)} copy-done((bf16[1,160,5120]{2,1,0:T(8,128)(2,1)S(1)}, bf16[1,160,5120]{2,1,0:T(8,128)(2,1)}, u32[]{:S(2)}) %copy-start) | copy-done | bytes 1638424
  10.5 1.1 %copy-done.3 = bf16[1,640,512]{2,1,0:T(8,128)(2,1)S(1)} copy-done((bf16[1,640,512]{2,1,0:T(8,128)(2,1)S(1)}, bf16[1,640,512]{2,1,0:T(8,128)(2,1)}, u32[]{:S(2)}) %copy-start.3) | copy-done | bytes 655384
  13.7 8.2 %collective-permute-done.1.no_ref.refs_0_.refs_10_ = bf16[640,512]{1,0:T(8,128)(2,1)S(1)} collective-permute-done((bf16[640,512]{1,0:T(8,128)(2,1)}, bf16[640,512]{1,0:T(8,128)(2,1)S(1)}, u32[]{:S(2)}, u32[]{:S(2)}) %collective-permute-start.1) | collective-permute-done | bytes 655392 | tf_op jit(solution)/shard_map/ppermute | solution.py:48
  22.5 1.8 %collective-permute-start.5 = (bf16[640,512]{1,0:T(8,128)(2,1)S(1)}, bf16[640,512]{1,0:T(8,128)(2,1)S(1)}, u32[]{:S(2)}, u32[]{:S(2)}) collective-permute-start(bf16[640,512]{1,0:T(8,128)(2,1)S(1)} %choose.3), channel_id=1, source_target_pairs={{0,4},{2,6},{4,0},{6,2},{8,12},{10,14},{12,8},{14,10},{1,5},{3,7},... | collective-permute-start | bytes 1966088 | tf_op jit(solution)/shard_map/ppermute | solution.py:48
  25.9 1.3 %collective-permute-start.10 = (bf16[640,512]{1,0:T(8,128)(2,1)S(1)}, bf16[640,512]{1,0:T(8,128)(2,1)S(1)}, u32[]{:S(2)}, u32[]{:S(2)}) collective-permute-start(bf16[640,512]{1,0:T(8,128)(2,1)S(1)} %choose.4), channel_id=1, source_target_pairs={{1,0},{3,2},{5,4},{4,5},{7,6},{6,7},{8,9},{9,8},{10,11},{11,10},{1... | collective-permute-start | bytes 1966088 | tf_op jit(solution)/shard_map/ppermute | solution.py:63
  27.7 10.6 %collective-permute-done.5.refs_2_.n.yes_ref.refs_4_ = bf16[640,512]{1,0:T(8,128)(2,1)S(1)} collective-permute-done((bf16[640,512]{1,0:T(8,128)(2,1)S(1)}, bf16[640,512]{1,0:T(8,128)(2,1)S(1)}, u32[]{:S(2)}, u32[]{:S(2)}) %collective-permute-start.5) | collective-permute-done | bytes 655392 | tf_op jit(solution)/shard_map/ppermute | solution.py:48
  39.0 3.7 %collective-permute-start.8 = (bf16[640,512]{1,0:T(8,128)(2,1)S(1)}, bf16[640,512]{1,0:T(8,128)(2,1)S(1)}, u32[]{:S(2)}, u32[]{:S(2)}) collective-permute-start(bf16[640,512]{1,0:T(8,128)(2,1)S(1)} %as_rows.2), channel_id=1, source_target_pairs={{0,4},{2,6},{4,0},{6,2},{8,12},{10,14},{12,8},{14,10},{1,5},{3,7},... | collective-permute-start | bytes 1966088 | tf_op jit(solution)/shard_map/ppermute | solution.py:48
  44.9 3.2 %collective-permute-start.17 = (bf16[640,512]{1,0:T(8,128)(2,1)S(1)}, bf16[640,512]{1,0:T(8,128)(2,1)S(1)}, u32[]{:S(2)}, u32[]{:S(2)}) collective-permute-start(bf16[640,512]{1,0:T(8,128)(2,1)S(1)} %choose.5), channel_id=1, source_target_pairs={{0,1},{2,3},{4,5},{6,7},{9,8},{11,10},{13,12},{15,14},{16,17},{18,... | collective-permute-start | bytes 1966088 | tf_op jit(solution)/shard_map/ppermute | solution.py:63
  49.1 7.1 %collective-permute-done.8.refs_9_.refs_2_.refs_6_ = bf16[640,512]{1,0:T(8,128)(2,1)S(1)} collective-permute-done((bf16[640,512]{1,0:T(8,128)(2,1)S(1)}, bf16[640,512]{1,0:T(8,128)(2,1)S(1)}, u32[]{:S(2)}, u32[]{:S(2)}) %collective-permute-start.8) | collective-permute-done | bytes 655392 | tf_op jit(solution)/shard_map/ppermute | solution.py:48
  56.2 6.6 %collective-permute-start.20 = (bf16[640,512]{1,0:T(8,128)(2,1)S(1)}, bf16[640,512]{1,0:T(8,128)(2,1)S(1)}, u32[]{:S(2)}, u32[]{:S(2)}) collective-permute-start(bf16[640,512]{1,0:T(8,128)(2,1)S(1)} %as_rows.3), channel_id=1, source_target_pairs={{0,4},{2,6},{12,8},{14,10},{1,5},{3,7},{13,9},{15,11},{16,20},{18,... | collective-permute-start | bytes 1966088 | tf_op jit(solution)/shard_map/ppermute | solution.py:48
  63.9 3.4 %collective-permute-start.18 = (bf16[640,512]{1,0:T(8,128)(2,1)S(1)}, bf16[640,512]{1,0:T(8,128)(2,1)S(1)}, u32[]{:S(2)}, u32[]{:S(2)}) collective-permute-start(bf16[640,512]{1,0:T(8,128)(2,1)S(1)} %collective-permute-done.8.refs_9_.refs_2_.refs_6_), channel_id=1, source_target_pairs={{0,1},{2,3},{13,12},{15,14},{16,17},{18,19},{29,28},{31,30}} | collective-permute-start | bytes 1966088 | tf_op jit(solution)/shard_map/ppermute | solution.py:63
  68.9 8.6 %collective-permute-done.20.refs_10_ = bf16[640,512]{1,0:T(8,128)(2,1)S(1)} collective-permute-done((bf16[640,512]{1,0:T(8,128)(2,1)S(1)}, bf16[640,512]{1,0:T(8,128)(2,1)S(1)}, u32[]{:S(2)}, u32[]{:S(2)}) %collective-permute-start.20) | collective-permute-done | bytes 655392 | tf_op jit(solution)/shard_map/ppermute | solution.py:48
  78.0 3.8 %collective-permute-done.18.refs_4_ = bf16[640,512]{1,0:T(8,128)(2,1)S(1)} collective-permute-done((bf16[640,512]{1,0:T(8,128)(2,1)S(1)}, bf16[640,512]{1,0:T(8,128)(2,1)S(1)}, u32[]{:S(2)}, u32[]{:S(2)}) %collective-permute-start.18) | collective-permute-done | bytes 655392 | tf_op jit(solution)/shard_map/ppermute | solution.py:63
  83.0 1.5 %collective-permute-start.22 = (bf16[160,512]{1,0:T(8,128)(2,1)S(1)}, bf16[160,512]{1,0:T(8,128)(2,1)S(1)}, u32[]{:S(2)}, u32[]{:S(2)}) collective-permute-start(bf16[160,512]{1,0:T(8,128)(2,1)S(1)} %get-tuple-element.53), channel_id=1, source_target_pairs={{0,16},{16,0},{1,17},{17,1},{2,18},{18,2},{3,19},{19,3},{4,20},{20... | collective-permute-start | bytes 491528 | tf_op jit(solution)/shard_map/ppermute | solution.py:43
  84.5 1.4 %collective-permute-start.23 = (bf16[160,512]{1,0:T(8,128)(2,1)S(1)}, bf16[160,512]{1,0:T(8,128)(2,1)S(1)}, u32[]{:S(2)}, u32[]{:S(2)}) collective-permute-start(bf16[160,512]{1,0:T(8,128)(2,1)S(1)} %get-tuple-element.55), channel_id=1, source_target_pairs={{4,16},{6,18},{8,28},{10,30},{20,0},{22,2},{24,12},{26,14},{5,17},... | collective-permute-start | bytes 491528 | tf_op jit(solution)/shard_map/ppermute | solution.py:347
  86.0 1.0 contrib.9.student_ref
  86.9 2.6 %collective-permute-done.22.one = bf16[160,512]{1,0:T(8,128)(2,1)S(1)} collective-permute-done((bf16[160,512]{1,0:T(8,128)(2,1)S(1)}, bf16[160,512]{1,0:T(8,128)(2,1)S(1)}, u32[]{:S(2)}, u32[]{:S(2)}) %collective-permute-start.22) | collective-permute-done | bytes 163872 | tf_op jit(solution)/shard_map/ppermute | solution.py:43
  89.6 4.2 %collective-permute-done.23.two = bf16[160,512]{1,0:T(8,128)(2,1)S(1)} collective-permute-done((bf16[160,512]{1,0:T(8,128)(2,1)S(1)}, bf16[160,512]{1,0:T(8,128)(2,1)S(1)}, u32[]{:S(2)}, u32[]{:S(2)}) %collective-permute-start.23) | collective-permute-done | bytes 163872 | tf_op jit(solution)/shard_map/ppermute | solution.py:347
  94.5 2.5 %collective-permute-start.24 = (bf16[160,512]{1,0:T(8,128)(2,1)S(1)}, bf16[160,512]{1,0:T(8,128)(2,1)S(1)}, u32[]{:S(2)}, u32[]{:S(2)}) collective-permute-start(bf16[160,512]{1,0:T(8,128)(2,1)S(1)} %difference.1.left_ref), channel_id=1, source_target_pairs={{0,1},{1,0},{2,3},{3,2},{4,5},{5,4},{6,7},{7,6},{8,9},{9,8},{10,11... | collective-permute-start | bytes 491528 | tf_op jit(solution)/shard_map/ppermute | solution.py:43
  97.0 1.5 %gradient.2.refs_8_ = f32[160,2560]{1,0:T(8,128)S(1)} custom-call(s32[16]{0:T(128)S(1)} %dynamic-slice_bitcast_fusion.s.refs_0_, bf16[160,512]{1,0:T(8,128)(2,1)S(1)} %difference.1.left_ref, bf16[640,512]{1,0:T(8,128)(2,1)S(1)} %collective-permute-done.no_ref.yes_ref.refs_0_, bf16[640,512]{1,0:T(8,128)(2,1)S(1)} %collective-permute-done.12.refs_1_, ...), custom_call_target="tpu_custom_call" | custom-call | flops 1 | bytes 1 | tf_op jit(solution)/shard_map/gradient/pallas_call | solution.py:82
  98.6 2.2 %collective-permute-done.24.left_ref = bf16[160,512]{1,0:T(8,128)(2,1)S(1)} collective-permute-done((bf16[160,512]{1,0:T(8,128)(2,1)S(1)}, bf16[160,512]{1,0:T(8,128)(2,1)S(1)}, u32[]{:S(2)}, u32[]{:S(2)}) %collective-permute-start.24) | collective-permute-done | bytes 163872 | tf_op jit(solution)/shard_map/ppermute | solution.py:43
  100.7 2.4 %gradient.3 = bf16[160,2560]{1,0:T(8,128)(2,1)} custom-call(s32[16]{0:T(128)S(1)} %dynamic-slice_bitcast_fusion.s.refs_0_, bf16[160,512]{1,0:T(8,128)(2,1)S(1)} %collective-permute-done.24.left_ref, bf16[640,512]{1,0:T(8,128)(2,1)S(1)} %collective-permute-done.10.refs_0_, bf16[640,512]{1,0:T(8,128)(2,1)S(1)} %collective-permute-done.25.refs_1_, ...), custom_call_target="tpu_custom_call" | custom-call | flops 1 | bytes 1 | tf_op jit(solution)/shard_map/gradient/pallas_call | solution.py:82
  (60 shorter events, 15.5 us)
Async XLA Ops:
  0.0 9.1 %collective-permute-start.2 = (bf16[640,512]{1,0:T(8,128)(2,1)}, bf16[640,512]{1,0:T(8,128)(2,1)S(1)}, u32[]{:S(2)}, u32[]{:S(2)}) collective-permute-start(bf16[640,512]{1,0:T(8,128)(2,1)} %bitcast.20), channel_id=1, source_target_pairs={{0,2},{2,0},{4,6},{6,4},{8,10},{10,8},{12,14},{14,12},{1,3},{3,1},... | collective-permute-start | bytes 1966088 | tf_op jit(solution)/shard_map/ppermute | solution.py:43
  0.5 12.1 %collective-permute-start.3 = (bf16[640,512]{1,0:T(8,128)(2,1)}, bf16[640,512]{1,0:T(8,128)(2,1)S(1)}, u32[]{:S(2)}, u32[]{:S(2)}) collective-permute-start(bf16[640,512]{1,0:T(8,128)(2,1)} %bitcast.15), channel_id=1, source_target_pairs={{0,2},{2,0},{4,6},{6,4},{8,10},{10,8},{12,14},{14,12},{1,3},{3,1},... | collective-permute-start | bytes 1966088 | tf_op jit(solution)/shard_map/ppermute | solution.py:43
  0.5 13.2 %collective-permute-start = (bf16[640,512]{1,0:T(8,128)(2,1)}, bf16[640,512]{1,0:T(8,128)(2,1)S(1)}, u32[]{:S(2)}, u32[]{:S(2)}) collective-permute-start(bf16[640,512]{1,0:T(8,128)(2,1)} %bitcast.21), channel_id=1, source_target_pairs={{4,8},{6,10},{8,4},{10,6},{5,9},{7,11},{9,5},{11,7},{20,24},{22,26... | collective-permute-start | bytes 1966088 | tf_op jit(solution)/shard_map/ppermute | solution.py:48
  1.2 20.7 %collective-permute-start.1 = (bf16[640,512]{1,0:T(8,128)(2,1)}, bf16[640,512]{1,0:T(8,128)(2,1)S(1)}, u32[]{:S(2)}, u32[]{:S(2)}) collective-permute-start(bf16[640,512]{1,0:T(8,128)(2,1)} %bitcast.22), channel_id=1, source_target_pairs={{0,4},{2,6},{4,0},{6,2},{8,12},{10,14},{12,8},{14,10},{1,5},{3,7},... | collective-permute-start | bytes 1966088 | tf_op jit(solution)/shard_map/ppermute | solution.py:48
  7.1 18.2 %collective-permute-start.9 = (bf16[640,512]{1,0:T(8,128)(2,1)}, bf16[640,512]{1,0:T(8,128)(2,1)S(1)}, u32[]{:S(2)}, u32[]{:S(2)}) collective-permute-start(bf16[640,512]{1,0:T(8,128)(2,1)} %bitcast.23), channel_id=1, source_target_pairs={{1,0},{3,2},{5,4},{7,6},{8,9},{10,11},{12,13},{14,15},{17,16},{19,... | collective-permute-start | bytes 1966088 | tf_op jit(solution)/shard_map/ppermute | solution.py:63
  22.5 15.9 %collective-permute-start.5 = (bf16[640,512]{1,0:T(8,128)(2,1)S(1)}, bf16[640,512]{1,0:T(8,128)(2,1)S(1)}, u32[]{:S(2)}, u32[]{:S(2)}) collective-permute-start(bf16[640,512]{1,0:T(8,128)(2,1)S(1)} %choose.3), channel_id=1, source_target_pairs={{0,4},{2,6},{4,0},{6,2},{8,12},{10,14},{12,8},{14,10},{1,5},{3,7},... | collective-permute-start | bytes 1966088 | tf_op jit(solution)/shard_map/ppermute | solution.py:48
  24.3 14.1 %collective-permute-start.4 = (bf16[640,512]{1,0:T(8,128)(2,1)S(1)}, bf16[640,512]{1,0:T(8,128)(2,1)S(1)}, u32[]{:S(2)}, u32[]{:S(2)}) collective-permute-start(bf16[640,512]{1,0:T(8,128)(2,1)S(1)} %collective-permute-done.1.no_ref.refs_0_.refs_10_), channel_id=1, source_target_pairs={{4,8},{6,10},{8,4},{10,6},{5,9},{7,11},{9,5},{11,7},{20,24},{22,26... | collective-permute-start | bytes 1966088 | tf_op jit(solution)/shard_map/ppermute | solution.py:48
  25.9 17.1 %collective-permute-start.10 = (bf16[640,512]{1,0:T(8,128)(2,1)S(1)}, bf16[640,512]{1,0:T(8,128)(2,1)S(1)}, u32[]{:S(2)}, u32[]{:S(2)}) collective-permute-start(bf16[640,512]{1,0:T(8,128)(2,1)S(1)} %choose.4), channel_id=1, source_target_pairs={{1,0},{3,2},{5,4},{4,5},{7,6},{6,7},{8,9},{9,8},{10,11},{11,10},{1... | collective-permute-start | bytes 1966088 | tf_op jit(solution)/shard_map/ppermute | solution.py:63
  27.2 17.1 %collective-permute-start.11 = (bf16[640,512]{1,0:T(8,128)(2,1)S(1)}, bf16[640,512]{1,0:T(8,128)(2,1)S(1)}, u32[]{:S(2)}, u32[]{:S(2)}) collective-permute-start(bf16[640,512]{1,0:T(8,128)(2,1)S(1)} %collective-permute-done.1.no_ref.refs_0_.refs_10_), channel_id=1, source_target_pairs={{0,2},{2,0},{4,6},{6,4},{8,10},{10,8},{12,14},{14,12},{1,3},{3,1},... | collective-permute-start | bytes 1966088 | tf_op jit(solution)/shard_map/ppermute | solution.py:43
  27.2 17.1 %collective-permute-start.12 = (bf16[640,512]{1,0:T(8,128)(2,1)S(1)}, bf16[640,512]{1,0:T(8,128)(2,1)S(1)}, u32[]{:S(2)}, u32[]{:S(2)}) collective-permute-start(bf16[640,512]{1,0:T(8,128)(2,1)S(1)} %collective-permute-done.no_ref.yes_ref.refs_0_), channel_id=1, source_target_pairs={{0,2},{2,0},{4,6},{6,4},{8,10},{10,8},{12,14},{14,12},{1,3},{3,1},... | collective-permute-start | bytes 1966088 | tf_op jit(solution)/shard_map/ppermute | solution.py:43
  39.0 17.2 %collective-permute-start.8 = (bf16[640,512]{1,0:T(8,128)(2,1)S(1)}, bf16[640,512]{1,0:T(8,128)(2,1)S(1)}, u32[]{:S(2)}, u32[]{:S(2)}) collective-permute-start(bf16[640,512]{1,0:T(8,128)(2,1)S(1)} %as_rows.2), channel_id=1, source_target_pairs={{0,4},{2,6},{4,0},{6,2},{8,12},{10,14},{12,8},{14,10},{1,5},{3,7},... | collective-permute-start | bytes 1966088 | tf_op jit(solution)/shard_map/ppermute | solution.py:48
  42.9 13.3 %collective-permute-start.7 = (bf16[640,512]{1,0:T(8,128)(2,1)S(1)}, bf16[640,512]{1,0:T(8,128)(2,1)S(1)}, u32[]{:S(2)}, u32[]{:S(2)}) collective-permute-start(bf16[640,512]{1,0:T(8,128)(2,1)S(1)} %bitcast.18), channel_id=1, source_target_pairs={{4,8},{6,10},{8,4},{10,6},{5,9},{7,11},{9,5},{11,7},{20,24},{22,26... | collective-permute-start | bytes 1966088 | tf_op jit(solution)/shard_map/ppermute | solution.py:48
  44.2 19.6 %collective-permute-start.15 = (bf16[640,512]{1,0:T(8,128)(2,1)S(1)}, bf16[640,512]{1,0:T(8,128)(2,1)S(1)}, u32[]{:S(2)}, u32[]{:S(2)}) collective-permute-start(bf16[640,512]{1,0:T(8,128)(2,1)S(1)} %collective-permute-done.5.refs_2_.n.yes_ref.refs_4_), channel_id=1, source_target_pairs={{0,2},{2,0},{4,6},{6,4},{8,10},{10,8},{12,14},{14,12},{1,3},{3,1},... | collective-permute-start | bytes 1966088 | tf_op jit(solution)/shard_map/ppermute | solution.py:43
  44.9 18.6 %collective-permute-start.17 = (bf16[640,512]{1,0:T(8,128)(2,1)S(1)}, bf16[640,512]{1,0:T(8,128)(2,1)S(1)}, u32[]{:S(2)}, u32[]{:S(2)}) collective-permute-start(bf16[640,512]{1,0:T(8,128)(2,1)S(1)} %choose.5), channel_id=1, source_target_pairs={{0,1},{2,3},{4,5},{6,7},{9,8},{11,10},{13,12},{15,14},{16,17},{18,... | collective-permute-start | bytes 1966088 | tf_op jit(solution)/shard_map/ppermute | solution.py:63
  56.2 12.1 %collective-permute-start.16 = (bf16[640,512]{1,0:T(8,128)(2,1)S(1)}, bf16[640,512]{1,0:T(8,128)(2,1)S(1)}, u32[]{:S(2)}, u32[]{:S(2)}) collective-permute-start(bf16[640,512]{1,0:T(8,128)(2,1)S(1)} %collective-permute-done.7.p.refs_5_), channel_id=1, source_target_pairs={{0,2},{2,0},{4,6},{6,4},{8,10},{10,8},{12,14},{14,12},{1,3},{3,1},... | collective-permute-start | bytes 1966088 | tf_op jit(solution)/shard_map/ppermute | solution.py:43
  56.2 21.2 %collective-permute-start.20 = (bf16[640,512]{1,0:T(8,128)(2,1)S(1)}, bf16[640,512]{1,0:T(8,128)(2,1)S(1)}, u32[]{:S(2)}, u32[]{:S(2)}) collective-permute-start(bf16[640,512]{1,0:T(8,128)(2,1)S(1)} %as_rows.3), channel_id=1, source_target_pairs={{0,4},{2,6},{12,8},{14,10},{1,5},{3,7},{13,9},{15,11},{16,20},{18,... | collective-permute-start | bytes 1966088 | tf_op jit(solution)/shard_map/ppermute | solution.py:48
  62.8 14.6 %collective-permute-start.19 = (bf16[640,512]{1,0:T(8,128)(2,1)S(1)}, bf16[640,512]{1,0:T(8,128)(2,1)S(1)}, u32[]{:S(2)}, u32[]{:S(2)}) collective-permute-start(bf16[640,512]{1,0:T(8,128)(2,1)S(1)} %collective-permute-done.5.refs_2_.n.yes_ref.refs_4_), channel_id=1, source_target_pairs={{4,8},{6,10},{8,4},{10,6},{5,9},{7,11},{9,5},{11,7},{20,24},{22,26... | collective-permute-start | bytes 1966088 | tf_op jit(solution)/shard_map/ppermute | solution.py:48
  63.6 18.2 %collective-permute-start.14 = (bf16[640,512]{1,0:T(8,128)(2,1)S(1)}, bf16[640,512]{1,0:T(8,128)(2,1)S(1)}, u32[]{:S(2)}, u32[]{:S(2)}) collective-permute-start(bf16[640,512]{1,0:T(8,128)(2,1)S(1)} %collective-permute-done.8.refs_9_.refs_2_.refs_6_), channel_id=1, source_target_pairs={{0,2},{2,0},{4,6},{6,4},{8,10},{10,8},{12,14},{14,12},{1,3},{3,1},... | collective-permute-start | bytes 1966088 | tf_op jit(solution)/shard_map/ppermute | solution.py:43
  63.9 17.9 %collective-permute-start.18 = (bf16[640,512]{1,0:T(8,128)(2,1)S(1)}, bf16[640,512]{1,0:T(8,128)(2,1)S(1)}, u32[]{:S(2)}, u32[]{:S(2)}) collective-permute-start(bf16[640,512]{1,0:T(8,128)(2,1)S(1)} %collective-permute-done.8.refs_9_.refs_2_.refs_6_), channel_id=1, source_target_pairs={{0,1},{2,3},{13,12},{15,14},{16,17},{18,19},{29,28},{31,30}} | collective-permute-start | bytes 1966088 | tf_op jit(solution)/shard_map/ppermute | solution.py:63
  77.4 7.1 %collective-permute-start.6 = (bf16[640,512]{1,0:T(8,128)(2,1)S(1)}, bf16[640,512]{1,0:T(8,128)(2,1)S(1)}, u32[]{:S(2)}, u32[]{:S(2)}) collective-permute-start(bf16[640,512]{1,0:T(8,128)(2,1)S(1)} %collective-permute-done.4.refs_0_.no_ref.refs_2_), channel_id=1, source_target_pairs={{0,2},{2,0},{4,6},{6,4},{8,10},{10,8},{12,14},{14,12},{1,3},{3,1},... | collective-permute-start | bytes 1966088 | tf_op jit(solution)/shard_map/ppermute | solution.py:43
  82.3 18.4 %collective-permute-start.25 = (bf16[640,512]{1,0:T(8,128)(2,1)S(1)}, bf16[640,512]{1,0:T(8,128)(2,1)S(1)}, u32[]{:S(2)}, u32[]{:S(2)}) collective-permute-start(bf16[640,512]{1,0:T(8,128)(2,1)S(1)} %collective-permute-done.10.refs_0_), channel_id=1, source_target_pairs={{0,2},{2,0},{4,6},{6,4},{8,10},{10,8},{12,14},{14,12},{1,3},{3,1},... | collective-permute-start | bytes 1966088 | tf_op jit(solution)/shard_map/ppermute | solution.py:43
  82.4 18.3 %collective-permute-start.26 = (bf16[640,512]{1,0:T(8,128)(2,1)S(1)}, bf16[640,512]{1,0:T(8,128)(2,1)S(1)}, u32[]{:S(2)}, u32[]{:S(2)}) collective-permute-start(bf16[640,512]{1,0:T(8,128)(2,1)S(1)} %collective-permute-done.17.refs_2_), channel_id=1, source_target_pairs={{0,2},{2,0},{4,6},{6,4},{8,10},{10,8},{12,14},{14,12},{1,3},{3,1},... | collective-permute-start | bytes 1966088 | tf_op jit(solution)/shard_map/ppermute | solution.py:43
  82.9 17.8 %collective-permute-start.27 = (bf16[640,512]{1,0:T(8,128)(2,1)S(1)}, bf16[640,512]{1,0:T(8,128)(2,1)S(1)}, u32[]{:S(2)}, u32[]{:S(2)}) collective-permute-start(bf16[640,512]{1,0:T(8,128)(2,1)S(1)} %collective-permute-done.18.refs_4_), channel_id=1, source_target_pairs={{0,2},{2,0},{4,6},{6,4},{8,10},{10,8},{12,14},{14,12},{1,3},{3,1},... | collective-permute-start | bytes 1966088 | tf_op jit(solution)/shard_map/ppermute | solution.py:43
  84.5 9.2 %collective-permute-start.23 = (bf16[160,512]{1,0:T(8,128)(2,1)S(1)}, bf16[160,512]{1,0:T(8,128)(2,1)S(1)}, u32[]{:S(2)}, u32[]{:S(2)}) collective-permute-start(bf16[160,512]{1,0:T(8,128)(2,1)S(1)} %get-tuple-element.55), channel_id=1, source_target_pairs={{4,16},{6,18},{8,28},{10,30},{20,0},{22,2},{24,12},{26,14},{5,17},... | collective-permute-start | bytes 491528 | tf_op jit(solution)/shard_map/ppermute | solution.py:347
  (10 other events, 73.1 us)
